TPU v7x, 32 devices: a whole 2x2x4 slice. The times are simulated.
32 devices in a mesh: dp: 4 (over z), mp: 8 (over y, x, core).
Axes of the slice: x: 2, y: 2, z: 4, core: 2. Of those that a mesh axis runs over, the one named last changes fastest.
Arguments:
- behaviors: bfloat16 [32, 2048, 1024], P('dp', 'mp'), may hold values from -8 to 8
- candidates: bfloat16 [32, 2048, 128], P('dp', 'mp'), may hold values from -12 to 12
- lengths: int32 [32], P('dp'), may hold values from 128 to 1024
- bilinear: bfloat16 [2048, 2048], P('mp'), may hold values from -1 to 2
- norm_gain: float32 [2048], replicated, may hold values from 0.1 to 1.9
- w_gate: bfloat16 [2048, 8192], P('dp', 'mp'), may hold values from -0.125 to 0.125
- w_up: bfloat16 [2048, 8192], P('dp', 'mp'), may hold values from -0.125 to 0.125
- w_down: bfloat16 [8192, 2048], P('mp', 'dp'), may hold values from -0.0625 to 0.0625
Outputs:
- interest: bfloat16 [32, 2048, 128], P('dp', 'mp')
All inputs are finite; a program needn't handle non-finite values.
Results may differ from a plain program's by a relative error of at most 0.015.
Values may be sent and summed in bfloat16 or wider, within the bound.
No kernel may reach another device: no remote copies, remote signals or barrier semaphores. Data moves between devices by JAX's collectives and lax.ppermute only.
A program may use at most 64 MiB of HBM per device.

v0:
```python
import math

import jax
import jax.numpy as jnp
from jax import lax
from jax.sharding import PartitionSpec as P


def attention_weights(scores, live):
    masked = jnp.where(live, scores, -1e30)
    highest = jnp.max(masked, axis=-1, keepdims=True)
    expons = jnp.where(live, jnp.exp(masked - highest), 0.0)
    return (expons / jnp.sum(expons, axis=-1, keepdims=True)).astype(jnp.bfloat16)


def shards(behaviors, candidates, lengths, bilinear, norm_gain, w_gate, w_up, w_down):
    user_count, width_part, cand_count = candidates.shape
    feature_width = bilinear.shape[1]
    behavior_count = behaviors.shape[2]
    query_part = jnp.einsum(
        "ek,ukc->uec",
        bilinear,
        lax.all_gather(candidates, "mp", axis=1, tiled=True),
        preferred_element_type=jnp.float32,
    )
    query = query_part.astype(jnp.bfloat16)
    partial_value = jnp.einsum("ukc,ukl->ucl", query, behaviors, preferred_element_type=jnp.float32)
    scale = 1.0 / math.sqrt(feature_width)
    live = (
        lax.broadcasted_iota(jnp.int32, (user_count, 1, behavior_count), 2) < lengths[:, None, None]
    )
    share = lax.psum_scatter(partial_value, "mp", scatter_dimension=1, tiled=True)
    probs_share = attention_weights(share * scale, live)
    probs = lax.all_gather(probs_share, "mp", axis=1, tiled=True)
    pooled = jnp.einsum(
        "ucl,ukl->ukc", probs, behaviors, preferred_element_type=jnp.float32
    ).astype(jnp.bfloat16)
    whole = lax.all_gather(pooled, "mp", axis=1, tiled=True)
    values = whole.astype(jnp.float32)
    square_mean = jnp.mean(values * values, axis=1, keepdims=True)
    normed = (values * lax.rsqrt(square_mean + 1e-06) * norm_gain[None, :, None]).astype(
        jnp.bfloat16
    )
    gate = jnp.einsum(
        "ukc,kf->ucf",
        normed,
        lax.all_gather(w_gate, "dp", axis=0, tiled=True),
        preferred_element_type=jnp.float32,
    )
    upward = jnp.einsum(
        "ukc,kf->ucf",
        normed,
        lax.all_gather(w_up, "dp", axis=0, tiled=True),
        preferred_element_type=jnp.float32,
    )
    hidden = (jax.nn.silu(gate) * upward).astype(jnp.bfloat16)
    down_full = lax.all_gather(w_down, "dp", axis=1, tiled=True)
    result = lax.psum_scatter(
        jnp.einsum("ucf,fk->kuc", hidden, down_full, preferred_element_type=jnp.float32).astype(
            jnp.bfloat16
        ),
        "mp",
        scatter_dimension=0,
        tiled=True,
    ).astype(jnp.float32)
    return jnp.transpose(result, (1, 0, 2)).astype(jnp.bfloat16)


def solution(mesh):
    return jax.shard_map(
        shards,
        mesh=mesh,
        in_specs=(
            P("dp", "mp", None),
            P("dp", "mp", None),
            P("dp"),
            P("mp", None),
            P(),
            P("dp", "mp"),
            P("dp", "mp"),
            P("mp", "dp"),
        ),
        out_specs=P("dp", "mp", None),
        check_vma=False,
    )
```

profile of v0, /device:TPU:0, one launch (start us, length us, event | category | flops | bytes accessed | tf_op | source)
XLA Modules:
  0.0 498.7 jit_solution(1023455317639719504)
XLA Ops:
  6.5 0.0 copy-start
  6.5 0.0 all-gather.7.cloned.1.call-start
  6.5 0.7 all-gather.7.cloned.1.call-update
  7.3 0.0 reduce-scatter.3.cloned.1.call-start
  7.3 41.3 %all-gather.7.cloned.1.call-done = bf16[8,2048,128]{2,1,0:T(8,128)(2,1)} async-done(((bf16[8,256,128]{2,1,0:T(8,128)(2,1)}), bf16[8,2048,128]{2,1,0:T(8,128)(2,1)}) %all-gather.7.cloned.1.call-update) | async-done | bytes 4194320 | tf_op jit(solution)/shard_map/all_gather | solution.py:23
  48.6 0.0 copy-done
  48.6 8.2 %fusion.24 = f32[8,128,1024]{2,1,0:T(8,128)} fusion(bf16[8,256,1024]{2,1,0:T(8,128)(2,1)} %param.8, bf16[8,2048,128]{2,1,0:T(8,128)(2,1)} %all-gather.7.cloned.1.call-done, bf16[256,2048]{1,0:T(8,128)(2,1)S(1)} %copy-done), kind=kOutput, calls=%fused_computation.18 | convolution fusion | flops 1610874880 | bytes 13631488 | tf_op jit(solution)/shard_map/ukc,ukl->ucl/dot_general | solution.py:27
  56.7 0.0 copy-start.1
  56.7 0.0 reduce-scatter.3.cloned.1.call-update
  56.8 0.0 all-gather.9.cloned.1.call-start
  56.8 0.6 copy-done.1
  57.4 0.1 iota_compare_fusion
  57.5 50.5 %reduce-scatter.3.cloned.1.call-done = f32[8,16,1024]{2,1,0:T(8,128)} async-done(((f32[8,128,1024]{2,1,0:T(8,128)}), f32[8,16,1024]{2,1,0:T(8,128)}) %reduce-scatter.3.cloned.1.call-update) | async-done | bytes 524304 | tf_op jit(solution)/shard_map/reduce_scatter | solution.py:32
  108.0 1.7 fusion.37
  109.7 0.8 divide_convert_fusion
  110.5 0.0 all-gather.9.cloned.1.call-update
  110.6 0.0 all-gather.11.cloned.1.call-start
  110.6 27.9 %all-gather.9.cloned.1.call-done = bf16[8,128,1024]{2,1,0:T(8,128)(2,1)} async-done(((bf16[8,16,1024]{2,1,0:T(8,128)(2,1)}), bf16[8,128,1024]{2,1,0:T(8,128)(2,1)}) %all-gather.9.cloned.1.call-update) | async-done | bytes 2097168 | tf_op jit(solution)/shard_map/all_gather | solution.py:34
  138.5 5.2 %fusion.27 = bf16[8,256,128]{1,2,0:T(8,128)(2,1)} fusion(bf16[8,128,1024]{2,1,0:T(8,128)(2,1)} %all-gather.9.cloned.1.call-done, bf16[8,256,1024]{2,1,0:T(8,128)(2,1)} %param.8), kind=kOutput, calls=%fused_computation.21 | convolution fusion | flops 537133056 | bytes 6815744 | tf_op jit(solution)/shard_map/ucl,ukl->ukc/dot_general | solution.py:35
  143.7 0.0 copy-start.2
  143.7 0.0 all-gather.11.cloned.1.call-update
  143.7 0.0 all-gather.13.cloned.1.call-start
  143.7 0.5 all-gather.13.cloned.1.call-update
  144.3 0.0 all-gather.15.cloned.1.call-start
  144.3 0.5 all-gather.15.cloned.1.call-update
  144.8 0.0 all-gather.17.cloned.1.call-start
  144.9 0.7 all-gather.17.cloned.1.call-update
  145.6 0.2 reduce-scatter.5.cloned.1.call-start
  145.8 35.4 %all-gather.11.cloned.1.call-done = bf16[8,2048,128]{1,2,0:T(8,128)(2,1)} async-done(((bf16[8,256,128]{1,2,0:T(8,128)(2,1)}), bf16[8,2048,128]{1,2,0:T(8,128)(2,1)}) %all-gather.11.cloned.1.call-update) | async-done | bytes 4194320 | tf_op jit(solution)/shard_map/all_gather | solution.py:38
  181.2 3.1 fusion.1
  184.3 79.1 %all-gather.13.cloned.1.call-done = bf16[2048,1024]{1,0:T(8,128)(2,1)} async-done(((bf16[512,1024]{1,0:T(8,128)(2,1)}), bf16[2048,1024]{1,0:T(8,128)(2,1)}) %all-gather.13.cloned.1.call-update) | async-done | bytes 4194320 | tf_op jit(solution)/shard_map/all_gather | solution.py:47
  263.4 0.0 copy-done.2
  263.4 9.9 %fusion.8 = f32[8,128,1024]{2,1,0:T(8,128)} fusion(bf16[2048,1024]{1,0:T(8,128)(2,1)} %all-gather.13.cloned.1.call-done, bf16[8,2048,128]{1,2,0:T(8,128)(2,1)} %all-gather.11.cloned.1.call-done, f32[2048]{0:T(1024)S(1)} %copy-done.2, f32[8,128]{1,0:T(8,128)S(1)} %add_rsqrt_fusion), kind=kOutput, calls=%fused_computation.10 | convolution fusion | flops 4303355904 | bytes 12595200 | tf_op jit(solution)/shard_map/ukc,kf->ucf/dot_general | solution.py:44
  273.3 70.7 %all-gather.15.cloned.1.call-done = bf16[2048,1024]{1,0:T(8,128)(2,1)} async-done(((bf16[512,1024]{1,0:T(8,128)(2,1)}), bf16[2048,1024]{1,0:T(8,128)(2,1)}) %all-gather.15.cloned.1.call-update) | async-done | bytes 4194320 | tf_op jit(solution)/shard_map/all_gather | solution.py:53
  344.0 80.8 %all-gather.17.cloned.1.call-done = bf16[1024,2048]{1,0:T(8,128)(2,1)} async-done(((bf16[1024,512]{1,0:T(8,128)(2,1)}), bf16[1024,2048]{1,0:T(8,128)(2,1)}) %all-gather.17.cloned.1.call-update) | async-done | bytes 4194320 | tf_op jit(solution)/shard_map/all_gather | solution.py:57
  424.9 15.2 %convert_bitcast_fusion = bf16[2048,8,128]{0,2,1:T(8,128)(2,1)} fusion(bf16[1024,2048]{1,0:T(8,128)(2,1)} %all-gather.17.cloned.1.call-done, f32[8,128,1024]{2,1,0:T(8,128)} %fusion.8, bf16[2048,1024]{1,0:T(8,128)(2,1)} %all-gather.15.cloned.1.call-done, bf16[8,2048,128]{1,2,0:T(8,128)(2,1)} %all-gather.11.cloned.1.call-done, f32[2048]{0:T(1024)S(1)} %copy-done.2, ...), kind=kOutput, calls=%fused_computation.12 | convolution fusion | flops 8606711808 | bytes 20983808 | tf_op jit(solution)/shard_map/ucf,fk->kuc/dot_general | solution.py:59
  440.1 0.0 reduce-scatter.5.cloned.1.call-update
  440.1 49.7 %reduce-scatter.5.cloned.1.call-done = bf16[256,8,128]{0,2,1:T(8,128)(2,1)} async-done(((bf16[2048,8,128]{0,2,1:T(8,128)(2,1)}), bf16[256,8,128]{0,2,1:T(8,128)(2,1)}) %reduce-scatter.5.cloned.1.call-update) | async-done | bytes 524304 | tf_op jit(solution)/shard_map/reduce_scatter | solution.py:58
  489.8 2.0 copy.9
  (1 shorter events, 0.0 us)
Async XLA Ops:
  6.5 42.0 %copy-start = (bf16[256,2048]{1,0:T(8,128)(2,1)S(1)}, bf16[256,2048]{1,0:T(8,128)(2,1)}, u32[]{:S(2)}) copy-start(bf16[256,2048]{1,0:T(8,128)(2,1)} %param.11) | copy-start | bytes 3145732
  6.5 42.0 %all-gather.7.cloned.1.call-start = ((), (), s32[]{:S(2)}) async-start(), calls=%async_computation.2 | async-start | bytes 4718592 | tf_op jit(solution)/shard_map/all_gather | solution.py:23
  7.3 100.8 %reduce-scatter.3.cloned.1.call-start = ((), (), s32[]{:S(2)}) async-start(), calls=%async_computation.3 | async-start | bytes 4718592 | tf_op jit(solution)/shard_map/reduce_scatter | solution.py:32
  56.7 0.7 copy-start.1
  56.8 81.7 %all-gather.9.cloned.1.call-start = ((), (), s32[]{:S(2)}) async-start(), calls=%async_computation.4 | async-start | bytes 2359296 | tf_op jit(solution)/shard_map/all_gather | solution.py:34
  110.6 70.6 %all-gather.11.cloned.1.call-start = ((), (), s32[]{:S(2)}) async-start(), calls=%async_computation.5 | async-start | bytes 4718592 | tf_op jit(solution)/shard_map/all_gather | solution.py:38
  143.7 119.7 %copy-start.2 = (f32[2048]{0:T(1024)S(1)}, f32[2048]{0:T(1024)}, u32[]{:S(2)}) copy-start(f32[2048]{0:T(1024)} %param.12) | copy-start | bytes 24580
  143.7 119.7 %all-gather.13.cloned.1.call-start = ((), (), s32[]{:S(2)}) async-start(), calls=%async_computation.6 | async-start | bytes 5242880 | tf_op jit(solution)/shard_map/all_gather | solution.py:47
  144.3 199.8 %all-gather.15.cloned.1.call-start = ((), (), s32[]{:S(2)}) async-start(), calls=%async_computation.7 | async-start | bytes 5242880 | tf_op jit(solution)/shard_map/all_gather | solution.py:53
  144.8 280.0 %all-gather.17.cloned.1.call-start = ((), (), s32[]{:S(2)}) async-start(), calls=%async_computation.8 | async-start | bytes 5242880 | tf_op jit(solution)/shard_map/all_gather | solution.py:57
  145.6 344.2 %reduce-scatter.5.cloned.1.call-start = ((), (), s32[]{:S(2)}) async-start(), calls=%async_computation.9 | async-start | bytes 4718592 | tf_op jit(solution)/shard_map/reduce_scatter | solution.py:58
Sparse Core Ops, SparseCore 0:
  9.2 39.2 all-gather.6
  56.9 51.0 reduce-scatter.2
  110.7 27.7 all-gather.8
  143.8 37.3 all-gather.10
  182.6 80.7 all-gather.12
  264.8 79.2 all-gather.14
  345.6 79.2 all-gather.16
  440.2 49.5 reduce-scatter.4
where the time goes:
time: 499 us
  waiting for transfers between devices  438 us (88%)
  matrix products  38.4 us (8%)
  between operations  13.5 us (3%)
  other arithmetic  5.68 us (1%)
    all_gather x1, waiting for transfers between devices, shards(): down_full = lax.all_gather(w_down, 'dp', axis=1, tiled=True)  80.8 us
    all_gather x1, waiting for transfers between devices, shards(): lax.all_gather(w_gate, 'dp', axis=0, tiled=True)  79.1 us
    all_gather x1, waiting for transfers between devices, shards(): lax.all_gather(w_up, 'dp', axis=0, tiled=True)  70.7 us
    reduce_scatter x1, waiting for transfers between devices, shards(): lax.psum_scatter(partial_value, 'mp', scatter_dimension=1, tiled=True)  50.5 us
    reduce_scatter x1, waiting for transfers between devices, shards(): lax.psum_scatter(jnp.einsum('ucf,fk->kuc', hidden, down_full, preferred_e...  49.7 us
    all_gather x1, waiting for transfers between devices, shards(): lax.all_gather(candidates, 'mp', axis=1, tiled=True)  41.3 us
    all_gather x1, waiting for transfers between devices, shards(): whole = lax.all_gather(pooled, 'mp', axis=1, tiled=True)  35.4 us
    all_gather x1, waiting for transfers between devices, shards(): probs = lax.all_gather(probs_share, 'mp', axis=1, tiled=True)  27.9 us
  transfers between devices with their start and end apart: 8, of which 8 were waited for; matrix products, arithmetic and copies ran while one was open for 3% of the time, Pallas kernels for 0%

commit v1 on v0

v1 whole, which is shorter than its diff:
```python
import math

import jax
import jax.numpy as jnp
from jax import lax
from jax.experimental import pallas as pl
from jax.experimental.pallas import tpu as pltpu
from jax.sharding import PartitionSpec as P


VMEM_WHOLE = pl.BlockSpec(memory_space=pltpu.VMEM)
SMEM_WHOLE = pl.BlockSpec(memory_space=pltpu.SMEM)
IN_PLACE = pl.BlockSpec(memory_space=pltpu.HBM)


def pick(x, index, size, axis):
    return lax.dynamic_slice_in_dim(x, index * size, size, axis)


def swap(x, axis_name, count, offset):
    return lax.ppermute(x, axis_name, [(i, i ^ offset) for i in range(count)])


def dot(a, b, dims):
    return lax.dot_general(a, b, (dims, ((), ())), preferred_element_type=jnp.float32)


def score_parts(where, cand_parts, bilinears, behaviors, rows, which):
    chips = len(cand_parts)
    group, chip_width, cands = cand_parts[0].shape
    width, features = bilinears[0].shape
    users, _, length = behaviors[0].shape
    blocks = cands // rows
    steps = group // 2

    def body(where_ref, *refs):
        cand_refs = refs[:chips]
        bilinear_refs = refs[chips : chips + 2]
        behavior_refs = refs[chips + 2 : chips + 4]
        out_refs = refs[chips + 4 :]
        chip, core = where_ref[0], where_ref[1]
        step = pl.program_id(0)
        queries = []
        for bilinear_ref in bilinear_refs:
            total = jnp.zeros((width, 2 * cands), jnp.float32)
            for t in range(chips):
                pair = jnp.concatenate([cand_refs[t][0], cand_refs[t][1]], axis=1)
                start = pl.multiple_of((chip ^ t) * chip_width, chip_width)
                if width % 128:
                    swapped = jnp.concatenate([pair[width:], pair[:width]], axis=0)
                    pair = jnp.where(core == 0, pair, swapped)
                    total += dot(bilinear_ref[:, pl.ds(start, chip_width)], pair, ((1,), (0,)))
                    continue
                for side in range(2):
                    at = pl.ds(pl.multiple_of(start + (core ^ side) * width, width), width)
                    part = pair[side * width : (side + 1) * width]
                    total += dot(bilinear_ref[:, at], part, ((1,), (0,)))
            queries.append(total.astype(jnp.bfloat16))
        for i in range(2):
            scores = jnp.zeros((cands, length), jnp.float32)
            for query, behavior_ref in zip(queries, behavior_refs):
                mine = query[:, i * cands : (i + 1) * cands]
                scores += dot(mine, behavior_ref[i], ((0,), (0,)))
            for b in range(blocks):
                target = chip ^ ((2 * step + i) * blocks + b)
                for t in range(chips):

                    @pl.when(target == t)
                    def _():
                        out_refs[t][...] = scores[b * rows : (b + 1) * rows]

    pair_block = lambda shape: pl.BlockSpec((2,) + shape, lambda i, w: (i, 0, 0))
    mine_block = lambda shape: pl.BlockSpec((2,) + shape, lambda i, w: ((w[1] * (users // 2) + which * group) // 2 + i, 0, 0))
    whole_block = lambda shape: pl.BlockSpec(shape, lambda i, w: (0, 0))
    return pl.pallas_call(
        body,
        grid_spec=pltpu.PrefetchScalarGridSpec(
            num_scalar_prefetch=1,
            grid=(steps,),
            in_specs=[pair_block((chip_width, cands))] * chips
            + [whole_block((width, features))] * 2
            + [mine_block((width, length))] * 2,
            out_specs=[whole_block((rows, length))] * chips,
        ),
        out_shape=[jax.ShapeDtypeStruct((rows, length), jnp.float32)] * chips,
        name="scores",
    )(where, *cand_parts, *bilinears, *behaviors)


def softmax_rows(where, lengths, parts, cands, features, which):
    rows, length = parts[0].shape
    half = lengths.shape[0] // 2

    def body(where_ref, lengths_ref, *refs):
        part_refs, out_ref = refs[:-1], refs[-1]
        user = where_ref[1] * half + which * (half // 2) + where_ref[0] * rows // cands
        total = part_refs[0][...]
        for part_ref in part_refs[1:]:
            total += part_ref[...]
        scores = total * (1.0 / math.sqrt(features))
        live = lax.broadcasted_iota(jnp.int32, (rows, length), 1) < lengths_ref[user]
        masked = jnp.where(live, scores, -1e30)
        highest = jnp.max(masked, axis=-1, keepdims=True)
        expons = jnp.where(live, jnp.exp(masked - highest), 0.0)
        out_ref[...] = (expons / jnp.sum(expons, axis=-1, keepdims=True)).astype(jnp.bfloat16)

    return pl.pallas_call(
        body,
        in_specs=[SMEM_WHOLE, SMEM_WHOLE] + [VMEM_WHOLE] * len(parts),
        out_specs=VMEM_WHOLE,
        out_shape=jax.ShapeDtypeStruct((rows, length), jnp.bfloat16),
        name="softmax",
    )(where, lengths, *parts)


def pool(where, prob_parts, behaviors, cands, which):
    chips = len(prob_parts)
    rows, length = prob_parts[0].shape
    users, width, _ = behaviors[0].shape
    half = users // 2
    group = half // 2

    def body(where_ref, *refs):
        prob_refs = refs[:chips]
        own_ref, other_ref, out_ref, probs = refs[chips:]
        chip, core = where_ref[0], where_ref[1]
        step = pl.program_id(0)

        @pl.when(step == 0)
        def _():
            for t in range(chips):
                start = pl.multiple_of((chip ^ t) * rows, rows)
                probs[pl.ds(start, rows), :] = prob_refs[t][...]

        mine = probs[pl.ds(pl.multiple_of(step * cands, cands), cands), :]
        for side, ref in ((core, own_ref), (1 - core, other_ref)):
            start = pl.multiple_of(side * width, width)
            out_ref[0, pl.ds(start, width), :] = dot(ref[0], mine, ((1,), (1,))).astype(
                jnp.bfloat16
            )

    mine_block = pl.BlockSpec(
        (1, width, length), lambda i, w: (w[1] * half + which * group + i, 0, 0)
    )
    return pl.pallas_call(
        body,
        grid_spec=pltpu.PrefetchScalarGridSpec(
            num_scalar_prefetch=1,
            grid=(group,),
            in_specs=[pl.BlockSpec((rows, length), lambda i, w: (0, 0))] * chips
            + [mine_block] * 2,
            out_specs=pl.BlockSpec((1, 2 * width, cands), lambda i, w: (i, 0, 0)),
            scratch_shapes=[pltpu.VMEM((group * cands, length), jnp.bfloat16)],
        ),
        out_shape=jax.ShapeDtypeStruct((group, 2 * width, cands), jnp.bfloat16),
        name="pool",
    )(where, *prob_parts, *behaviors)


def pack_weights(where, arrays, axis, row=None, lanes=0):
    units = arrays[0].shape[axis] // 2
    depth = arrays[0].shape[1 - axis]
    count = len(arrays)

    def body(where_ref, *refs):
        for which in range(2):
            start = pl.multiple_of((where_ref[3] ^ which) * units, units)
            for i in range(count):
                if axis == 1:
                    value = refs[i][:, pl.ds(start, units)]
                    refs[count + which][i * units : (i + 1) * units, :] = value.T
                else:
                    refs[extra + which][...] = refs[i][pl.ds(start, units), :].T
        if row is not None:
            refs[-1][...] = jnp.broadcast_to(refs[count][...], (lanes, row.shape[1])).T

    shape = (count * units, depth) if axis == 1 else (depth, units)
    out_shape = [jax.ShapeDtypeStruct(shape, jnp.bfloat16)] * 2
    if row is not None:
        arrays = (*arrays, row)
        out_shape += [jax.ShapeDtypeStruct((row.shape[1], lanes), row.dtype)]
    extra = len(arrays)
    return pl.pallas_call(
        body,
        in_specs=[SMEM_WHOLE] + [VMEM_WHOLE] * extra,
        out_specs=[VMEM_WHOLE] * len(out_shape),
        out_shape=out_shape,
        name="pack",
    )(where, *arrays)


def start_loads(sems, base, pairs):
    copies = []
    for i, (source, target) in enumerate(pairs):
        copies.append(pltpu.make_async_copy(source, target, sems.at[base + i]))
        copies[-1].start()
    return copies


def normalize(raw, normed, gain_ref):
    users, features, cands = raw.shape
    chunk = 256 if features % 256 == 0 else features
    for u in range(users):

        def square(k, total):
            rows = pl.ds(pl.multiple_of(k * chunk, chunk), chunk)
            values = raw[u, rows, :].astype(jnp.float32)
            return total + jnp.sum(values * values, axis=0, keepdims=True)

        total = lax.fori_loop(0, features // chunk, square, jnp.zeros((1, cands), jnp.float32))
        scale = lax.rsqrt(total * (1.0 / features) + 1e-06)

        def apply(k, carry):
            rows = pl.ds(pl.multiple_of(k * chunk, chunk), chunk)
            values = raw[u, rows, :].astype(jnp.float32)
            normed[rows, u * cands : (u + 1) * cands] = (
                values * scale * gain_ref[rows, :]
            ).astype(jnp.bfloat16)
            return carry

        lax.fori_loop(0, features // chunk, apply, 0)


def feed_forward(where, groups, orders, gain, expand, down, hidden=None):
    count, chips = len(groups), len(groups[0])
    size, chip_width, cands = groups[0][0].shape
    features = gain.shape[0]
    weights = expand if hidden is None else down
    layers = len(weights[0])
    units = expand[0][0].shape[0] // 2
    block = features // layers
    lanes = size * cands
    expands, downs = hidden is None, down is not None
    outs = chips if orders is None else 2

    def body(where_ref, *refs):
        refs = list(refs)
        take = lambda n: [refs.pop(0) for _ in range(n)]
        chip, layer = where_ref[0], where_ref[2]
        at_chip = lambda t: pl.ds(pl.multiple_of((chip ^ t) * chip_width, chip_width), chip_width)
        at_layer = lambda s: pl.ds(pl.multiple_of((layer ^ s) * block, block), block)
        if expands:
            part_refs = take(count * chips)
            (gain_ref,) = take(1)
            expand_refs = take(2 * layers)
        else:
            (hidden_ref,) = take(1)
        if downs:
            down_refs = take(2 * layers)
            out_refs = take(outs * count)
            if expands:
                (hidden_ref,) = take(1)
        else:
            (hidden_ref,) = take(1)
        (sems,) = take(1)
        if expands:
            raw, normed, wide = take(3)
            part_loads = start_loads(
                sems,
                0,
                [
                    (part_refs[g * chips + t], raw.at[pl.ds(g * size, size), at_chip(t), :])
                    for g in range(count)
                    for t in range(chips)
                ],
            )
            expand_loads = start_loads(
                sems,
                count * chips,
                [
                    (expand_refs[i * layers + s], wide.at[i, :, at_layer(s)])
                    for i in range(2)
                    for s in range(layers)
                ],
            )
        if downs:
            (narrow,) = take(1)
            down_loads = start_loads(
                sems,
                count * chips + 2 * layers,
                [
                    (down_refs[i * layers + s], narrow.at[at_layer(s), pl.ds(i * units, units)])
                    for i in range(2)
                    for s in range(layers)
                ],
            )
        if expands:
            for copy in part_loads:
                copy.wait()
            normalize(raw, normed, gain_ref)
            tile = min(256, units)
            for i in range(2):
                for s in range(layers):
                    expand_loads[i * layers + s].wait()
                for f in range(0, units, tile):
                    gate = dot(wide[i, f : f + tile, :], normed[...], ((1,), (0,)))
                    upward = dot(
                        wide[i, units + f : units + f + tile, :], normed[...], ((1,), (0,))
                    )
                    hidden_ref[i * units + f : i * units + f + tile, :] = (
                        gate / (1.0 + jnp.exp(-gate)) * upward
                    ).astype(jnp.bfloat16)
        if downs:
            for copy in down_loads:
                copy.wait()
            for g in range(count):
                for i in range(chips):
                    target = chips - 1 - i if orders is None else orders[g][i]
                    result = dot(
                        narrow[at_chip(target), :],
                        hidden_ref[:, g * lanes : (g + 1) * lanes],
                        ((1,), (0,)),
                    ).astype(jnp.bfloat16)
                    for u in range(size):
                        mine = result[:, u * cands : (u + 1) * cands]
                        if orders is None:
                            out_refs[chips * g + target][u] = mine
                        else:
                            out_refs[2 * g + (i >= chips // 2)][i % (chips // 2), u] = mine

    total = count * lanes
    hidden_shape = (2 * units, total)
    inputs, in_specs, scratch = [where], [SMEM_WHOLE], []
    if expands:
        inputs += sum(groups, []) + [gain] + expand[0] + expand[1]
        in_specs += [IN_PLACE] * (count * chips) + [VMEM_WHOLE] + [IN_PLACE] * (2 * layers)
        scratch += [
            pltpu.VMEM((count * size, features, cands), jnp.bfloat16),
            pltpu.VMEM((features, total), jnp.bfloat16),
            pltpu.VMEM((2, 2 * units, features), jnp.bfloat16),
        ]
    else:
        inputs += [hidden]
        in_specs += [VMEM_WHOLE]
    scratch = [pltpu.SemaphoreType.DMA((count * chips + 4 * layers,))] + scratch
    if downs:
        inputs += down[0] + down[1]
        in_specs += [IN_PLACE] * (2 * layers)
        shape = (size, chip_width, cands)
        if orders is not None:
            shape = (chips // 2,) + shape
        out_shape = [jax.ShapeDtypeStruct(shape, jnp.bfloat16)] * (outs * count)
        scratch += [pltpu.VMEM((features, 2 * units), jnp.bfloat16)]
        if expands:
            scratch = [pltpu.VMEM(hidden_shape, jnp.bfloat16)] + scratch
    else:
        out_shape = [jax.ShapeDtypeStruct(hidden_shape, jnp.bfloat16)]
    return pl.pallas_call(
        body,
        in_specs=in_specs,
        out_specs=[VMEM_WHOLE] * len(out_shape),
        out_shape=out_shape,
        scratch_shapes=scratch,
        name="feed_forward",
    )(*inputs)


def make_shards(dp_count, mp_count):
    chips = mp_count // 2

    def across(x, t):
        return swap(x, "mp", mp_count, 2 * t)

    def beside(x):
        return swap(x, "mp", mp_count, 1)

    def to_chips(x):
        return [x] + [across(x, t) for t in range(chips - 1, 0, -1)][::-1]

    bits = [1 << i for i in range((chips - 1).bit_length())]

    def doubled(x, order):
        parts = {0: x}
        for bit in order:
            new = {bit: across(x, bit)}
            new.update({t | bit: across(part, bit) for t, part in parts.items() if t})
            parts.update(new)
        return [parts[t] for t in range(chips)]

    def block_order(order):
        blocks = [0]
        for bit in order[::-1]:
            blocks = blocks + [t | bit for t in blocks]
        return blocks

    def halved(near, far, order):
        for bit in order:
            got = across(far, bit)
            total = near.astype(jnp.float32) + got.astype(jnp.float32)
            count = total.shape[0] // 2
            near = total[:count]
            far = total[count:].astype(jnp.bfloat16)
        return total[0]

    def shards(behaviors, candidates, lengths, bilinear, norm_gain, w_gate, w_up, w_down):
        users, width, cands = candidates.shape
        features = bilinear.shape[1]
        half = users // 2
        group = half // 2
        rows = group * cands // chips
        member, layer = lax.axis_index("mp"), lax.axis_index("dp")
        core, chip = member % 2, member // 2
        far_layer = dp_count // 2
        side = layer // far_layer
        where = jnp.stack([chip, core, layer, side]).astype(jnp.int32)

        given_cands = beside(candidates)
        cand_parts = []
        for g in range(2):
            own_cands = jnp.concatenate(
                [pick(x, core * 2 + g, group, 0) for x in (candidates, given_cands)], axis=1
            )
            cand_parts.append(to_chips(own_cands))
        behavior_sides = [behaviors, beside(behaviors)]
        bilinears = [bilinear, beside(bilinear)]

        def layer_swap(x, s):
            return swap(x, "dp", dp_count, s)

        def spread(own, other):
            got = {far_layer: layer_swap(other, far_layer), 0: own}
            for s in range(1, far_layer):
                got[s] = layer_swap(own, s)
            return got

        def forward(got):
            return [
                got[s] if s in got else layer_swap(got[far_layer], s ^ far_layer)
                for s in range(dp_count)
            ]

        expand_got = spread(*pack_weights(where, (w_gate, w_up), 1))
        *down_packs, gain = pack_weights(where, (w_down,), 0, norm_gain[None, :], cands)
        down_got = spread(*down_packs)
        parts, pooled = [], []
        for g in range(2):
            shares = score_parts(where, cand_parts[g], bilinears, behavior_sides, rows, g)
            parts.append([shares[0]] + [across(shares[t], t) for t in range(chips - 1, 0, -1)])
        expand_own = forward(expand_got)
        down_own = forward(down_got)
        for g in range(2):
            probs = softmax_rows(where, lengths, parts[g], cands, features, g)
            prob_parts = to_chips(probs)
            pooled.append(pool(where, prob_parts, behavior_sides, cands, g))
        orders = [bits, bits[::-1]]

        partner_pooled, own_parts, partner_parts = [], [], []
        for g in range(2):
            partner_pooled.append(layer_swap(pooled[g], far_layer))
            own_parts.append(doubled(pooled[g], orders[g]))
            partner_parts.append(to_chips(partner_pooled[g]))

        def besides(pieces):
            other = []
            for piece in pieces:
                other.append(beside(piece))
            return [pieces, other]

        expand = besides(expand_own)
        down = besides(down_own)
        blocks = [block_order(order) for order in orders]
        (own_hidden,) = feed_forward(where, own_parts, blocks, gain, expand, None)
        (partner_hidden,) = feed_forward(where, [partner_parts[0]], None, gain, expand, None)
        totals = []
        for g in range(2):
            shares = feed_forward(
                where, [partner_parts[g]], None, gain, expand, down, (partner_hidden, None)[g]
            )
            total = shares[0].astype(jnp.float32)
            for t in range(chips - 1, 0, -1):
                total = total + across(shares[t], t).astype(jnp.float32)
            totals.append(layer_swap(total.astype(jnp.bfloat16), far_layer))
        own_blocks = feed_forward(where, own_parts, blocks, gain, expand, down, own_hidden)
        interest = []
        for i, order in enumerate(orders):
            interest.append(
                halved(*own_blocks[2 * i : 2 * i + 2], order) + totals[i].astype(jnp.float32)
            )
        interest = jnp.concatenate(interest, axis=0).astype(jnp.bfloat16)
        kept = pick(interest, core, width, 1)
        given = beside(pick(interest, 1 - core, width, 1))
        return jnp.concatenate(
            [jnp.where(core == 0, kept, given), jnp.where(core == 0, given, kept)], axis=0
        )

    return shards


def solution(mesh):
    return jax.shard_map(
        make_shards(mesh.shape["dp"], mesh.shape["mp"]),
        mesh=mesh,
        in_specs=(
            P("dp", "mp", None),
            P("dp", "mp", None),
            P("dp"),
            P("mp", None),
            P(),
            P("dp", "mp"),
            P("dp", "mp"),
            P("mp", "dp"),
        ),
        out_specs=P("dp", "mp", None),
        check_vma=False,
    )
```

time: 499 us -> 287 us (0.58)
  waiting for transfers between devices: 438 us -> 139 us
  starting transfers between devices: 0.46 us -> 68.9 us
  Pallas kernels: 0 us -> 68.1 us
  matrix products: 38.4 us -> 0 us
  between operations: 13.5 us -> 0.47 us
    all_gather x6 -> x0, waiting for transfers between devices: 335 us -> none  [the longest x1 80.8 us: shards(): down_full = lax.all_gather(w_down, 'dp', axis=1, tiled=True)]
    ppermute x0 -> x62, waiting for transfers between devices: none -> 139 us  [swap(): return lax.ppermute(x, axis_name, [(i, i ^ offset) for i in range(count)])]
    reduce_scatter x2 -> x0, waiting for transfers between devices: 100 us -> none  [the longest x1 50.5 us: shards(): lax.psum_scatter(partial_value, 'mp', scatter_dimension=1, tiled=True)]
    ppermute x0 -> x62, starting transfers between devices: none -> 68.9 us  [swap(): return lax.ppermute(x, axis_name, [(i, i ^ offset) for i in range(count)])]
    pallas_call x0 -> x13, Pallas kernels: none -> 68.1 us  [the longest x5 39 us: feed_forward(): pl.pallas_call(body, in_specs=in_specs, out_specs=[VMEM_WHOLE] * len(out_...]
    dot_general x4 -> x0, matrix products: 38.4 us -> none  [the longest x1 15.2 us: shards(): jnp.einsum('ucf,fk->kuc', hidden, down_full, preferred_element_type=jnp.f...]
  transfers between devices with their start and end apart: 8 -> 62, of which waited for: 8 -> 23; matrix products, arithmetic and copies ran while one was open for 3% -> 2% of each run, Pallas kernels for 0% -> 24%
where the time goes in v1:
time: 287 us; the launch traced here: 286 us
  waiting for transfers between devices  139 us (48%)
  starting transfers between devices  68.9 us (24%)
  Pallas kernels  68.1 us (24%)
  other arithmetic  5.2 us (2%)
  local copies, waits for them, and re-layouts  4.66 us (2%)
    ppermute x62, waiting for transfers between devices, swap(): return lax.ppermute(x, axis_name, [(i, i ^ offset) for i in range(count)])  139 us
    ppermute x62, starting transfers between devices, swap(): return lax.ppermute(x, axis_name, [(i, i ^ offset) for i in range(count)])  68.9 us
    pallas_call x5, Pallas kernels, feed_forward(): pl.pallas_call(body, in_specs=in_specs, out_specs=[VMEM_WHOLE] * len(out_...  39 us
    pallas_call x2, Pallas kernels, score_parts(): pl.pallas_call(body, grid_spec=pltpu.PrefetchScalarGridSpec(num_scalar_pr...  11.2 us
    pallas_call x2, Pallas kernels, pool(): pl.pallas_call(body, grid_spec=pltpu.PrefetchScalarGridSpec(num_scalar_pr...  7.47 us
    pallas_call x2, Pallas kernels, pack_weights(): pl.pallas_call(body, in_specs=[SMEM_WHOLE] + [VMEM_WHOLE] * extra, out_sp...  6.29 us
  transfers between devices with their start and end apart: 62, of which 23 were waited for; matrix products, arithmetic and copies ran while one was open for 2% of the time, Pallas kernels for 24%

profile of v1, /device:TPU:0, one launch (start us, length us, event | category | flops | bytes accessed | tf_op | source)
XLA Modules:
  0.0 286.5 jit_solution(661344854903992462)
XLA Ops:
  1.2 2.8 pack.2
  4.0 3.1 %collective-permute-start.34 = (bf16[512,512]{1,0:T(8,128)(2,1)}, bf16[512,512]{1,0:T(8,128)(2,1)S(1)}, u32[]{:S(2)}, u32[]{:S(2)}) collective-permute-start(bf16[512,512]{1,0:T(8,128)(2,1)} %get-tuple-element.41.refs_1_.refs_13_), channel_id=1, source_target_pairs={{0,8},{8,0},{16,24},{24,16},{1,9},{9,1},{17,25},{25,17},{2,10},{10... | collective-permute-start | bytes 1572872 | tf_op jit(solution)/shard_map/ppermute | solution.py:21
  7.1 2.6 collective-permute-start.35
  10.7 1.6 collective-permute-start.1
  12.3 18.2 %collective-permute-done.34.refs_2_.refs_14_ = bf16[512,512]{1,0:T(8,128)(2,1)S(1)} collective-permute-done((bf16[512,512]{1,0:T(8,128)(2,1)}, bf16[512,512]{1,0:T(8,128)(2,1)S(1)}, u32[]{:S(2)}, u32[]{:S(2)}) %collective-permute-start.34) | collective-permute-done | bytes 524320 | tf_op jit(solution)/shard_map/ppermute | solution.py:21
  30.5 1.7 collective-permute-start.2
  33.0 3.5 %pack.3 = (bf16[1024,512]{1,0:T(8,128)(2,1)}, bf16[1024,512]{1,0:T(8,128)(2,1)}) custom-call(s32[4]{0:T(128)} %pad_add_fusion.where_ref, bf16[512,1024]{1,0:T(8,128)(2,1)} %refs_0_.3, bf16[512,1024]{1,0:T(8,128)(2,1)} %refs_1_.1), custom_call_target="tpu_custom_call" | custom-call | tf_op jit(solution)/shard_map/pack/pallas_call | solution.py:183
  36.9 2.4 collective-permute-start.3
  40.0 7.0 %collective-permute-done.3.refs_3_ = bf16[2,512,128]{2,1,0:T(8,128)(2,1)S(1)} collective-permute-done((bf16[2,512,128]{2,1,0:T(8,128)(2,1)S(1)}, bf16[2,512,128]{2,1,0:T(8,128)(2,1)S(1)}, u32[]{:S(2)}, u32[]{:S(2)}) %collective-permute-start.3) | collective-permute-done | bytes 262176 | tf_op jit(solution)/shard_map/ppermute | solution.py:21
  47.0 1.5 collective-permute-start.16
  48.5 3.3 %collective-permute-done.15.refs_1_ = bf16[2,512,128]{2,1,0:T(8,128)(2,1)S(1)} collective-permute-done((bf16[2,512,128]{2,1,0:T(8,128)(2,1)S(1)}, bf16[2,512,128]{2,1,0:T(8,128)(2,1)S(1)}, u32[]{:S(2)}, u32[]{:S(2)}) %collective-permute-start.15) | collective-permute-done | bytes 262176 | tf_op jit(solution)/shard_map/ppermute | solution.py:21
  52.5 2.7 collective-permute-start.27
  55.1 1.4 collective-permute-start.17
  56.6 6.7 %collective-permute-done.17.refs_3_ = bf16[2,512,128]{2,1,0:T(8,128)(2,1)} collective-permute-done((bf16[2,512,128]{2,1,0:T(8,128)(2,1)S(1)}, bf16[2,512,128]{2,1,0:T(8,128)(2,1)}, u32[]{:S(2)}, u32[]{:S(2)}) %collective-permute-start.17) | collective-permute-done | bytes 262176 | tf_op jit(solution)/shard_map/ppermute | solution.py:21
  63.6 21.9 %collective-permute-done.28.refs_11_.refs_7_ = bf16[1024,512]{1,0:T(8,128)(2,1)S(1)} collective-permute-done((bf16[1024,512]{1,0:T(8,128)(2,1)}, bf16[1024,512]{1,0:T(8,128)(2,1)S(1)}, u32[]{:S(2)}, u32[]{:S(2)}) %collective-permute-start.28) | collective-permute-done | bytes 1048608 | tf_op jit(solution)/shard_map/ppermute | solution.py:21
  85.5 16.2 %collective-permute-done.27.refs_10_.refs_6_ = bf16[1024,512]{1,0:T(8,128)(2,1)S(1)} collective-permute-done((bf16[1024,512]{1,0:T(8,128)(2,1)}, bf16[1024,512]{1,0:T(8,128)(2,1)S(1)}, u32[]{:S(2)}, u32[]{:S(2)}) %collective-permute-start.27) | collective-permute-done | bytes 1048608 | tf_op jit(solution)/shard_map/ppermute | solution.py:21
  101.7 11.3 %collective-permute-done.36.refs_4_.refs_16_ = bf16[512,512]{1,0:T(8,128)(2,1)} collective-permute-done((bf16[512,512]{1,0:T(8,128)(2,1)}, bf16[512,512]{1,0:T(8,128)(2,1)}, u32[]{:S(2)}, u32[]{:S(2)}) %collective-permute-start.36) | collective-permute-done | bytes 524320 | tf_op jit(solution)/shard_map/ppermute | solution.py:21
  113.6 5.6 %scores.2 = (f32[64,1024]{1,0:T(8,128)}, f32[64,1024]{1,0:T(8,128)}, f32[64,1024]{1,0:T(8,128)}, f32[64,1024]{1,0:T(8,128)}) custom-call(s32[4]{0:T(128)} %pad_add_fusion.where_ref, bf16[2,512,128]{2,1,0:T(8,128)(2,1)} %copy-done.7, bf16[2,512,128]{2,1,0:T(8,128)(2,1)} %copy-done.19, bf16[2,512,128]{2,1,0:T(8,128)(2,1)} %copy-done.20, ...), custom_call_target="tpu_custom_call" | custom-call | tf_op jit(solution)/shard_map/scores/pallas_call | solution.py:75
  119.2 1.5 collective-permute-start.6
  120.7 1.6 collective-permute-start.7
  122.9 11.2 %collective-permute-done.29.refs_12_.refs_8_ = bf16[1024,512]{1,0:T(8,128)(2,1)} collective-permute-done((bf16[1024,512]{1,0:T(8,128)(2,1)S(1)}, bf16[1024,512]{1,0:T(8,128)(2,1)}, u32[]{:S(2)}, u32[]{:S(2)}) %collective-permute-start.29) | collective-permute-done | bytes 1048608 | tf_op jit(solution)/shard_map/ppermute | solution.py:21
  134.5 5.6 %scores.3 = (f32[64,1024]{1,0:T(8,128)}, f32[64,1024]{1,0:T(8,128)}, f32[64,1024]{1,0:T(8,128)}, f32[64,1024]{1,0:T(8,128)}) custom-call(s32[4]{0:T(128)} %pad_add_fusion.where_ref, bf16[2,512,128]{2,1,0:T(8,128)(2,1)} %copy-done.6, bf16[2,512,128]{2,1,0:T(8,128)(2,1)} %copy-done.16, bf16[2,512,128]{2,1,0:T(8,128)(2,1)} %copy-done.18, ...), custom_call_target="tpu_custom_call" | custom-call | tf_op jit(solution)/shard_map/scores/pallas_call | solution.py:75
  140.1 1.5 collective-permute-start.18
  141.7 1.5 collective-permute-start.19
  143.2 6.5 %collective-permute-done.18.refs_1_ = f32[64,1024]{1,0:T(8,128)S(1)} collective-permute-done((f32[64,1024]{1,0:T(8,128)}, f32[64,1024]{1,0:T(8,128)S(1)}, u32[]{:S(2)}, u32[]{:S(2)}) %collective-permute-start.18) | collective-permute-done | bytes 262176 | tf_op jit(solution)/shard_map/ppermute | solution.py:21
  149.7 1.5 collective-permute-start.20
  151.2 2.1 softmax.2.refs_0_
  153.3 1.9 collective-permute-done.19.refs_2_
  156.0 1.3 collective-permute-done.20.refs_3_
  157.8 3.0 %collective-permute-done.9.refs_1_ = bf16[64,1024]{1,0:T(8,128)(2,1)S(1)} collective-permute-done((bf16[64,1024]{1,0:T(8,128)(2,1)}, bf16[64,1024]{1,0:T(8,128)(2,1)S(1)}, u32[]{:S(2)}, u32[]{:S(2)}) %collective-permute-start.9) | collective-permute-done | bytes 131104 | tf_op jit(solution)/shard_map/ppermute | solution.py:21
  160.9 1.5 collective-permute-start.11
  162.3 2.1 softmax.3.refs_0_
  165.0 2.5 collective-permute-done.11.refs_3_
  168.1 3.8 %pool.2.refs_0_ = bf16[2,512,128]{2,1,0:T(8,128)(2,1)} custom-call(s32[4]{0:T(128)} %pad_add_fusion.where_ref, bf16[64,1024]{1,0:T(8,128)(2,1)} %softmax.2.refs_0_, bf16[64,1024]{1,0:T(8,128)(2,1)} %copy-done.36, bf16[64,1024]{1,0:T(8,128)(2,1)} %copy-done.38, bf16[64,1024]{1,0:T(8,128)(2,1)} %copy-done.39, bf16[8,256,1024]{2,1,0:T(8,128)(2,1)} %refs_4_.7, ...), custom_call_target="tpu_custom_call" | custom-call | tf_op jit(solution)/shard_map/pool/pallas_call | solution.py:145
  172.0 1.7 collective-permute-start.12
  173.7 1.3 collective-permute-start.23
  175.0 6.4 %collective-permute-done.23.refs_3_ = bf16[64,1024]{1,0:T(8,128)(2,1)S(1)} collective-permute-done((bf16[64,1024]{1,0:T(8,128)(2,1)S(1)}, bf16[64,1024]{1,0:T(8,128)(2,1)S(1)}, u32[]{:S(2)}, u32[]{:S(2)}) %collective-permute-start.23) | collective-permute-done | bytes 131104 | tf_op jit(solution)/shard_map/ppermute | solution.py:21
  182.3 3.7 %pool.3.refs_4_ = bf16[2,512,128]{2,1,0:T(8,128)(2,1)} custom-call(s32[4]{0:T(128)} %pad_add_fusion.where_ref, bf16[64,1024]{1,0:T(8,128)(2,1)} %softmax.3.refs_0_, bf16[64,1024]{1,0:T(8,128)(2,1)} %copy-done.35, bf16[64,1024]{1,0:T(8,128)(2,1)} %copy-done.37, bf16[64,1024]{1,0:T(8,128)(2,1)} %copy-done.40, bf16[8,256,1024]{2,1,0:T(8,128)(2,1)} %refs_4_.7, ...), custom_call_target="tpu_custom_call" | custom-call | tf_op jit(solution)/shard_map/pool/pallas_call | solution.py:145
  187.1 2.6 collective-permute-start.53
  190.6 1.2 collective-permute-start.45
  191.8 3.3 %collective-permute-start.46 = (bf16[2,512,128]{2,1,0:T(8,128)(2,1)S(1)}, bf16[2,512,128]{2,1,0:T(8,128)(2,1)S(1)}, u32[]{:S(2)}, u32[]{:S(2)}) collective-permute-start(bf16[2,512,128]{2,1,0:T(8,128)(2,1)S(1)} %collective-permute-done.43.refs_0_), channel_id=1, source_target_pairs={{0,6},{1,7},{2,4},{3,5},{4,2},{5,3},{6,0},{7,1},{8,14},{9,15},{10,... | collective-permute-start | bytes 786440 | tf_op jit(solution)/shard_map/ppermute | solution.py:21
  195.1 4.2 %collective-permute-done.25.refs_6_ = bf16[2,512,128]{2,1,0:T(8,128)(2,1)S(1)} collective-permute-done((bf16[2,512,128]{2,1,0:T(8,128)(2,1)}, bf16[2,512,128]{2,1,0:T(8,128)(2,1)S(1)}, u32[]{:S(2)}, u32[]{:S(2)}) %collective-permute-start.25) | collective-permute-done | bytes 262176 | tf_op jit(solution)/shard_map/ppermute | solution.py:21
  200.1 1.1 collective-permute-start.14
  202.2 5.5 %collective-permute-done.45.refs_2_ = bf16[2,512,128]{2,1,0:T(8,128)(2,1)S(1)} collective-permute-done((bf16[2,512,128]{2,1,0:T(8,128)(2,1)S(1)}, bf16[2,512,128]{2,1,0:T(8,128)(2,1)S(1)}, u32[]{:S(2)}, u32[]{:S(2)}) %collective-permute-start.45) | collective-permute-done | bytes 262176 | tf_op jit(solution)/shard_map/ppermute | solution.py:21
  208.6 1.1 collective-permute-start.55
  209.7 7.3 %feed_forward.7.refs_0_ = bf16[1024,256]{1,0:T(8,128)(2,1)} custom-call(s32[4]{0:T(128)} %pad_add_fusion.where_ref, bf16[2,512,128]{2,1,0:T(8,128)(2,1)} %copy-done.23, bf16[2,512,128]{2,1,0:T(8,128)(2,1)} %copy-done.28, bf16[2,512,128]{2,1,0:T(8,128)(2,1)} %copy-done.29, bf16[2,512,128]{2,1,0:T(8,128)(2,1)} %copy-done.30, ...), custom_call_target="tpu_custom_call" | custom-call | tf_op jit(solution)/shard_map/feed_forward/pallas_call | solution.py:348
  217.0 1.5 collective-permute-start.56
  218.6 5.5 %feed_forward.8 = (bf16[2,512,128]{2,1,0:T(8,128)(2,1)}, bf16[2,512,128]{2,1,0:T(8,128)(2,1)}, bf16[2,512,128]{2,1,0:T(8,128)(2,1)}, bf16[2,512,128]{2,1,0:T(8,128)(2,1)}) custom-call(s32[4]{0:T(128)} %pad_add_fusion.where_ref, bf16[1024,256]{1,0:T(8,128)(2,1)} %feed_forward.7.refs_0_, bf16[512,512]{1,0:T(8,128)(2,1)} %get-tuple-element.41.refs_1_.refs_13_, ...), custom_call_target="tpu_custom_call" | custom-call | tf_op jit(solution)/shard_map/feed_forward/pallas_call | solution.py:348
  225.8 1.1 collective-permute-start.48
  226.9 1.5 collective-permute-start.47
  228.4 10.8 %feed_forward.5.refs_0_ = bf16[1024,512]{1,0:T(8,128)(2,1)} custom-call(s32[4]{0:T(128)} %pad_add_fusion.where_ref, bf16[2,512,128]{2,1,0:T(8,128)(2,1)} %pool.2.refs_0_, bf16[2,512,128]{2,1,0:T(8,128)(2,1)} %copy-done.15, bf16[2,512,128]{2,1,0:T(8,128)(2,1)} %copy-done.17, bf16[2,512,128]{2,1,0:T(8,128)(2,1)} %copy-done.26, ...), custom_call_target="tpu_custom_call" | custom-call | tf_op jit(solution)/shard_map/feed_forward/pallas_call | solution.py:348
  239.1 6.8 %feed_forward.6 = (bf16[2,2,512,128]{3,2,1,0:T(8,128)(2,1)}, bf16[2,2,512,128]{3,2,1,0:T(8,128)(2,1)}, bf16[2,2,512,128]{3,2,1,0:T(8,128)(2,1)}, bf16[2,2,512,128]{3,2,1,0:T(8,128)(2,1)}) custom-call(s32[4]{0:T(128)} %pad_add_fusion.where_ref, bf16[1024,512]{1,0:T(8,128)(2,1)} %feed_forward.5.refs_0_, bf16[512,512]{1,0:T(8,128)(2,1)} %get-tuple-element.41.refs_1_.refs_13_, ...), custom_call_target="tpu_custom_call" | custom-call | tf_op jit(solution)/shard_map/feed_forward/pallas_call | solution.py:348
  247.7 8.6 %feed_forward.9 = (bf16[2,512,128]{2,1,0:T(8,128)(2,1)}, bf16[2,512,128]{2,1,0:T(8,128)(2,1)}, bf16[2,512,128]{2,1,0:T(8,128)(2,1)}, bf16[2,512,128]{2,1,0:T(8,128)(2,1)}) custom-call(s32[4]{0:T(128)} %pad_add_fusion.where_ref, bf16[2,512,128]{2,1,0:T(8,128)(2,1)} %copy-done.11, bf16[2,512,128]{2,1,0:T(8,128)(2,1)} %copy-done.12, ...), custom_call_target="tpu_custom_call" | custom-call | tf_op jit(solution)/shard_map/feed_forward/pallas_call | solution.py:348
  256.3 1.2 collective-permute-start.59
  258.4 1.5 collective-permute-start.57
  259.9 1.1 collective-permute-start.51
  261.2 1.8 collective-permute-done.59
  263.0 2.6 collective-permute-start.50
  265.5 1.8 collective-permute-done.58
  268.5 4.4 %collective-permute-start.60 = (bf16[2,512,128]{2,1,0:T(8,128)(2,1)S(1)}, bf16[2,512,128]{2,1,0:T(8,128)(2,1)S(1)}, u32[]{:S(2)}, u32[]{:S(2)}) collective-permute-start(bf16[2,512,128]{2,1,0:T(8,128)(2,1)S(1)} %add_convert_fusion), channel_id=1, source_target_pairs={{0,16},{8,24},{16,0},{24,8},{1,17},{9,25},{17,1},{25,9},{2,18},{10... | collective-permute-start | bytes 786440 | tf_op jit(solution)/shard_map/ppermute | solution.py:21
  273.9 1.4 collective-permute-done.51
  277.1 2.5 collective-permute-done.42
  280.6 2.2 collective-permute-done.52
  284.0 1.5 collective-permute-done.61
  (171 shorter events, 26.5 us)
Async XLA Ops:
  0.0 113.1 %collective-permute-start.5 = (bf16[8,256,1024]{2,1,0:T(8,128)(2,1)}, bf16[8,256,1024]{2,1,0:T(8,128)(2,1)}, u32[]{:S(2)}, u32[]{:S(2)}) collective-permute-start(bf16[8,256,1024]{2,1,0:T(8,128)(2,1)} %refs_4_.7), channel_id=1, source_target_pairs={{0,1},{1,0},{2,3},{3,2},{4,5},{5,4},{6,7},{7,6},{8,9},{9,8},{10,11... | collective-permute-start | bytes 12582920 | tf_op jit(solution)/shard_map/ppermute | solution.py:21
  0.5 10.1 %collective-permute-start = (bf16[8,256,128]{2,1,0:T(8,128)(2,1)}, bf16[8,256,128]{2,1,0:T(8,128)(2,1)S(1)}, u32[]{:S(2)}, u32[]{:S(2)}) collective-permute-start(bf16[8,256,128]{2,1,0:T(8,128)(2,1)} %param.9), channel_id=1, source_target_pairs={{0,1},{1,0},{2,3},{3,2},{4,5},{5,4},{6,7},{7,6},{8,9},{9,8},{10,11... | collective-permute-start | bytes 1572872 | tf_op jit(solution)/shard_map/ppermute | solution.py:21
  4.0 26.5 %collective-permute-start.34 = (bf16[512,512]{1,0:T(8,128)(2,1)}, bf16[512,512]{1,0:T(8,128)(2,1)S(1)}, u32[]{:S(2)}, u32[]{:S(2)}) collective-permute-start(bf16[512,512]{1,0:T(8,128)(2,1)} %get-tuple-element.41.refs_1_.refs_13_), channel_id=1, source_target_pairs={{0,8},{8,0},{16,24},{24,16},{1,9},{9,1},{17,25},{25,17},{2,10},{10... | collective-permute-start | bytes 1572872 | tf_op jit(solution)/shard_map/ppermute | solution.py:21
  7.1 25.9 %collective-permute-start.35 = (bf16[512,512]{1,0:T(8,128)(2,1)}, bf16[512,512]{1,0:T(8,128)(2,1)S(1)}, u32[]{:S(2)}, u32[]{:S(2)}) collective-permute-start(bf16[512,512]{1,0:T(8,128)(2,1)} %get-tuple-element.42), channel_id=1, source_target_pairs={{0,16},{8,24},{16,0},{24,8},{1,17},{9,25},{17,1},{25,9},{2,18},{10... | collective-permute-start | bytes 1572872 | tf_op jit(solution)/shard_map/ppermute | solution.py:21
  9.6 26.8 %collective-permute-start.37 = (bf16[512,512]{1,0:T(8,128)(2,1)}, bf16[512,512]{1,0:T(8,128)(2,1)S(1)}, u32[]{:S(2)}, u32[]{:S(2)}) collective-permute-start(bf16[512,512]{1,0:T(8,128)(2,1)} %get-tuple-element.41.refs_1_.refs_13_), channel_id=1, source_target_pairs={{0,1},{1,0},{2,3},{3,2},{4,5},{5,4},{6,7},{7,6},{8,9},{9,8},{10,11... | collective-permute-start | bytes 1572872 | tf_op jit(solution)/shard_map/ppermute | solution.py:21
  10.7 26.2 %collective-permute-start.1 = (bf16[2,512,128]{2,1,0:T(8,128)(2,1)S(1)}, bf16[2,512,128]{2,1,0:T(8,128)(2,1)S(1)}, u32[]{:S(2)}, u32[]{:S(2)}) collective-permute-start(bf16[2,512,128]{2,1,0:T(8,128)(2,1)S(1)} %pad_maximum_fusion.1.refs_0_), channel_id=1, source_target_pairs={{0,2},{1,3},{2,0},{3,1},{4,6},{5,7},{6,4},{7,5},{8,10},{9,11},{10,... | collective-permute-start | bytes 786440 | tf_op jit(solution)/shard_map/ppermute | solution.py:21
  30.5 8.9 %collective-permute-start.2 = (bf16[2,512,128]{2,1,0:T(8,128)(2,1)S(1)}, bf16[2,512,128]{2,1,0:T(8,128)(2,1)S(1)}, u32[]{:S(2)}, u32[]{:S(2)}) collective-permute-start(bf16[2,512,128]{2,1,0:T(8,128)(2,1)S(1)} %pad_maximum_fusion.1.refs_0_), channel_id=1, source_target_pairs={{0,4},{1,5},{2,6},{3,7},{4,0},{5,1},{6,2},{7,3},{8,12},{9,13},{10,... | collective-permute-start | bytes 786440 | tf_op jit(solution)/shard_map/ppermute | solution.py:21
  33.0 30.2 %collective-permute-start.4 = (bf16[256,2048]{1,0:T(8,128)(2,1)}, bf16[256,2048]{1,0:T(8,128)(2,1)}, u32[]{:S(2)}, u32[]{:S(2)}) collective-permute-start(bf16[256,2048]{1,0:T(8,128)(2,1)} %refs_4_.6), channel_id=1, source_target_pairs={{0,1},{1,0},{2,3},{3,2},{4,5},{5,4},{6,7},{7,6},{8,9},{9,8},{10,11... | collective-permute-start | bytes 3145736 | tf_op jit(solution)/shard_map/ppermute | solution.py:21
  36.5 49.0 %collective-permute-start.28 = (bf16[1024,512]{1,0:T(8,128)(2,1)}, bf16[1024,512]{1,0:T(8,128)(2,1)S(1)}, u32[]{:S(2)}, u32[]{:S(2)}) collective-permute-start(bf16[1024,512]{1,0:T(8,128)(2,1)} %get-tuple-element.40), channel_id=1, source_target_pairs={{0,16},{8,24},{16,0},{24,8},{1,17},{9,25},{17,1},{25,9},{2,18},{10... | collective-permute-start | bytes 3145736 | tf_op jit(solution)/shard_map/ppermute | solution.py:21
  36.9 10.1 %collective-permute-start.3 = (bf16[2,512,128]{2,1,0:T(8,128)(2,1)S(1)}, bf16[2,512,128]{2,1,0:T(8,128)(2,1)S(1)}, u32[]{:S(2)}, u32[]{:S(2)}) collective-permute-start(bf16[2,512,128]{2,1,0:T(8,128)(2,1)S(1)} %pad_maximum_fusion.1.refs_0_), channel_id=1, source_target_pairs={{0,6},{1,7},{2,4},{3,5},{4,2},{5,3},{6,0},{7,1},{8,14},{9,15},{10,... | collective-permute-start | bytes 786440 | tf_op jit(solution)/shard_map/ppermute | solution.py:21
  39.4 79.8 %copy-start.6 = (bf16[2,512,128]{2,1,0:T(8,128)(2,1)}, bf16[2,512,128]{2,1,0:T(8,128)(2,1)S(1)}, u32[]{:S(2)}) copy-start(bf16[2,512,128]{2,1,0:T(8,128)(2,1)S(1)} %pad_maximum_fusion.2.refs_0_) | copy-start | bytes 786436
  39.4 12.4 %collective-permute-start.15 = (bf16[2,512,128]{2,1,0:T(8,128)(2,1)S(1)}, bf16[2,512,128]{2,1,0:T(8,128)(2,1)S(1)}, u32[]{:S(2)}, u32[]{:S(2)}) collective-permute-start(bf16[2,512,128]{2,1,0:T(8,128)(2,1)S(1)} %pad_maximum_fusion.2.refs_0_), channel_id=1, source_target_pairs={{0,2},{1,3},{2,0},{3,1},{4,6},{5,7},{6,4},{7,5},{8,10},{9,11},{10,... | collective-permute-start | bytes 786440 | tf_op jit(solution)/shard_map/ppermute | solution.py:21
  47.0 8.1 %collective-permute-start.16 = (bf16[2,512,128]{2,1,0:T(8,128)(2,1)S(1)}, bf16[2,512,128]{2,1,0:T(8,128)(2,1)S(1)}, u32[]{:S(2)}, u32[]{:S(2)}) collective-permute-start(bf16[2,512,128]{2,1,0:T(8,128)(2,1)S(1)} %pad_maximum_fusion.2.refs_0_), channel_id=1, source_target_pairs={{0,4},{1,5},{2,6},{3,7},{4,0},{5,1},{6,2},{7,3},{8,12},{9,13},{10,... | collective-permute-start | bytes 786440 | tf_op jit(solution)/shard_map/ppermute | solution.py:21
  52.5 49.3 %collective-permute-start.27 = (bf16[1024,512]{1,0:T(8,128)(2,1)}, bf16[1024,512]{1,0:T(8,128)(2,1)S(1)}, u32[]{:S(2)}, u32[]{:S(2)}) collective-permute-start(bf16[1024,512]{1,0:T(8,128)(2,1)} %get-tuple-element.39.refs_9_.refs_5_), channel_id=1, source_target_pairs={{0,8},{8,0},{16,24},{24,16},{1,9},{9,1},{17,25},{25,17},{2,10},{10... | collective-permute-start | bytes 3145736 | tf_op jit(solution)/shard_map/ppermute | solution.py:21
  55.1 8.1 %collective-permute-start.17 = (bf16[2,512,128]{2,1,0:T(8,128)(2,1)S(1)}, bf16[2,512,128]{2,1,0:T(8,128)(2,1)}, u32[]{:S(2)}, u32[]{:S(2)}) collective-permute-start(bf16[2,512,128]{2,1,0:T(8,128)(2,1)S(1)} %pad_maximum_fusion.2.refs_0_), channel_id=1, source_target_pairs={{0,6},{1,7},{2,4},{3,5},{4,2},{5,3},{6,0},{7,1},{8,14},{9,15},{10,... | collective-permute-start | bytes 786440 | tf_op jit(solution)/shard_map/ppermute | solution.py:21
  63.2 56.0 %collective-permute-start.30 = (bf16[1024,512]{1,0:T(8,128)(2,1)}, bf16[1024,512]{1,0:T(8,128)(2,1)S(1)}, u32[]{:S(2)}, u32[]{:S(2)}) collective-permute-start(bf16[1024,512]{1,0:T(8,128)(2,1)} %get-tuple-element.39.refs_9_.refs_5_), channel_id=1, source_target_pairs={{0,1},{1,0},{2,3},{3,2},{4,5},{5,4},{6,7},{7,6},{8,9},{9,8},{10,11... | collective-permute-start | bytes 3145736 | tf_op jit(solution)/shard_map/ppermute | solution.py:21
  63.2 49.8 %collective-permute-start.36 = (bf16[512,512]{1,0:T(8,128)(2,1)}, bf16[512,512]{1,0:T(8,128)(2,1)}, u32[]{:S(2)}, u32[]{:S(2)}) collective-permute-start(bf16[512,512]{1,0:T(8,128)(2,1)} %copy-done.4), channel_id=1, source_target_pairs={{0,8},{8,0},{16,24},{24,16},{1,9},{9,1},{17,25},{25,17},{2,10},{10... | collective-permute-start | bytes 1572872 | tf_op jit(solution)/shard_map/ppermute | solution.py:21
  85.5 48.5 %copy-start = (bf16[1024,512]{1,0:T(8,128)(2,1)}, bf16[1024,512]{1,0:T(8,128)(2,1)S(1)}, u32[]{:S(2)}) copy-start(bf16[1024,512]{1,0:T(8,128)(2,1)S(1)} %collective-permute-done.28.refs_11_.refs_7_) | copy-start | bytes 3145732
  85.5 48.5 %collective-permute-start.29 = (bf16[1024,512]{1,0:T(8,128)(2,1)S(1)}, bf16[1024,512]{1,0:T(8,128)(2,1)}, u32[]{:S(2)}, u32[]{:S(2)}) collective-permute-start(bf16[1024,512]{1,0:T(8,128)(2,1)S(1)} %collective-permute-done.28.refs_11_.refs_7_), channel_id=1, source_target_pairs={{0,8},{8,0},{16,24},{24,16},{1,9},{9,1},{17,25},{25,17},{2,10},{10... | collective-permute-start | bytes 3145736 | tf_op jit(solution)/shard_map/ppermute | solution.py:21
  101.7 19.0 %collective-permute-start.38 = (bf16[512,512]{1,0:T(8,128)(2,1)}, bf16[512,512]{1,0:T(8,128)(2,1)}, u32[]{:S(2)}, u32[]{:S(2)}) collective-permute-start(bf16[512,512]{1,0:T(8,128)(2,1)} %copy-done.3), channel_id=1, source_target_pairs={{0,1},{1,0},{2,3},{3,2},{4,5},{5,4},{6,7},{7,6},{8,9},{9,8},{10,11... | collective-permute-start | bytes 1572872 | tf_op jit(solution)/shard_map/ppermute | solution.py:21
  113.0 7.7 %collective-permute-start.39 = (bf16[512,512]{1,0:T(8,128)(2,1)}, bf16[512,512]{1,0:T(8,128)(2,1)}, u32[]{:S(2)}, u32[]{:S(2)}) collective-permute-start(bf16[512,512]{1,0:T(8,128)(2,1)} %copy-done.4), channel_id=1, source_target_pairs={{0,1},{1,0},{2,3},{3,2},{4,5},{5,4},{6,7},{7,6},{8,9},{9,8},{10,11... | collective-permute-start | bytes 1572872 | tf_op jit(solution)/shard_map/ppermute | solution.py:21
  113.1 9.3 %collective-permute-start.40 = (bf16[512,512]{1,0:T(8,128)(2,1)}, bf16[512,512]{1,0:T(8,128)(2,1)}, u32[]{:S(2)}, u32[]{:S(2)}) collective-permute-start(bf16[512,512]{1,0:T(8,128)(2,1)} %collective-permute-done.36.refs_4_.refs_16_), channel_id=1, source_target_pairs={{0,1},{1,0},{2,3},{3,2},{4,5},{5,4},{6,7},{7,6},{8,9},{9,8},{10,11... | collective-permute-start | bytes 1572872 | tf_op jit(solution)/shard_map/ppermute | solution.py:21
  119.2 14.8 %collective-permute-start.6 = (f32[64,1024]{1,0:T(8,128)}, f32[64,1024]{1,0:T(8,128)S(1)}, u32[]{:S(2)}, u32[]{:S(2)}) collective-permute-start(f32[64,1024]{1,0:T(8,128)} %get-tuple-element.31), channel_id=1, source_target_pairs={{0,6},{1,7},{2,4},{3,5},{4,2},{5,3},{6,0},{7,1},{8,14},{9,15},{10,... | collective-permute-start | bytes 786440 | tf_op jit(solution)/shard_map/ppermute | solution.py:21
  120.7 51.2 %collective-permute-start.31 = (bf16[1024,512]{1,0:T(8,128)(2,1)S(1)}, bf16[1024,512]{1,0:T(8,128)(2,1)}, u32[]{:S(2)}, u32[]{:S(2)}) collective-permute-start(bf16[1024,512]{1,0:T(8,128)(2,1)S(1)} %collective-permute-done.27.refs_10_.refs_6_), channel_id=1, source_target_pairs={{0,1},{1,0},{2,3},{3,2},{4,5},{5,4},{6,7},{7,6},{8,9},{9,8},{10,11... | collective-permute-start | bytes 3145736 | tf_op jit(solution)/shard_map/ppermute | solution.py:21
  120.7 19.4 %collective-permute-start.7 = (f32[64,1024]{1,0:T(8,128)}, f32[64,1024]{1,0:T(8,128)}, u32[]{:S(2)}, u32[]{:S(2)}) collective-permute-start(f32[64,1024]{1,0:T(8,128)} %get-tuple-element.32), channel_id=1, source_target_pairs={{0,4},{1,5},{2,6},{3,7},{4,0},{5,1},{6,2},{7,3},{8,12},{9,13},{10,... | collective-permute-start | bytes 786440 | tf_op jit(solution)/shard_map/ppermute | solution.py:21
  122.3 19.3 %collective-permute-start.8 = (f32[64,1024]{1,0:T(8,128)}, f32[64,1024]{1,0:T(8,128)}, u32[]{:S(2)}, u32[]{:S(2)}) collective-permute-start(f32[64,1024]{1,0:T(8,128)} %get-tuple-element.33), channel_id=1, source_target_pairs={{0,2},{1,3},{2,0},{3,1},{4,6},{5,7},{6,4},{7,5},{8,10},{9,11},{10,... | collective-permute-start | bytes 786440 | tf_op jit(solution)/shard_map/ppermute | solution.py:21
  134.0 52.0 %collective-permute-start.32 = (bf16[1024,512]{1,0:T(8,128)(2,1)S(1)}, bf16[1024,512]{1,0:T(8,128)(2,1)}, u32[]{:S(2)}, u32[]{:S(2)}) collective-permute-start(bf16[1024,512]{1,0:T(8,128)(2,1)S(1)} %collective-permute-done.28.refs_11_.refs_7_), channel_id=1, source_target_pairs={{0,1},{1,0},{2,3},{3,2},{4,5},{5,4},{6,7},{7,6},{8,9},{9,8},{10,11... | collective-permute-start | bytes 3145736 | tf_op jit(solution)/shard_map/ppermute | solution.py:21
  134.0 53.0 %collective-permute-start.33 = (bf16[1024,512]{1,0:T(8,128)(2,1)}, bf16[1024,512]{1,0:T(8,128)(2,1)}, u32[]{:S(2)}, u32[]{:S(2)}) collective-permute-start(bf16[1024,512]{1,0:T(8,128)(2,1)} %collective-permute-done.29.refs_12_.refs_8_), channel_id=1, source_target_pairs={{0,1},{1,0},{2,3},{3,2},{4,5},{5,4},{6,7},{7,6},{8,9},{9,8},{10,11... | collective-permute-start | bytes 3145736 | tf_op jit(solution)/shard_map/ppermute | solution.py:21
  140.1 9.6 %collective-permute-start.18 = (f32[64,1024]{1,0:T(8,128)}, f32[64,1024]{1,0:T(8,128)S(1)}, u32[]{:S(2)}, u32[]{:S(2)}) collective-permute-start(f32[64,1024]{1,0:T(8,128)} %get-tuple-element.35), channel_id=1, source_target_pairs={{0,6},{1,7},{2,4},{3,5},{4,2},{5,3},{6,0},{7,1},{8,14},{9,15},{10,... | collective-permute-start | bytes 786440 | tf_op jit(solution)/shard_map/ppermute | solution.py:21
  141.7 13.6 %collective-permute-start.19 = (f32[64,1024]{1,0:T(8,128)}, f32[64,1024]{1,0:T(8,128)S(1)}, u32[]{:S(2)}, u32[]{:S(2)}) collective-permute-start(f32[64,1024]{1,0:T(8,128)} %get-tuple-element.36), channel_id=1, source_target_pairs={{0,4},{1,5},{2,6},{3,7},{4,0},{5,1},{6,2},{7,3},{8,12},{9,13},{10,... | collective-permute-start | bytes 786440 | tf_op jit(solution)/shard_map/ppermute | solution.py:21
  149.7 7.6 %collective-permute-start.20 = (f32[64,1024]{1,0:T(8,128)}, f32[64,1024]{1,0:T(8,128)S(1)}, u32[]{:S(2)}, u32[]{:S(2)}) collective-permute-start(f32[64,1024]{1,0:T(8,128)} %get-tuple-element.37), channel_id=1, source_target_pairs={{0,2},{1,3},{2,0},{3,1},{4,6},{5,7},{6,4},{7,5},{8,10},{9,11},{10,... | collective-permute-start | bytes 786440 | tf_op jit(solution)/shard_map/ppermute | solution.py:21
  155.2 5.6 %collective-permute-start.9 = (bf16[64,1024]{1,0:T(8,128)(2,1)}, bf16[64,1024]{1,0:T(8,128)(2,1)S(1)}, u32[]{:S(2)}, u32[]{:S(2)}) collective-permute-start(bf16[64,1024]{1,0:T(8,128)(2,1)} %softmax.2.refs_0_), channel_id=1, source_target_pairs={{0,2},{1,3},{2,0},{3,1},{4,6},{5,7},{6,4},{7,5},{8,10},{9,11},{10,... | collective-permute-start | bytes 393224 | tf_op jit(solution)/shard_map/ppermute | solution.py:21
  157.3 7.1 %collective-permute-start.10 = (bf16[64,1024]{1,0:T(8,128)(2,1)}, bf16[64,1024]{1,0:T(8,128)(2,1)S(1)}, u32[]{:S(2)}, u32[]{:S(2)}) collective-permute-start(bf16[64,1024]{1,0:T(8,128)(2,1)} %softmax.2.refs_0_), channel_id=1, source_target_pairs={{0,4},{1,5},{2,6},{3,7},{4,0},{5,1},{6,2},{7,3},{8,12},{9,13},{10,... | collective-permute-start | bytes 393224 | tf_op jit(solution)/shard_map/ppermute | solution.py:21
  160.9 6.6 %collective-permute-start.11 = (bf16[64,1024]{1,0:T(8,128)(2,1)}, bf16[64,1024]{1,0:T(8,128)(2,1)S(1)}, u32[]{:S(2)}, u32[]{:S(2)}) collective-permute-start(bf16[64,1024]{1,0:T(8,128)(2,1)} %softmax.2.refs_0_), channel_id=1, source_target_pairs={{0,6},{1,7},{2,4},{3,5},{4,2},{5,3},{6,0},{7,1},{8,14},{9,15},{10,... | collective-permute-start | bytes 393224 | tf_op jit(solution)/shard_map/ppermute | solution.py:21
  164.4 7.5 %collective-permute-start.21 = (bf16[64,1024]{1,0:T(8,128)(2,1)}, bf16[64,1024]{1,0:T(8,128)(2,1)S(1)}, u32[]{:S(2)}, u32[]{:S(2)}) collective-permute-start(bf16[64,1024]{1,0:T(8,128)(2,1)} %softmax.3.refs_0_), channel_id=1, source_target_pairs={{0,2},{1,3},{2,0},{3,1},{4,6},{5,7},{6,4},{7,5},{8,10},{9,11},{10,... | collective-permute-start | bytes 393224 | tf_op jit(solution)/shard_map/ppermute | solution.py:21
  167.5 6.2 %collective-permute-start.22 = (bf16[64,1024]{1,0:T(8,128)(2,1)}, bf16[64,1024]{1,0:T(8,128)(2,1)S(1)}, u32[]{:S(2)}, u32[]{:S(2)}) collective-permute-start(bf16[64,1024]{1,0:T(8,128)(2,1)} %softmax.3.refs_0_), channel_id=1, source_target_pairs={{0,4},{1,5},{2,6},{3,7},{4,0},{5,1},{6,2},{7,3},{8,12},{9,13},{10,... | collective-permute-start | bytes 393224 | tf_op jit(solution)/shard_map/ppermute | solution.py:21
  171.9 17.7 %collective-permute-start.43 = (bf16[2,512,128]{2,1,0:T(8,128)(2,1)}, bf16[2,512,128]{2,1,0:T(8,128)(2,1)S(1)}, u32[]{:S(2)}, u32[]{:S(2)}) collective-permute-start(bf16[2,512,128]{2,1,0:T(8,128)(2,1)} %pool.2.refs_0_), channel_id=1, source_target_pairs={{0,16},{8,24},{16,0},{24,8},{1,17},{9,25},{17,1},{25,9},{2,18},{10... | collective-permute-start | bytes 786440 | tf_op jit(solution)/shard_map/ppermute | solution.py:21
  172.0 18.6 %collective-permute-start.12 = (bf16[2,512,128]{2,1,0:T(8,128)(2,1)}, bf16[2,512,128]{2,1,0:T(8,128)(2,1)S(1)}, u32[]{:S(2)}, u32[]{:S(2)}) collective-permute-start(bf16[2,512,128]{2,1,0:T(8,128)(2,1)} %pool.2.refs_0_), channel_id=1, source_target_pairs={{0,2},{1,3},{2,0},{3,1},{4,6},{5,7},{6,4},{7,5},{8,10},{9,11},{10,... | collective-permute-start | bytes 786440 | tf_op jit(solution)/shard_map/ppermute | solution.py:21
  173.7 7.7 %collective-permute-start.23 = (bf16[64,1024]{1,0:T(8,128)(2,1)S(1)}, bf16[64,1024]{1,0:T(8,128)(2,1)S(1)}, u32[]{:S(2)}, u32[]{:S(2)}) collective-permute-start(bf16[64,1024]{1,0:T(8,128)(2,1)S(1)} %copy-done.8), channel_id=1, source_target_pairs={{0,6},{1,7},{2,4},{3,5},{4,2},{5,3},{6,0},{7,1},{8,14},{9,15},{10,... | collective-permute-start | bytes 393224 | tf_op jit(solution)/shard_map/ppermute | solution.py:21
  181.4 10.4 %collective-permute-start.13 = (bf16[2,512,128]{2,1,0:T(8,128)(2,1)}, bf16[2,512,128]{2,1,0:T(8,128)(2,1)S(1)}, u32[]{:S(2)}, u32[]{:S(2)}) collective-permute-start(bf16[2,512,128]{2,1,0:T(8,128)(2,1)} %pool.2.refs_0_), channel_id=1, source_target_pairs={{0,4},{1,5},{2,6},{3,7},{4,0},{5,1},{6,2},{7,3},{8,12},{9,13},{10,... | collective-permute-start | bytes 786440 | tf_op jit(solution)/shard_map/ppermute | solution.py:21
  186.0 13.3 %collective-permute-start.25 = (bf16[2,512,128]{2,1,0:T(8,128)(2,1)}, bf16[2,512,128]{2,1,0:T(8,128)(2,1)S(1)}, u32[]{:S(2)}, u32[]{:S(2)}) collective-permute-start(bf16[2,512,128]{2,1,0:T(8,128)(2,1)} %pool.3.refs_4_), channel_id=1, source_target_pairs={{0,4},{1,5},{2,6},{3,7},{4,0},{5,1},{6,2},{7,3},{8,12},{9,13},{10,... | collective-permute-start | bytes 786440 | tf_op jit(solution)/shard_map/ppermute | solution.py:21
  187.1 13.1 %collective-permute-start.53 = (bf16[2,512,128]{2,1,0:T(8,128)(2,1)}, bf16[2,512,128]{2,1,0:T(8,128)(2,1)S(1)}, u32[]{:S(2)}, u32[]{:S(2)}) collective-permute-start(bf16[2,512,128]{2,1,0:T(8,128)(2,1)} %pool.3.refs_4_), channel_id=1, source_target_pairs={{0,16},{8,24},{16,0},{24,8},{1,17},{9,25},{17,1},{25,9},{2,18},{10... | collective-permute-start | bytes 786440 | tf_op jit(solution)/shard_map/ppermute | solution.py:21
  189.7 11.6 %collective-permute-start.44 = (bf16[2,512,128]{2,1,0:T(8,128)(2,1)S(1)}, bf16[2,512,128]{2,1,0:T(8,128)(2,1)S(1)}, u32[]{:S(2)}, u32[]{:S(2)}) collective-permute-start(bf16[2,512,128]{2,1,0:T(8,128)(2,1)S(1)} %collective-permute-done.43.refs_0_), channel_id=1, source_target_pairs={{0,2},{1,3},{2,0},{3,1},{4,6},{5,7},{6,4},{7,5},{8,10},{9,11},{10,... | collective-permute-start | bytes 786440 | tf_op jit(solution)/shard_map/ppermute | solution.py:21
  190.6 17.1 %collective-permute-start.45 = (bf16[2,512,128]{2,1,0:T(8,128)(2,1)S(1)}, bf16[2,512,128]{2,1,0:T(8,128)(2,1)S(1)}, u32[]{:S(2)}, u32[]{:S(2)}) collective-permute-start(bf16[2,512,128]{2,1,0:T(8,128)(2,1)S(1)} %collective-permute-done.43.refs_0_), channel_id=1, source_target_pairs={{0,4},{1,5},{2,6},{3,7},{4,0},{5,1},{6,2},{7,3},{8,12},{9,13},{10,... | collective-permute-start | bytes 786440 | tf_op jit(solution)/shard_map/ppermute | solution.py:21
  191.8 16.8 %collective-permute-start.46 = (bf16[2,512,128]{2,1,0:T(8,128)(2,1)S(1)}, bf16[2,512,128]{2,1,0:T(8,128)(2,1)S(1)}, u32[]{:S(2)}, u32[]{:S(2)}) collective-permute-start(bf16[2,512,128]{2,1,0:T(8,128)(2,1)S(1)} %collective-permute-done.43.refs_0_), channel_id=1, source_target_pairs={{0,6},{1,7},{2,4},{3,5},{4,2},{5,3},{6,0},{7,1},{8,14},{9,15},{10,... | collective-permute-start | bytes 786440 | tf_op jit(solution)/shard_map/ppermute | solution.py:21
  199.2 17.8 %collective-permute-start.24 = (bf16[2,512,128]{2,1,0:T(8,128)(2,1)}, bf16[2,512,128]{2,1,0:T(8,128)(2,1)S(1)}, u32[]{:S(2)}, u32[]{:S(2)}) collective-permute-start(bf16[2,512,128]{2,1,0:T(8,128)(2,1)} %pool.3.refs_4_), channel_id=1, source_target_pairs={{0,2},{1,3},{2,0},{3,1},{4,6},{5,7},{6,4},{7,5},{8,10},{9,11},{10,... | collective-permute-start | bytes 786440 | tf_op jit(solution)/shard_map/ppermute | solution.py:21
  200.1 24.0 %collective-permute-start.14 = (bf16[2,512,128]{2,1,0:T(8,128)(2,1)S(1)}, bf16[2,512,128]{2,1,0:T(8,128)(2,1)S(1)}, u32[]{:S(2)}, u32[]{:S(2)}) collective-permute-start(bf16[2,512,128]{2,1,0:T(8,128)(2,1)S(1)} %collective-permute-done.12.refs_1_), channel_id=1, source_target_pairs={{0,4},{1,5},{2,6},{3,7},{4,0},{5,1},{6,2},{7,3},{8,12},{9,13},{10,... | collective-permute-start | bytes 786440 | tf_op jit(solution)/shard_map/ppermute | solution.py:21
  201.3 23.8 %collective-permute-start.26 = (bf16[2,512,128]{2,1,0:T(8,128)(2,1)S(1)}, bf16[2,512,128]{2,1,0:T(8,128)(2,1)S(1)}, u32[]{:S(2)}, u32[]{:S(2)}) collective-permute-start(bf16[2,512,128]{2,1,0:T(8,128)(2,1)S(1)} %collective-permute-done.25.refs_6_), channel_id=1, source_target_pairs={{0,2},{1,3},{2,0},{3,1},{4,6},{5,7},{6,4},{7,5},{8,10},{9,11},{10,... | collective-permute-start | bytes 786440 | tf_op jit(solution)/shard_map/ppermute | solution.py:21
  207.6 19.3 %collective-permute-start.54 = (bf16[2,512,128]{2,1,0:T(8,128)(2,1)S(1)}, bf16[2,512,128]{2,1,0:T(8,128)(2,1)S(1)}, u32[]{:S(2)}, u32[]{:S(2)}) collective-permute-start(bf16[2,512,128]{2,1,0:T(8,128)(2,1)S(1)} %collective-permute-done.53.refs_0_), channel_id=1, source_target_pairs={{0,2},{1,3},{2,0},{3,1},{4,6},{5,7},{6,4},{7,5},{8,10},{9,11},{10,... | collective-permute-start | bytes 786440 | tf_op jit(solution)/shard_map/ppermute | solution.py:21
  208.6 37.4 %collective-permute-start.55 = (bf16[2,512,128]{2,1,0:T(8,128)(2,1)S(1)}, bf16[2,512,128]{2,1,0:T(8,128)(2,1)S(1)}, u32[]{:S(2)}, u32[]{:S(2)}) collective-permute-start(bf16[2,512,128]{2,1,0:T(8,128)(2,1)S(1)} %collective-permute-done.53.refs_0_), channel_id=1, source_target_pairs={{0,4},{1,5},{2,6},{3,7},{4,0},{5,1},{6,2},{7,3},{8,12},{9,13},{10,... | collective-permute-start | bytes 786440 | tf_op jit(solution)/shard_map/ppermute | solution.py:21
  217.0 29.9 %collective-permute-start.56 = (bf16[2,512,128]{2,1,0:T(8,128)(2,1)S(1)}, bf16[2,512,128]{2,1,0:T(8,128)(2,1)S(1)}, u32[]{:S(2)}, u32[]{:S(2)}) collective-permute-start(bf16[2,512,128]{2,1,0:T(8,128)(2,1)S(1)} %collective-permute-done.53.refs_0_), channel_id=1, source_target_pairs={{0,6},{1,7},{2,4},{3,5},{4,2},{5,3},{6,0},{7,1},{8,14},{9,15},{10,... | collective-permute-start | bytes 786440 | tf_op jit(solution)/shard_map/ppermute | solution.py:21
  224.1 33.4 %collective-permute-start.49 = (bf16[2,512,128]{2,1,0:T(8,128)(2,1)}, bf16[2,512,128]{2,1,0:T(8,128)(2,1)S(1)}, u32[]{:S(2)}, u32[]{:S(2)}) collective-permute-start(bf16[2,512,128]{2,1,0:T(8,128)(2,1)} %get-tuple-element.48), channel_id=1, source_target_pairs={{0,2},{1,3},{2,0},{3,1},{4,6},{5,7},{6,4},{7,5},{8,10},{9,11},{10,... | collective-permute-start | bytes 786440 | tf_op jit(solution)/shard_map/ppermute | solution.py:21
  225.8 32.6 %collective-permute-start.48 = (bf16[2,512,128]{2,1,0:T(8,128)(2,1)}, bf16[2,512,128]{2,1,0:T(8,128)(2,1)S(1)}, u32[]{:S(2)}, u32[]{:S(2)}) collective-permute-start(bf16[2,512,128]{2,1,0:T(8,128)(2,1)} %get-tuple-element.47), channel_id=1, source_target_pairs={{0,4},{1,5},{2,6},{3,7},{4,0},{5,1},{6,2},{7,3},{8,12},{9,13},{10,... | collective-permute-start | bytes 786440 | tf_op jit(solution)/shard_map/ppermute | solution.py:21
  226.9 33.0 %collective-permute-start.47 = (bf16[2,512,128]{2,1,0:T(8,128)(2,1)}, bf16[2,512,128]{2,1,0:T(8,128)(2,1)S(1)}, u32[]{:S(2)}, u32[]{:S(2)}) collective-permute-start(bf16[2,512,128]{2,1,0:T(8,128)(2,1)} %get-tuple-element.46), channel_id=1, source_target_pairs={{0,6},{1,7},{2,4},{3,5},{4,2},{5,3},{6,0},{7,1},{8,14},{9,15},{10,... | collective-permute-start | bytes 786440 | tf_op jit(solution)/shard_map/ppermute | solution.py:21
  246.0 26.9 %collective-permute-start.41 = (bf16[2,2,512,128]{3,2,1,0:T(8,128)(2,1)}, bf16[2,2,512,128]{3,2,1,0:T(8,128)(2,1)S(1)}, u32[]{:S(2)}, u32[]{:S(2)}) collective-permute-start(bf16[2,2,512,128]{3,2,1,0:T(8,128)(2,1)} %get-tuple-element.44), channel_id=1, source_target_pairs={{0,2},{1,3},{2,0},{3,1},{4,6},{5,7},{6,4},{7,5},{8,10},{9,11},{10,... | collective-permute-start | bytes 1572872 | tf_op jit(solution)/shard_map/ppermute | solution.py:21
  256.3 6.6 %collective-permute-start.59 = (bf16[2,512,128]{2,1,0:T(8,128)(2,1)}, bf16[2,512,128]{2,1,0:T(8,128)(2,1)S(1)}, u32[]{:S(2)}, u32[]{:S(2)}) collective-permute-start(bf16[2,512,128]{2,1,0:T(8,128)(2,1)} %get-tuple-element.54), channel_id=1, source_target_pairs={{0,2},{1,3},{2,0},{3,1},{4,6},{5,7},{6,4},{7,5},{8,10},{9,11},{10,... | collective-permute-start | bytes 786440 | tf_op jit(solution)/shard_map/ppermute | solution.py:21
  257.5 9.9 %collective-permute-start.58 = (bf16[2,512,128]{2,1,0:T(8,128)(2,1)}, bf16[2,512,128]{2,1,0:T(8,128)(2,1)S(1)}, u32[]{:S(2)}, u32[]{:S(2)}) collective-permute-start(bf16[2,512,128]{2,1,0:T(8,128)(2,1)} %get-tuple-element.53), channel_id=1, source_target_pairs={{0,4},{1,5},{2,6},{3,7},{4,0},{5,1},{6,2},{7,3},{8,12},{9,13},{10,... | collective-permute-start | bytes 786440 | tf_op jit(solution)/shard_map/ppermute | solution.py:21
  258.4 8.9 %collective-permute-start.57 = (bf16[2,512,128]{2,1,0:T(8,128)(2,1)}, bf16[2,512,128]{2,1,0:T(8,128)(2,1)S(1)}, u32[]{:S(2)}, u32[]{:S(2)}) collective-permute-start(bf16[2,512,128]{2,1,0:T(8,128)(2,1)} %get-tuple-element.52), channel_id=1, source_target_pairs={{0,6},{1,7},{2,4},{3,5},{4,2},{5,3},{6,0},{7,1},{8,14},{9,15},{10,... | collective-permute-start | bytes 786440 | tf_op jit(solution)/shard_map/ppermute | solution.py:21
  259.9 15.4 %collective-permute-start.51 = (bf16[2,2,512,128]{3,2,1,0:T(8,128)(2,1)}, bf16[2,2,512,128]{3,2,1,0:T(8,128)(2,1)S(1)}, u32[]{:S(2)}, u32[]{:S(2)}) collective-permute-start(bf16[2,2,512,128]{3,2,1,0:T(8,128)(2,1)} %get-tuple-element.50), channel_id=1, source_target_pairs={{0,4},{1,5},{2,6},{3,7},{4,0},{5,1},{6,2},{7,3},{8,12},{9,13},{10,... | collective-permute-start | bytes 1572872 | tf_op jit(solution)/shard_map/ppermute | solution.py:21
  263.0 14.1 %collective-permute-start.50 = (bf16[2,512,128]{2,1,0:T(8,128)(2,1)S(1)}, bf16[2,512,128]{2,1,0:T(8,128)(2,1)S(1)}, u32[]{:S(2)}, u32[]{:S(2)}) collective-permute-start(bf16[2,512,128]{2,1,0:T(8,128)(2,1)S(1)} %add_convert_fusion.1), channel_id=1, source_target_pairs={{0,16},{8,24},{16,0},{24,8},{1,17},{9,25},{17,1},{25,9},{2,18},{10... | collective-permute-start | bytes 786440 | tf_op jit(solution)/shard_map/ppermute | solution.py:21
  268.5 12.2 %collective-permute-start.60 = (bf16[2,512,128]{2,1,0:T(8,128)(2,1)S(1)}, bf16[2,512,128]{2,1,0:T(8,128)(2,1)S(1)}, u32[]{:S(2)}, u32[]{:S(2)}) collective-permute-start(bf16[2,512,128]{2,1,0:T(8,128)(2,1)S(1)} %add_convert_fusion), channel_id=1, source_target_pairs={{0,16},{8,24},{16,0},{24,8},{1,17},{9,25},{17,1},{25,9},{2,18},{10... | collective-permute-start | bytes 786440 | tf_op jit(solution)/shard_map/ppermute | solution.py:21
  273.1 6.5 %collective-permute-start.42 = (bf16[1,2,512,128]{3,2,1,0:T(8,128)(2,1)S(1)}, bf16[1,2,512,128]{3,2,1,0:T(8,128)(2,1)}, u32[]{:S(2)}, u32[]{:S(2)}) collective-permute-start(bf16[1,2,512,128]{3,2,1,0:T(8,128)(2,1)S(1)} %slice.39), channel_id=1, source_target_pairs={{0,4},{1,5},{2,6},{3,7},{4,0},{5,1},{6,2},{7,3},{8,12},{9,13},{10,... | collective-permute-start | bytes 786440 | tf_op jit(solution)/shard_map/ppermute | solution.py:21
  276.2 6.7 %collective-permute-start.52 = (bf16[1,2,512,128]{3,2,1,0:T(8,128)(2,1)}, bf16[1,2,512,128]{3,2,1,0:T(8,128)(2,1)}, u32[]{:S(2)}, u32[]{:S(2)}) collective-permute-start(bf16[1,2,512,128]{3,2,1,0:T(8,128)(2,1)} %slice.38), channel_id=1, source_target_pairs={{0,2},{1,3},{2,0},{3,1},{4,6},{5,7},{6,4},{7,5},{8,10},{9,11},{10,... | collective-permute-start | bytes 786440 | tf_op jit(solution)/shard_map/ppermute | solution.py:21
  283.9 1.6 collective-permute-start.61
  (39 other events, 417.3 us)

commit v2 on v1

--- a/solution.py
+++ b/solution.py
@@ -157,36 +157,68 @@
     )(where, *prob_parts, *behaviors)
 
 
-def pack_weights(where, arrays, axis, row=None, lanes=0):
-    units = arrays[0].shape[axis] // 2
-    depth = arrays[0].shape[1 - axis]
-    count = len(arrays)
-
-    def body(where_ref, *refs):
-        for which in range(2):
-            start = pl.multiple_of((where_ref[3] ^ which) * units, units)
-            for i in range(count):
-                if axis == 1:
-                    value = refs[i][:, pl.ds(start, units)]
-                    refs[count + which][i * units : (i + 1) * units, :] = value.T
-                else:
-                    refs[extra + which][...] = refs[i][pl.ds(start, units), :].T
-        if row is not None:
-            refs[-1][...] = jnp.broadcast_to(refs[count][...], (lanes, row.shape[1])).T
-
-    shape = (count * units, depth) if axis == 1 else (depth, units)
-    out_shape = [jax.ShapeDtypeStruct(shape, jnp.bfloat16)] * 2
-    if row is not None:
-        arrays = (*arrays, row)
-        out_shape += [jax.ShapeDtypeStruct((row.shape[1], lanes), row.dtype)]
-    extra = len(arrays)
+def tile_of(units):
+    return min(256, units)
+
+
+def pack_expand(gate, up, far_layer):
+    depth, units = gate.shape[0], gate.shape[1] // 2
+    tile = tile_of(units)
+    tiles = units // tile
+
+    def body(gate_ref, up_ref, own_ref, other_ref, gates, ups, outs, sems):
+        side = lax.axis_index("dp") // far_layer
+        loads = []
+        for k, which in enumerate((1, 0)):
+            at = pl.ds(pl.multiple_of((side ^ which) * units, units), units)
+            for i, (ref, buffer) in enumerate(((gate_ref, gates), (up_ref, ups))):
+                loads.append(pltpu.make_async_copy(ref.at[:, at], buffer.at[k], sems.at[k, i]))
+                loads[-1].start()
+        stores = []
+        for k, target in enumerate((other_ref, own_ref)):
+            for i, buffer in enumerate((gates, ups)):
+                loads[2 * k + i].wait()
+                for f in range(tiles):
+                    outs[k, (2 * f + i) * tile : (2 * f + i + 1) * tile, :] = buffer[
+                        k, :, f * tile : (f + 1) * tile
+                    ].T
+            stores.append(pltpu.make_async_copy(outs.at[k], target, sems.at[k, 2]))
+            stores[-1].start()
+        for store in stores:
+            store.wait()
+
     return pl.pallas_call(
         body,
-        in_specs=[SMEM_WHOLE] + [VMEM_WHOLE] * extra,
-        out_specs=[VMEM_WHOLE] * len(out_shape),
-        out_shape=out_shape,
-        name="pack",
-    )(where, *arrays)
+        in_specs=[IN_PLACE] * 2,
+        out_specs=[IN_PLACE] * 2,
+        out_shape=[jax.ShapeDtypeStruct((2 * units, depth), gate.dtype)] * 2,
+        scratch_shapes=[
+            pltpu.VMEM((2, depth, units), gate.dtype),
+            pltpu.VMEM((2, depth, units), gate.dtype),
+            pltpu.VMEM((2, 2 * units, depth), gate.dtype),
+            pltpu.SemaphoreType.DMA((2, 3)),
+        ],
+        name="pack_expand",
+    )(gate, up)
+
+
+def pack_down(where, down, row, lanes):
+    units, width = down.shape[0] // 2, down.shape[1]
+
+    def body(where_ref, down_ref, row_ref, own_ref, other_ref, column_ref):
+        for which, ref in enumerate((own_ref, other_ref)):
+            start = pl.multiple_of((where_ref[3] ^ which) * units, units)
+            ref[...] = down_ref[pl.ds(start, units), :].T
+        column_ref[...] = jnp.broadcast_to(row_ref[...], (lanes, row.shape[1])).T
+
+    return pl.pallas_call(
+        body,
+        in_specs=[SMEM_WHOLE] + [VMEM_WHOLE] * 2,
+        out_specs=[VMEM_WHOLE] * 3,
+        out_shape=[jax.ShapeDtypeStruct((width, units), down.dtype)] * 2
+        + [jax.ShapeDtypeStruct((row.shape[1], lanes), row.dtype)],
+        name="pack_down",
+    )(where, down, row)
 
 
 def start_loads(sems, base, pairs):
@@ -244,12 +276,11 @@
             (gain_ref,) = take(1)
             expand_refs = take(2 * layers)
         else:
-            (hidden_ref,) = take(1)
+            (given_ref,) = take(1)
         if downs:
             down_refs = take(2 * layers)
             out_refs = take(outs * count)
-            if expands:
-                (hidden_ref,) = take(1)
+            (hidden_ref,) = take(1)
         else:
             (hidden_ref,) = take(1)
         (sems,) = take(1)
@@ -273,6 +304,8 @@
                     for s in range(layers)
                 ],
             )
+        else:
+            given_loads = start_loads(sems, 0, [(given_ref, hidden_ref)])
         if downs:
             (narrow,) = take(1)
             down_loads = start_loads(
@@ -288,20 +321,20 @@
             for copy in part_loads:
                 copy.wait()
             normalize(raw, normed, gain_ref)
-            tile = min(256, units)
+            tile = tile_of(units)
             for i in range(2):
                 for s in range(layers):
                     expand_loads[i * layers + s].wait()
                 for f in range(0, units, tile):
-                    gate = dot(wide[i, f : f + tile, :], normed[...], ((1,), (0,)))
+                    gate = dot(wide[i, 2 * f : 2 * f + tile, :], normed[...], ((1,), (0,)))
                     upward = dot(
-                        wide[i, units + f : units + f + tile, :], normed[...], ((1,), (0,))
+                        wide[i, 2 * f + tile : 2 * (f + tile), :], normed[...], ((1,), (0,))
                     )
                     hidden_ref[i * units + f : i * units + f + tile, :] = (
                         gate / (1.0 + jnp.exp(-gate)) * upward
                     ).astype(jnp.bfloat16)
         if downs:
-            for copy in down_loads:
+            for copy in down_loads if expands else given_loads + down_loads:
                 copy.wait()
             for g in range(count):
                 for i in range(chips):
@@ -331,7 +364,7 @@
         ]
     else:
         inputs += [hidden]
-        in_specs += [VMEM_WHOLE]
+        in_specs += [IN_PLACE]
     scratch = [pltpu.SemaphoreType.DMA((count * chips + 4 * layers,))] + scratch
     if downs:
         inputs += down[0] + down[1]
@@ -341,8 +374,7 @@
             shape = (chips // 2,) + shape
         out_shape = [jax.ShapeDtypeStruct(shape, jnp.bfloat16)] * (outs * count)
         scratch += [pltpu.VMEM((features, 2 * units), jnp.bfloat16)]
-        if expands:
-            scratch = [pltpu.VMEM(hidden_shape, jnp.bfloat16)] + scratch
+        scratch = [pltpu.VMEM(hidden_shape, jnp.bfloat16)] + scratch
     else:
         out_shape = [jax.ShapeDtypeStruct(hidden_shape, jnp.bfloat16)]
     return pl.pallas_call(
@@ -384,13 +416,16 @@
         return blocks
 
     def halved(near, far, order):
+        wide = lambda x: x.astype(jnp.float32)
+        near = [wide(near[i]) for i in range(chips // 2)]
         for bit in order:
             got = across(far, bit)
-            total = near.astype(jnp.float32) + got.astype(jnp.float32)
-            count = total.shape[0] // 2
-            near = total[:count]
-            far = total[count:].astype(jnp.bfloat16)
-        return total[0]
+            near = [block + wide(got[j]) for j, block in enumerate(near)]
+            count = len(near) // 2
+            if count:
+                far = jnp.stack(near[count:]).astype(jnp.bfloat16)
+                near = near[:count]
+        return near[0]
 
     def shards(behaviors, candidates, lengths, bilinear, norm_gain, w_gate, w_up, w_down):
         users, width, cands = candidates.shape
@@ -429,8 +464,8 @@
                 for s in range(dp_count)
             ]
 
-        expand_got = spread(*pack_weights(where, (w_gate, w_up), 1))
-        *down_packs, gain = pack_weights(where, (w_down,), 0, norm_gain[None, :], cands)
+        expand_got = spread(*pack_expand(w_gate, w_up, far_layer))
+        *down_packs, gain = pack_down(where, w_down, norm_gain[None, :], cands)
         down_got = spread(*down_packs)
         parts, pooled = [], []
         for g in range(2):

time: 287 us -> 284 us (0.990)
  transfers between devices with their start and end apart: 62 -> 62, of which waited for: 23 -> 21; matrix products, arithmetic and copies ran while one was open for 2% -> 2% of each run, Pallas kernels for 24% -> 24%
where the time goes in v2:
time: 284 us
  waiting for transfers between devices  140 us (49%)
  Pallas kernels  67.3 us (24%)
  starting transfers between devices  67 us (24%)
  other arithmetic  5.65 us (2%)
  local copies, waits for them, and re-layouts  3.92 us (1%)
    ppermute x62, waiting for transfers between devices, swap(): return lax.ppermute(x, axis_name, [(i, i ^ offset) for i in range(count)])  140 us
    ppermute x62, starting transfers between devices, swap(): return lax.ppermute(x, axis_name, [(i, i ^ offset) for i in range(count)])  67 us
    pallas_call x5, Pallas kernels, feed_forward(): pl.pallas_call(body, in_specs=in_specs, out_specs=[VMEM_WHOLE] * len(out_...  38.6 us
    pallas_call x2, Pallas kernels, score_parts(): pl.pallas_call(body, grid_spec=pltpu.PrefetchScalarGridSpec(num_scalar_pr...  11.2 us
    pallas_call x2, Pallas kernels, pool(): pl.pallas_call(body, grid_spec=pltpu.PrefetchScalarGridSpec(num_scalar_pr...  7.46 us
  transfers between devices with their start and end apart: 62, of which 21 were waited for; matrix products, arithmetic and copies ran while one was open for 2% of the time, Pallas kernels for 24%

profile of v2, /device:TPU:0, one launch (start us, length us, event | category | flops | bytes accessed | tf_op | source)
XLA Modules:
  0.0 284.0 jit_solution(6870008716936821442)
XLA Ops:
  1.1 2.9 %pack_down.1 = (bf16[512,512]{1,0:T(8,128)(2,1)}, bf16[512,512]{1,0:T(8,128)(2,1)}, f32[2048,128]{1,0:T(8,128)}) custom-call(s32[4]{0:T(128)} %pad_add_fusion.where_ref, bf16[1024,512]{1,0:T(8,128)(2,1)} %down_ref.1, f32[1,2048]{1,0:T(1,128)} %bitcast.13), custom_call_target="tpu_custom_call" | custom-call | tf_op jit(solution)/shard_map/pack_down/pallas_call | solution.py:214
  4.0 4.1 %collective-permute-start.35 = (bf16[512,512]{1,0:T(8,128)(2,1)}, bf16[512,512]{1,0:T(8,128)(2,1)S(1)}, u32[]{:S(2)}, u32[]{:S(2)}) collective-permute-start(bf16[512,512]{1,0:T(8,128)(2,1)} %get-tuple-element.42), channel_id=1, source_target_pairs={{0,16},{8,24},{16,0},{24,8},{1,17},{9,25},{17,1},{25,9},{2,18},{10... | collective-permute-start | bytes 1572872 | tf_op jit(solution)/shard_map/ppermute | solution.py:21
  8.1 1.6 collective-permute-start.34
  10.7 1.6 collective-permute-start.15
  12.3 19.4 %collective-permute-done.35.refs_3_.refs_15_ = bf16[512,512]{1,0:T(8,128)(2,1)S(1)} collective-permute-done((bf16[512,512]{1,0:T(8,128)(2,1)}, bf16[512,512]{1,0:T(8,128)(2,1)S(1)}, u32[]{:S(2)}, u32[]{:S(2)}) %collective-permute-start.35) | collective-permute-done | bytes 524320 | tf_op jit(solution)/shard_map/ppermute | solution.py:21
  31.7 1.6 collective-permute-start.16
  33.3 3.0 %pack_expand.1 = (bf16[1024,512]{1,0:T(8,128)(2,1)}, bf16[1024,512]{1,0:T(8,128)(2,1)}) custom-call(bf16[512,1024]{1,0:T(8,128)(2,1)} %gate_ref.1, bf16[512,1024]{1,0:T(8,128)(2,1)} %up_ref.1), custom_call_target="tpu_custom_call" | custom-call | tf_op jit(solution)/shard_map/pack_expand/pallas_call | solution.py:190
  36.5 2.4 collective-permute-start.17
  39.3 1.3 collective-permute-start.1
  40.6 6.1 %collective-permute-done.17.refs_3_ = bf16[2,512,128]{2,1,0:T(8,128)(2,1)} collective-permute-done((bf16[2,512,128]{2,1,0:T(8,128)(2,1)S(1)}, bf16[2,512,128]{2,1,0:T(8,128)(2,1)}, u32[]{:S(2)}, u32[]{:S(2)}) %collective-permute-start.17) | collective-permute-done | bytes 262176 | tf_op jit(solution)/shard_map/ppermute | solution.py:21
  46.7 1.4 collective-permute-start.2
  48.1 3.1 %collective-permute-done.1.refs_1_ = bf16[2,512,128]{2,1,0:T(8,128)(2,1)S(1)} collective-permute-done((bf16[2,512,128]{2,1,0:T(8,128)(2,1)S(1)}, bf16[2,512,128]{2,1,0:T(8,128)(2,1)S(1)}, u32[]{:S(2)}, u32[]{:S(2)}) %collective-permute-start.1) | collective-permute-done | bytes 262176 | tf_op jit(solution)/shard_map/ppermute | solution.py:21
  51.9 2.9 %collective-permute-start.27 = (bf16[1024,512]{1,0:T(8,128)(2,1)}, bf16[1024,512]{1,0:T(8,128)(2,1)S(1)}, u32[]{:S(2)}, u32[]{:S(2)}) collective-permute-start(bf16[1024,512]{1,0:T(8,128)(2,1)} %get-tuple-element.39.refs_9_.refs_5_), channel_id=1, source_target_pairs={{0,8},{8,0},{16,24},{24,16},{1,9},{9,1},{17,25},{25,17},{2,10},{10... | collective-permute-start | bytes 3145736 | tf_op jit(solution)/shard_map/ppermute | solution.py:21
  54.9 2.4 collective-permute-start.3
  57.3 5.6 %collective-permute-done.3.refs_3_ = bf16[2,512,128]{2,1,0:T(8,128)(2,1)} collective-permute-done((bf16[2,512,128]{2,1,0:T(8,128)(2,1)S(1)}, bf16[2,512,128]{2,1,0:T(8,128)(2,1)}, u32[]{:S(2)}, u32[]{:S(2)}) %collective-permute-start.3) | collective-permute-done | bytes 262176 | tf_op jit(solution)/shard_map/ppermute | solution.py:21
  63.0 1.4 collective-permute-start.36
  64.4 21.1 %collective-permute-done.28.refs_11_.refs_7_ = bf16[1024,512]{1,0:T(8,128)(2,1)S(1)} collective-permute-done((bf16[1024,512]{1,0:T(8,128)(2,1)}, bf16[1024,512]{1,0:T(8,128)(2,1)S(1)}, u32[]{:S(2)}, u32[]{:S(2)}) %collective-permute-start.28) | collective-permute-done | bytes 1048608 | tf_op jit(solution)/shard_map/ppermute | solution.py:21
  85.5 15.2 %collective-permute-done.27.refs_10_.refs_6_ = bf16[1024,512]{1,0:T(8,128)(2,1)S(1)} collective-permute-done((bf16[1024,512]{1,0:T(8,128)(2,1)}, bf16[1024,512]{1,0:T(8,128)(2,1)S(1)}, u32[]{:S(2)}, u32[]{:S(2)}) %collective-permute-start.27) | collective-permute-done | bytes 1048608 | tf_op jit(solution)/shard_map/ppermute | solution.py:21
  100.7 11.3 %collective-permute-done.36.refs_4_.refs_16_ = bf16[512,512]{1,0:T(8,128)(2,1)} collective-permute-done((bf16[512,512]{1,0:T(8,128)(2,1)}, bf16[512,512]{1,0:T(8,128)(2,1)}, u32[]{:S(2)}, u32[]{:S(2)}) %collective-permute-start.36) | collective-permute-done | bytes 524320 | tf_op jit(solution)/shard_map/ppermute | solution.py:21
  112.6 5.6 %scores.3 = (f32[64,1024]{1,0:T(8,128)}, f32[64,1024]{1,0:T(8,128)}, f32[64,1024]{1,0:T(8,128)}, f32[64,1024]{1,0:T(8,128)}) custom-call(s32[4]{0:T(128)} %pad_add_fusion.where_ref, bf16[2,512,128]{2,1,0:T(8,128)(2,1)} %copy-done.8, bf16[2,512,128]{2,1,0:T(8,128)(2,1)} %copy-done.17, bf16[2,512,128]{2,1,0:T(8,128)(2,1)} %copy-done.19, ...), custom_call_target="tpu_custom_call" | custom-call | tf_op jit(solution)/shard_map/scores/pallas_call | solution.py:75
  118.2 2.5 collective-permute-start.18
  121.8 5.6 %scores.2 = (f32[64,1024]{1,0:T(8,128)}, f32[64,1024]{1,0:T(8,128)}, f32[64,1024]{1,0:T(8,128)}, f32[64,1024]{1,0:T(8,128)}) custom-call(s32[4]{0:T(128)} %pad_add_fusion.where_ref, bf16[2,512,128]{2,1,0:T(8,128)(2,1)} %copy-done.9, bf16[2,512,128]{2,1,0:T(8,128)(2,1)} %copy-done.18, bf16[2,512,128]{2,1,0:T(8,128)(2,1)} %copy-done.20, ...), custom_call_target="tpu_custom_call" | custom-call | tf_op jit(solution)/shard_map/scores/pallas_call | solution.py:75
  127.5 5.5 %collective-permute-done.29.refs_12_.refs_8_ = bf16[1024,512]{1,0:T(8,128)(2,1)} collective-permute-done((bf16[1024,512]{1,0:T(8,128)(2,1)S(1)}, bf16[1024,512]{1,0:T(8,128)(2,1)}, u32[]{:S(2)}, u32[]{:S(2)}) %collective-permute-start.29) | collective-permute-done | bytes 1048608 | tf_op jit(solution)/shard_map/ppermute | solution.py:21
  133.0 2.4 collective-permute-start.6
  136.5 4.6 %collective-permute-done.6.refs_1_ = f32[64,1024]{1,0:T(8,128)} collective-permute-done((f32[64,1024]{1,0:T(8,128)}, f32[64,1024]{1,0:T(8,128)}, u32[]{:S(2)}, u32[]{:S(2)}) %collective-permute-start.6) | collective-permute-done | bytes 262176 | tf_op jit(solution)/shard_map/ppermute | solution.py:21
  141.1 1.5 collective-permute-start.8
  142.6 2.1 softmax.3.refs_0_
  144.7 1.9 collective-permute-done.7.refs_2_
  146.6 1.5 collective-permute-start.21
  148.1 1.5 collective-permute-start.22
  149.7 2.6 collective-permute-done.21.refs_1_
  152.3 2.4 collective-permute-start.23
  154.7 2.1 softmax.2.refs_0_
  158.5 2.5 collective-permute-start.11
  161.0 2.0 collective-permute-done.10.refs_2_
  164.1 3.8 %pool.3.refs_4_ = bf16[2,512,128]{2,1,0:T(8,128)(2,1)} custom-call(s32[4]{0:T(128)} %pad_add_fusion.where_ref, bf16[64,1024]{1,0:T(8,128)(2,1)} %softmax.3.refs_0_, bf16[64,1024]{1,0:T(8,128)(2,1)} %copy-done.29, bf16[64,1024]{1,0:T(8,128)(2,1)} %copy-done.30, bf16[64,1024]{1,0:T(8,128)(2,1)} %collective-permute-done.23.refs_3_, ...), custom_call_target="tpu_custom_call" | custom-call | tf_op jit(solution)/shard_map/pool/pallas_call | solution.py:145
  167.9 1.2 collective-permute-start.25
  170.0 3.6 %pool.2.refs_0_ = bf16[2,512,128]{2,1,0:T(8,128)(2,1)} custom-call(s32[4]{0:T(128)} %pad_add_fusion.where_ref, bf16[64,1024]{1,0:T(8,128)(2,1)} %softmax.2.refs_0_, bf16[64,1024]{1,0:T(8,128)(2,1)} %collective-permute-done.9.refs_1_, bf16[64,1024]{1,0:T(8,128)(2,1)} %copy-done.31, bf16[64,1024]{1,0:T(8,128)(2,1)} %collective-permute-done.11.refs_3_, ...), custom_call_target="tpu_custom_call" | custom-call | tf_op jit(solution)/shard_map/pool/pallas_call | solution.py:145
  173.6 1.2 collective-permute-start.12
  175.8 2.8 %collective-permute-start.43 = (bf16[2,512,128]{2,1,0:T(8,128)(2,1)}, bf16[2,512,128]{2,1,0:T(8,128)(2,1)S(1)}, u32[]{:S(2)}, u32[]{:S(2)}) collective-permute-start(bf16[2,512,128]{2,1,0:T(8,128)(2,1)} %pool.2.refs_0_), channel_id=1, source_target_pairs={{0,16},{8,24},{16,0},{24,8},{1,17},{9,25},{17,1},{25,9},{2,18},{10... | collective-permute-start | bytes 786440 | tf_op jit(solution)/shard_map/ppermute | solution.py:21
  179.6 4.4 %collective-permute-done.12.refs_1_ = bf16[2,512,128]{2,1,0:T(8,128)(2,1)S(1)} collective-permute-done((bf16[2,512,128]{2,1,0:T(8,128)(2,1)}, bf16[2,512,128]{2,1,0:T(8,128)(2,1)S(1)}, u32[]{:S(2)}, u32[]{:S(2)}) %collective-permute-start.12) | collective-permute-done | bytes 262176 | tf_op jit(solution)/shard_map/ppermute | solution.py:21
  184.3 7.7 %collective-permute-done.53.refs_0_ = bf16[2,512,128]{2,1,0:T(8,128)(2,1)S(1)} collective-permute-done((bf16[2,512,128]{2,1,0:T(8,128)(2,1)S(1)}, bf16[2,512,128]{2,1,0:T(8,128)(2,1)S(1)}, u32[]{:S(2)}, u32[]{:S(2)}) %collective-permute-start.53) | collective-permute-done | bytes 262176 | tf_op jit(solution)/shard_map/ppermute | solution.py:21
  192.0 1.7 collective-permute-start.54
  194.1 3.4 %collective-permute-done.43.refs_0_ = bf16[2,512,128]{2,1,0:T(8,128)(2,1)S(1)} collective-permute-done((bf16[2,512,128]{2,1,0:T(8,128)(2,1)}, bf16[2,512,128]{2,1,0:T(8,128)(2,1)S(1)}, u32[]{:S(2)}, u32[]{:S(2)}) %collective-permute-start.43) | collective-permute-done | bytes 262176 | tf_op jit(solution)/shard_map/ppermute | solution.py:21
  197.5 1.3 collective-permute-start.56
  200.2 1.6 collective-permute-start.45
  201.8 10.7 %feed_forward.5.refs_0_ = bf16[1024,512]{1,0:T(8,128)(2,1)} custom-call(s32[4]{0:T(128)} %pad_add_fusion.where_ref, bf16[2,512,128]{2,1,0:T(8,128)(2,1)} %pool.2.refs_0_, bf16[2,512,128]{2,1,0:T(8,128)(2,1)} %copy-done.24, bf16[2,512,128]{2,1,0:T(8,128)(2,1)} %copy-done.25, bf16[2,512,128]{2,1,0:T(8,128)(2,1)} %copy-done.27, ...), custom_call_target="tpu_custom_call" | custom-call | tf_op jit(solution)/shard_map/feed_forward/pallas_call | solution.py:380
  212.5 6.5 %feed_forward.6 = (bf16[2,2,512,128]{3,2,1,0:T(8,128)(2,1)}, bf16[2,2,512,128]{3,2,1,0:T(8,128)(2,1)}, bf16[2,2,512,128]{3,2,1,0:T(8,128)(2,1)}, bf16[2,2,512,128]{3,2,1,0:T(8,128)(2,1)}) custom-call(s32[4]{0:T(128)} %pad_add_fusion.where_ref, bf16[1024,512]{1,0:T(8,128)(2,1)} %feed_forward.5.refs_0_, bf16[512,512]{1,0:T(8,128)(2,1)} %get-tuple-element.41.refs_1_.refs_13_, ...), custom_call_target="tpu_custom_call" | custom-call | tf_op jit(solution)/shard_map/feed_forward/pallas_call | solution.py:380
  219.6 1.6 collective-permute-start.46
  221.9 8.6 %feed_forward.9 = (bf16[2,512,128]{2,1,0:T(8,128)(2,1)}, bf16[2,512,128]{2,1,0:T(8,128)(2,1)}, bf16[2,512,128]{2,1,0:T(8,128)(2,1)}, bf16[2,512,128]{2,1,0:T(8,128)(2,1)}) custom-call(s32[4]{0:T(128)} %pad_add_fusion.where_ref, bf16[2,512,128]{2,1,0:T(8,128)(2,1)} %copy-done.12, bf16[2,512,128]{2,1,0:T(8,128)(2,1)} %copy-done.13, ...), custom_call_target="tpu_custom_call" | custom-call | tf_op jit(solution)/shard_map/feed_forward/pallas_call | solution.py:380
  230.5 1.4 collective-permute-start.57
  232.0 1.6 collective-permute-start.58
  234.8 1.5 collective-permute-start.41
  236.3 7.3 %feed_forward.7.refs_0_ = bf16[1024,256]{1,0:T(8,128)(2,1)} custom-call(s32[4]{0:T(128)} %pad_add_fusion.where_ref, bf16[2,512,128]{2,1,0:T(8,128)(2,1)} %copy-done.16, bf16[2,512,128]{2,1,0:T(8,128)(2,1)} %copy-done.21, bf16[2,512,128]{2,1,0:T(8,128)(2,1)} %copy-done.23, bf16[2,512,128]{2,1,0:T(8,128)(2,1)} %copy-done.26, ...), custom_call_target="tpu_custom_call" | custom-call | tf_op jit(solution)/shard_map/feed_forward/pallas_call | solution.py:380
  243.6 5.4 %feed_forward.8 = (bf16[2,512,128]{2,1,0:T(8,128)(2,1)}, bf16[2,512,128]{2,1,0:T(8,128)(2,1)}, bf16[2,512,128]{2,1,0:T(8,128)(2,1)}, bf16[2,512,128]{2,1,0:T(8,128)(2,1)}) custom-call(s32[4]{0:T(128)} %pad_add_fusion.where_ref, bf16[1024,256]{1,0:T(8,128)(2,1)} %feed_forward.7.refs_0_, bf16[512,512]{1,0:T(8,128)(2,1)} %get-tuple-element.41.refs_1_.refs_13_, ...), custom_call_target="tpu_custom_call" | custom-call | tf_op jit(solution)/shard_map/feed_forward/pallas_call | solution.py:380
  249.1 1.4 collective-permute-start.47
  251.2 1.5 collective-permute-start.49
  252.9 10.4 %collective-permute-done.47 = bf16[2,512,128]{2,1,0:T(8,128)(2,1)S(1)} collective-permute-done((bf16[2,512,128]{2,1,0:T(8,128)(2,1)}, bf16[2,512,128]{2,1,0:T(8,128)(2,1)S(1)}, u32[]{:S(2)}, u32[]{:S(2)}) %collective-permute-start.47) | collective-permute-done | bytes 262176 | tf_op jit(solution)/shard_map/ppermute | solution.py:21
  263.4 1.5 collective-permute-start.52
  264.9 4.0 %collective-permute-done.49 = bf16[2,512,128]{2,1,0:T(8,128)(2,1)S(1)} collective-permute-done((bf16[2,512,128]{2,1,0:T(8,128)(2,1)}, bf16[2,512,128]{2,1,0:T(8,128)(2,1)S(1)}, u32[]{:S(2)}, u32[]{:S(2)}) %collective-permute-start.49) | collective-permute-done | bytes 262176 | tf_op jit(solution)/shard_map/ppermute | solution.py:21
  268.9 1.8 add_convert_fusion.2
  272.3 8.0 %collective-permute-done.50 = bf16[2,512,128]{2,1,0:T(8,128)(2,1)S(1)} collective-permute-done((bf16[2,512,128]{2,1,0:T(8,128)(2,1)}, bf16[2,512,128]{2,1,0:T(8,128)(2,1)S(1)}, u32[]{:S(2)}, u32[]{:S(2)}) %collective-permute-start.50) | collective-permute-done | bytes 262176 | tf_op jit(solution)/shard_map/ppermute | solution.py:21
  280.3 1.1 fusion.1
  281.5 1.5 collective-permute-done.61
  (151 shorter events, 19.8 us)
Async XLA Ops:
  0.0 112.1 %collective-permute-start.5 = (bf16[8,256,1024]{2,1,0:T(8,128)(2,1)}, bf16[8,256,1024]{2,1,0:T(8,128)(2,1)}, u32[]{:S(2)}, u32[]{:S(2)}) collective-permute-start(bf16[8,256,1024]{2,1,0:T(8,128)(2,1)} %refs_4_.7), channel_id=1, source_target_pairs={{0,1},{1,0},{2,3},{3,2},{4,5},{5,4},{6,7},{7,6},{8,9},{9,8},{10,11... | collective-permute-start | bytes 12582920 | tf_op jit(solution)/shard_map/ppermute | solution.py:21
  0.5 10.2 %collective-permute-start = (bf16[8,256,128]{2,1,0:T(8,128)(2,1)}, bf16[8,256,128]{2,1,0:T(8,128)(2,1)S(1)}, u32[]{:S(2)}, u32[]{:S(2)}) collective-permute-start(bf16[8,256,128]{2,1,0:T(8,128)(2,1)} %param.9), channel_id=1, source_target_pairs={{0,1},{1,0},{2,3},{3,2},{4,5},{5,4},{6,7},{7,6},{8,9},{9,8},{10,11... | collective-permute-start | bytes 1572872 | tf_op jit(solution)/shard_map/ppermute | solution.py:21
  4.0 27.7 %collective-permute-start.35 = (bf16[512,512]{1,0:T(8,128)(2,1)}, bf16[512,512]{1,0:T(8,128)(2,1)S(1)}, u32[]{:S(2)}, u32[]{:S(2)}) collective-permute-start(bf16[512,512]{1,0:T(8,128)(2,1)} %get-tuple-element.42), channel_id=1, source_target_pairs={{0,16},{8,24},{16,0},{24,8},{1,17},{9,25},{17,1},{25,9},{2,18},{10... | collective-permute-start | bytes 1572872 | tf_op jit(solution)/shard_map/ppermute | solution.py:21
  8.1 25.2 %collective-permute-start.34 = (bf16[512,512]{1,0:T(8,128)(2,1)}, bf16[512,512]{1,0:T(8,128)(2,1)S(1)}, u32[]{:S(2)}, u32[]{:S(2)}) collective-permute-start(bf16[512,512]{1,0:T(8,128)(2,1)} %get-tuple-element.41.refs_1_.refs_13_), channel_id=1, source_target_pairs={{0,8},{8,0},{16,24},{24,16},{1,9},{9,1},{17,25},{25,17},{2,10},{10... | collective-permute-start | bytes 1572872 | tf_op jit(solution)/shard_map/ppermute | solution.py:21
  9.7 26.7 %collective-permute-start.37 = (bf16[512,512]{1,0:T(8,128)(2,1)}, bf16[512,512]{1,0:T(8,128)(2,1)S(1)}, u32[]{:S(2)}, u32[]{:S(2)}) collective-permute-start(bf16[512,512]{1,0:T(8,128)(2,1)} %get-tuple-element.41.refs_1_.refs_13_), channel_id=1, source_target_pairs={{0,1},{1,0},{2,3},{3,2},{4,5},{5,4},{6,7},{7,6},{8,9},{9,8},{10,11... | collective-permute-start | bytes 1572872 | tf_op jit(solution)/shard_map/ppermute | solution.py:21
  10.7 101.9 %copy-start.8 = (bf16[2,512,128]{2,1,0:T(8,128)(2,1)}, bf16[2,512,128]{2,1,0:T(8,128)(2,1)S(1)}, u32[]{:S(2)}) copy-start(bf16[2,512,128]{2,1,0:T(8,128)(2,1)S(1)} %pad_maximum_fusion.2.refs_0_) | copy-start | bytes 786436
  10.7 25.7 %collective-permute-start.15 = (bf16[2,512,128]{2,1,0:T(8,128)(2,1)S(1)}, bf16[2,512,128]{2,1,0:T(8,128)(2,1)S(1)}, u32[]{:S(2)}, u32[]{:S(2)}) collective-permute-start(bf16[2,512,128]{2,1,0:T(8,128)(2,1)S(1)} %pad_maximum_fusion.2.refs_0_), channel_id=1, source_target_pairs={{0,2},{1,3},{2,0},{3,1},{4,6},{5,7},{6,4},{7,5},{8,10},{9,11},{10,... | collective-permute-start | bytes 786440 | tf_op jit(solution)/shard_map/ppermute | solution.py:21
  31.7 7.6 %collective-permute-start.16 = (bf16[2,512,128]{2,1,0:T(8,128)(2,1)S(1)}, bf16[2,512,128]{2,1,0:T(8,128)(2,1)S(1)}, u32[]{:S(2)}, u32[]{:S(2)}) collective-permute-start(bf16[2,512,128]{2,1,0:T(8,128)(2,1)S(1)} %pad_maximum_fusion.2.refs_0_), channel_id=1, source_target_pairs={{0,4},{1,5},{2,6},{3,7},{4,0},{5,1},{6,2},{7,3},{8,12},{9,13},{10,... | collective-permute-start | bytes 786440 | tf_op jit(solution)/shard_map/ppermute | solution.py:21
  33.3 29.7 %collective-permute-start.4 = (bf16[256,2048]{1,0:T(8,128)(2,1)}, bf16[256,2048]{1,0:T(8,128)(2,1)}, u32[]{:S(2)}, u32[]{:S(2)}) collective-permute-start(bf16[256,2048]{1,0:T(8,128)(2,1)} %refs_4_.6), channel_id=1, source_target_pairs={{0,1},{1,0},{2,3},{3,2},{4,5},{5,4},{6,7},{7,6},{8,9},{9,8},{10,11... | collective-permute-start | bytes 3145736 | tf_op jit(solution)/shard_map/ppermute | solution.py:21
  36.4 49.1 %collective-permute-start.28 = (bf16[1024,512]{1,0:T(8,128)(2,1)}, bf16[1024,512]{1,0:T(8,128)(2,1)S(1)}, u32[]{:S(2)}, u32[]{:S(2)}) collective-permute-start(bf16[1024,512]{1,0:T(8,128)(2,1)} %get-tuple-element.40), channel_id=1, source_target_pairs={{0,16},{8,24},{16,0},{24,8},{1,17},{9,25},{17,1},{25,9},{2,18},{10... | collective-permute-start | bytes 3145736 | tf_op jit(solution)/shard_map/ppermute | solution.py:21
  36.5 10.2 %collective-permute-start.17 = (bf16[2,512,128]{2,1,0:T(8,128)(2,1)S(1)}, bf16[2,512,128]{2,1,0:T(8,128)(2,1)}, u32[]{:S(2)}, u32[]{:S(2)}) collective-permute-start(bf16[2,512,128]{2,1,0:T(8,128)(2,1)S(1)} %pad_maximum_fusion.2.refs_0_), channel_id=1, source_target_pairs={{0,6},{1,7},{2,4},{3,5},{4,2},{5,3},{6,0},{7,1},{8,14},{9,15},{10,... | collective-permute-start | bytes 786440 | tf_op jit(solution)/shard_map/ppermute | solution.py:21
  39.3 11.9 %collective-permute-start.1 = (bf16[2,512,128]{2,1,0:T(8,128)(2,1)S(1)}, bf16[2,512,128]{2,1,0:T(8,128)(2,1)S(1)}, u32[]{:S(2)}, u32[]{:S(2)}) collective-permute-start(bf16[2,512,128]{2,1,0:T(8,128)(2,1)S(1)} %pad_maximum_fusion.1.refs_0_), channel_id=1, source_target_pairs={{0,2},{1,3},{2,0},{3,1},{4,6},{5,7},{6,4},{7,5},{8,10},{9,11},{10,... | collective-permute-start | bytes 786440 | tf_op jit(solution)/shard_map/ppermute | solution.py:21
  46.7 8.2 %collective-permute-start.2 = (bf16[2,512,128]{2,1,0:T(8,128)(2,1)S(1)}, bf16[2,512,128]{2,1,0:T(8,128)(2,1)S(1)}, u32[]{:S(2)}, u32[]{:S(2)}) collective-permute-start(bf16[2,512,128]{2,1,0:T(8,128)(2,1)S(1)} %pad_maximum_fusion.1.refs_0_), channel_id=1, source_target_pairs={{0,4},{1,5},{2,6},{3,7},{4,0},{5,1},{6,2},{7,3},{8,12},{9,13},{10,... | collective-permute-start | bytes 786440 | tf_op jit(solution)/shard_map/ppermute | solution.py:21
  51.9 48.8 %collective-permute-start.27 = (bf16[1024,512]{1,0:T(8,128)(2,1)}, bf16[1024,512]{1,0:T(8,128)(2,1)S(1)}, u32[]{:S(2)}, u32[]{:S(2)}) collective-permute-start(bf16[1024,512]{1,0:T(8,128)(2,1)} %get-tuple-element.39.refs_9_.refs_5_), channel_id=1, source_target_pairs={{0,8},{8,0},{16,24},{24,16},{1,9},{9,1},{17,25},{25,17},{2,10},{10... | collective-permute-start | bytes 3145736 | tf_op jit(solution)/shard_map/ppermute | solution.py:21
  54.9 8.1 %collective-permute-start.3 = (bf16[2,512,128]{2,1,0:T(8,128)(2,1)S(1)}, bf16[2,512,128]{2,1,0:T(8,128)(2,1)}, u32[]{:S(2)}, u32[]{:S(2)}) collective-permute-start(bf16[2,512,128]{2,1,0:T(8,128)(2,1)S(1)} %pad_maximum_fusion.1.refs_0_), channel_id=1, source_target_pairs={{0,6},{1,7},{2,4},{3,5},{4,2},{5,3},{6,0},{7,1},{8,14},{9,15},{10,... | collective-permute-start | bytes 786440 | tf_op jit(solution)/shard_map/ppermute | solution.py:21
  63.0 55.2 %collective-permute-start.30 = (bf16[1024,512]{1,0:T(8,128)(2,1)}, bf16[1024,512]{1,0:T(8,128)(2,1)S(1)}, u32[]{:S(2)}, u32[]{:S(2)}) collective-permute-start(bf16[1024,512]{1,0:T(8,128)(2,1)} %get-tuple-element.39.refs_9_.refs_5_), channel_id=1, source_target_pairs={{0,1},{1,0},{2,3},{3,2},{4,5},{5,4},{6,7},{7,6},{8,9},{9,8},{10,11... | collective-permute-start | bytes 3145736 | tf_op jit(solution)/shard_map/ppermute | solution.py:21
  63.0 49.1 %collective-permute-start.36 = (bf16[512,512]{1,0:T(8,128)(2,1)}, bf16[512,512]{1,0:T(8,128)(2,1)}, u32[]{:S(2)}, u32[]{:S(2)}) collective-permute-start(bf16[512,512]{1,0:T(8,128)(2,1)} %copy-done.4), channel_id=1, source_target_pairs={{0,8},{8,0},{16,24},{24,16},{1,9},{9,1},{17,25},{25,17},{2,10},{10... | collective-permute-start | bytes 1572872 | tf_op jit(solution)/shard_map/ppermute | solution.py:21
  85.5 50.0 %copy-start = (bf16[1024,512]{1,0:T(8,128)(2,1)}, bf16[1024,512]{1,0:T(8,128)(2,1)S(1)}, u32[]{:S(2)}) copy-start(bf16[1024,512]{1,0:T(8,128)(2,1)S(1)} %collective-permute-done.28.refs_11_.refs_7_) | copy-start | bytes 3145732
  85.5 47.5 %collective-permute-start.29 = (bf16[1024,512]{1,0:T(8,128)(2,1)S(1)}, bf16[1024,512]{1,0:T(8,128)(2,1)}, u32[]{:S(2)}, u32[]{:S(2)}) collective-permute-start(bf16[1024,512]{1,0:T(8,128)(2,1)S(1)} %collective-permute-done.28.refs_11_.refs_7_), channel_id=1, source_target_pairs={{0,8},{8,0},{16,24},{24,16},{1,9},{9,1},{17,25},{25,17},{2,10},{10... | collective-permute-start | bytes 3145736 | tf_op jit(solution)/shard_map/ppermute | solution.py:21
  100.7 20.0 %collective-permute-start.38 = (bf16[512,512]{1,0:T(8,128)(2,1)}, bf16[512,512]{1,0:T(8,128)(2,1)}, u32[]{:S(2)}, u32[]{:S(2)}) collective-permute-start(bf16[512,512]{1,0:T(8,128)(2,1)} %copy-done.5), channel_id=1, source_target_pairs={{0,1},{1,0},{2,3},{3,2},{4,5},{5,4},{6,7},{7,6},{8,9},{9,8},{10,11... | collective-permute-start | bytes 1572872 | tf_op jit(solution)/shard_map/ppermute | solution.py:21
  112.1 9.2 %collective-permute-start.39 = (bf16[512,512]{1,0:T(8,128)(2,1)}, bf16[512,512]{1,0:T(8,128)(2,1)}, u32[]{:S(2)}, u32[]{:S(2)}) collective-permute-start(bf16[512,512]{1,0:T(8,128)(2,1)} %copy-done.4), channel_id=1, source_target_pairs={{0,1},{1,0},{2,3},{3,2},{4,5},{5,4},{6,7},{7,6},{8,9},{9,8},{10,11... | collective-permute-start | bytes 1572872 | tf_op jit(solution)/shard_map/ppermute | solution.py:21
  112.1 9.2 %collective-permute-start.40 = (bf16[512,512]{1,0:T(8,128)(2,1)}, bf16[512,512]{1,0:T(8,128)(2,1)}, u32[]{:S(2)}, u32[]{:S(2)}) collective-permute-start(bf16[512,512]{1,0:T(8,128)(2,1)} %collective-permute-done.36.refs_4_.refs_16_), channel_id=1, source_target_pairs={{0,1},{1,0},{2,3},{3,2},{4,5},{5,4},{6,7},{7,6},{8,9},{9,8},{10,11... | collective-permute-start | bytes 1572872 | tf_op jit(solution)/shard_map/ppermute | solution.py:21
  118.2 17.3 %collective-permute-start.18 = (f32[64,1024]{1,0:T(8,128)}, f32[64,1024]{1,0:T(8,128)S(1)}, u32[]{:S(2)}, u32[]{:S(2)}) collective-permute-start(f32[64,1024]{1,0:T(8,128)} %get-tuple-element.35), channel_id=1, source_target_pairs={{0,6},{1,7},{2,4},{3,5},{4,2},{5,3},{6,0},{7,1},{8,14},{9,15},{10,... | collective-permute-start | bytes 786440 | tf_op jit(solution)/shard_map/ppermute | solution.py:21
  120.7 14.8 %collective-permute-start.19 = (f32[64,1024]{1,0:T(8,128)}, f32[64,1024]{1,0:T(8,128)}, u32[]{:S(2)}, u32[]{:S(2)}) collective-permute-start(f32[64,1024]{1,0:T(8,128)} %get-tuple-element.36), channel_id=1, source_target_pairs={{0,4},{1,5},{2,6},{3,7},{4,0},{5,1},{6,2},{7,3},{8,12},{9,13},{10,... | collective-permute-start | bytes 786440 | tf_op jit(solution)/shard_map/ppermute | solution.py:21
  121.2 52.4 %collective-permute-start.31 = (bf16[1024,512]{1,0:T(8,128)(2,1)S(1)}, bf16[1024,512]{1,0:T(8,128)(2,1)}, u32[]{:S(2)}, u32[]{:S(2)}) collective-permute-start(bf16[1024,512]{1,0:T(8,128)(2,1)S(1)} %collective-permute-done.27.refs_10_.refs_6_), channel_id=1, source_target_pairs={{0,1},{1,0},{2,3},{3,2},{4,5},{5,4},{6,7},{7,6},{8,9},{9,8},{10,11... | collective-permute-start | bytes 3145736 | tf_op jit(solution)/shard_map/ppermute | solution.py:21
  121.3 14.8 %collective-permute-start.20 = (f32[64,1024]{1,0:T(8,128)}, f32[64,1024]{1,0:T(8,128)}, u32[]{:S(2)}, u32[]{:S(2)}) collective-permute-start(f32[64,1024]{1,0:T(8,128)} %get-tuple-element.37), channel_id=1, source_target_pairs={{0,2},{1,3},{2,0},{3,1},{4,6},{5,7},{6,4},{7,5},{8,10},{9,11},{10,... | collective-permute-start | bytes 786440 | tf_op jit(solution)/shard_map/ppermute | solution.py:21
  133.0 8.1 %collective-permute-start.6 = (f32[64,1024]{1,0:T(8,128)}, f32[64,1024]{1,0:T(8,128)}, u32[]{:S(2)}, u32[]{:S(2)}) collective-permute-start(f32[64,1024]{1,0:T(8,128)} %get-tuple-element.31), channel_id=1, source_target_pairs={{0,6},{1,7},{2,4},{3,5},{4,2},{5,3},{6,0},{7,1},{8,14},{9,15},{10,... | collective-permute-start | bytes 786440 | tf_op jit(solution)/shard_map/ppermute | solution.py:21
  135.5 39.4 %collective-permute-start.32 = (bf16[1024,512]{1,0:T(8,128)(2,1)S(1)}, bf16[1024,512]{1,0:T(8,128)(2,1)S(1)}, u32[]{:S(2)}, u32[]{:S(2)}) collective-permute-start(bf16[1024,512]{1,0:T(8,128)(2,1)S(1)} %collective-permute-done.28.refs_11_.refs_7_), channel_id=1, source_target_pairs={{0,1},{1,0},{2,3},{3,2},{4,5},{5,4},{6,7},{7,6},{8,9},{9,8},{10,11... | collective-permute-start | bytes 3145736 | tf_op jit(solution)/shard_map/ppermute | solution.py:21
  135.5 39.4 %collective-permute-start.33 = (bf16[1024,512]{1,0:T(8,128)(2,1)}, bf16[1024,512]{1,0:T(8,128)(2,1)}, u32[]{:S(2)}, u32[]{:S(2)}) collective-permute-start(bf16[1024,512]{1,0:T(8,128)(2,1)} %collective-permute-done.29.refs_12_.refs_8_), channel_id=1, source_target_pairs={{0,1},{1,0},{2,3},{3,2},{4,5},{5,4},{6,7},{7,6},{8,9},{9,8},{10,11... | collective-permute-start | bytes 3145736 | tf_op jit(solution)/shard_map/ppermute | solution.py:21
  136.0 10.6 %collective-permute-start.7 = (f32[64,1024]{1,0:T(8,128)}, f32[64,1024]{1,0:T(8,128)}, u32[]{:S(2)}, u32[]{:S(2)}) collective-permute-start(f32[64,1024]{1,0:T(8,128)} %get-tuple-element.32), channel_id=1, source_target_pairs={{0,4},{1,5},{2,6},{3,7},{4,0},{5,1},{6,2},{7,3},{8,12},{9,13},{10,... | collective-permute-start | bytes 786440 | tf_op jit(solution)/shard_map/ppermute | solution.py:21
  141.1 7.0 %collective-permute-start.8 = (f32[64,1024]{1,0:T(8,128)}, f32[64,1024]{1,0:T(8,128)}, u32[]{:S(2)}, u32[]{:S(2)}) collective-permute-start(f32[64,1024]{1,0:T(8,128)} %get-tuple-element.33), channel_id=1, source_target_pairs={{0,2},{1,3},{2,0},{3,1},{4,6},{5,7},{6,4},{7,5},{8,10},{9,11},{10,... | collective-permute-start | bytes 786440 | tf_op jit(solution)/shard_map/ppermute | solution.py:21
  146.6 5.6 %collective-permute-start.21 = (bf16[64,1024]{1,0:T(8,128)(2,1)}, bf16[64,1024]{1,0:T(8,128)(2,1)S(1)}, u32[]{:S(2)}, u32[]{:S(2)}) collective-permute-start(bf16[64,1024]{1,0:T(8,128)(2,1)} %softmax.3.refs_0_), channel_id=1, source_target_pairs={{0,2},{1,3},{2,0},{3,1},{4,6},{5,7},{6,4},{7,5},{8,10},{9,11},{10,... | collective-permute-start | bytes 393224 | tf_op jit(solution)/shard_map/ppermute | solution.py:21
  148.1 8.7 %collective-permute-start.22 = (bf16[64,1024]{1,0:T(8,128)(2,1)}, bf16[64,1024]{1,0:T(8,128)(2,1)S(1)}, u32[]{:S(2)}, u32[]{:S(2)}) collective-permute-start(bf16[64,1024]{1,0:T(8,128)(2,1)} %softmax.3.refs_0_), channel_id=1, source_target_pairs={{0,4},{1,5},{2,6},{3,7},{4,0},{5,1},{6,2},{7,3},{8,12},{9,13},{10,... | collective-permute-start | bytes 393224 | tf_op jit(solution)/shard_map/ppermute | solution.py:21
  152.3 6.2 %collective-permute-start.23 = (bf16[64,1024]{1,0:T(8,128)(2,1)}, bf16[64,1024]{1,0:T(8,128)(2,1)}, u32[]{:S(2)}, u32[]{:S(2)}) collective-permute-start(bf16[64,1024]{1,0:T(8,128)(2,1)} %softmax.3.refs_0_), channel_id=1, source_target_pairs={{0,6},{1,7},{2,4},{3,5},{4,2},{5,3},{6,0},{7,1},{8,14},{9,15},{10,... | collective-permute-start | bytes 393224 | tf_op jit(solution)/shard_map/ppermute | solution.py:21
  156.8 6.2 %collective-permute-start.10 = (bf16[64,1024]{1,0:T(8,128)(2,1)}, bf16[64,1024]{1,0:T(8,128)(2,1)S(1)}, u32[]{:S(2)}, u32[]{:S(2)}) collective-permute-start(bf16[64,1024]{1,0:T(8,128)(2,1)} %softmax.2.refs_0_), channel_id=1, source_target_pairs={{0,4},{1,5},{2,6},{3,7},{4,0},{5,1},{6,2},{7,3},{8,12},{9,13},{10,... | collective-permute-start | bytes 393224 | tf_op jit(solution)/shard_map/ppermute | solution.py:21
  158.5 9.4 %collective-permute-start.11 = (bf16[64,1024]{1,0:T(8,128)(2,1)}, bf16[64,1024]{1,0:T(8,128)(2,1)}, u32[]{:S(2)}, u32[]{:S(2)}) collective-permute-start(bf16[64,1024]{1,0:T(8,128)(2,1)} %softmax.2.refs_0_), channel_id=1, source_target_pairs={{0,6},{1,7},{2,4},{3,5},{4,2},{5,3},{6,0},{7,1},{8,14},{9,15},{10,... | collective-permute-start | bytes 393224 | tf_op jit(solution)/shard_map/ppermute | solution.py:21
  163.0 6.2 %collective-permute-start.9 = (bf16[64,1024]{1,0:T(8,128)(2,1)}, bf16[64,1024]{1,0:T(8,128)(2,1)}, u32[]{:S(2)}, u32[]{:S(2)}) collective-permute-start(bf16[64,1024]{1,0:T(8,128)(2,1)} %softmax.2.refs_0_), channel_id=1, source_target_pairs={{0,2},{1,3},{2,0},{3,1},{4,6},{5,7},{6,4},{7,5},{8,10},{9,11},{10,... | collective-permute-start | bytes 393224 | tf_op jit(solution)/shard_map/ppermute | solution.py:21
  167.9 7.9 %collective-permute-start.25 = (bf16[2,512,128]{2,1,0:T(8,128)(2,1)}, bf16[2,512,128]{2,1,0:T(8,128)(2,1)}, u32[]{:S(2)}, u32[]{:S(2)}) collective-permute-start(bf16[2,512,128]{2,1,0:T(8,128)(2,1)} %pool.3.refs_4_), channel_id=1, source_target_pairs={{0,4},{1,5},{2,6},{3,7},{4,0},{5,1},{6,2},{7,3},{8,12},{9,13},{10,... | collective-permute-start | bytes 786440 | tf_op jit(solution)/shard_map/ppermute | solution.py:21
  169.2 9.5 %collective-permute-start.24 = (bf16[2,512,128]{2,1,0:T(8,128)(2,1)}, bf16[2,512,128]{2,1,0:T(8,128)(2,1)}, u32[]{:S(2)}, u32[]{:S(2)}) collective-permute-start(bf16[2,512,128]{2,1,0:T(8,128)(2,1)} %pool.3.refs_4_), channel_id=1, source_target_pairs={{0,2},{1,3},{2,0},{3,1},{4,6},{5,7},{6,4},{7,5},{8,10},{9,11},{10,... | collective-permute-start | bytes 786440 | tf_op jit(solution)/shard_map/ppermute | solution.py:21
  173.6 10.4 %collective-permute-start.12 = (bf16[2,512,128]{2,1,0:T(8,128)(2,1)}, bf16[2,512,128]{2,1,0:T(8,128)(2,1)S(1)}, u32[]{:S(2)}, u32[]{:S(2)}) collective-permute-start(bf16[2,512,128]{2,1,0:T(8,128)(2,1)} %pool.2.refs_0_), channel_id=1, source_target_pairs={{0,2},{1,3},{2,0},{3,1},{4,6},{5,7},{6,4},{7,5},{8,10},{9,11},{10,... | collective-permute-start | bytes 786440 | tf_op jit(solution)/shard_map/ppermute | solution.py:21
  174.9 17.2 %collective-permute-start.53 = (bf16[2,512,128]{2,1,0:T(8,128)(2,1)S(1)}, bf16[2,512,128]{2,1,0:T(8,128)(2,1)S(1)}, u32[]{:S(2)}, u32[]{:S(2)}) collective-permute-start(bf16[2,512,128]{2,1,0:T(8,128)(2,1)S(1)} %copy-done.7), channel_id=1, source_target_pairs={{0,16},{8,24},{16,0},{24,8},{1,17},{9,25},{17,1},{25,9},{2,18},{10... | collective-permute-start | bytes 786440 | tf_op jit(solution)/shard_map/ppermute | solution.py:21
  174.9 18.8 %collective-permute-start.13 = (bf16[2,512,128]{2,1,0:T(8,128)(2,1)}, bf16[2,512,128]{2,1,0:T(8,128)(2,1)S(1)}, u32[]{:S(2)}, u32[]{:S(2)}) collective-permute-start(bf16[2,512,128]{2,1,0:T(8,128)(2,1)} %pool.2.refs_0_), channel_id=1, source_target_pairs={{0,4},{1,5},{2,6},{3,7},{4,0},{5,1},{6,2},{7,3},{8,12},{9,13},{10,... | collective-permute-start | bytes 786440 | tf_op jit(solution)/shard_map/ppermute | solution.py:21
  175.8 21.7 %collective-permute-start.43 = (bf16[2,512,128]{2,1,0:T(8,128)(2,1)}, bf16[2,512,128]{2,1,0:T(8,128)(2,1)S(1)}, u32[]{:S(2)}, u32[]{:S(2)}) collective-permute-start(bf16[2,512,128]{2,1,0:T(8,128)(2,1)} %pool.2.refs_0_), channel_id=1, source_target_pairs={{0,16},{8,24},{16,0},{24,8},{1,17},{9,25},{17,1},{25,9},{2,18},{10... | collective-permute-start | bytes 786440 | tf_op jit(solution)/shard_map/ppermute | solution.py:21
  178.7 20.2 %collective-permute-start.26 = (bf16[2,512,128]{2,1,0:T(8,128)(2,1)}, bf16[2,512,128]{2,1,0:T(8,128)(2,1)}, u32[]{:S(2)}, u32[]{:S(2)}) collective-permute-start(bf16[2,512,128]{2,1,0:T(8,128)(2,1)} %collective-permute-done.25.refs_6_), channel_id=1, source_target_pairs={{0,2},{1,3},{2,0},{3,1},{4,6},{5,7},{6,4},{7,5},{8,10},{9,11},{10,... | collective-permute-start | bytes 786440 | tf_op jit(solution)/shard_map/ppermute | solution.py:21
  184.0 15.5 %collective-permute-start.14 = (bf16[2,512,128]{2,1,0:T(8,128)(2,1)S(1)}, bf16[2,512,128]{2,1,0:T(8,128)(2,1)S(1)}, u32[]{:S(2)}, u32[]{:S(2)}) collective-permute-start(bf16[2,512,128]{2,1,0:T(8,128)(2,1)S(1)} %collective-permute-done.12.refs_1_), channel_id=1, source_target_pairs={{0,4},{1,5},{2,6},{3,7},{4,0},{5,1},{6,2},{7,3},{8,12},{9,13},{10,... | collective-permute-start | bytes 786440 | tf_op jit(solution)/shard_map/ppermute | solution.py:21
  192.0 27.0 %collective-permute-start.54 = (bf16[2,512,128]{2,1,0:T(8,128)(2,1)S(1)}, bf16[2,512,128]{2,1,0:T(8,128)(2,1)S(1)}, u32[]{:S(2)}, u32[]{:S(2)}) collective-permute-start(bf16[2,512,128]{2,1,0:T(8,128)(2,1)S(1)} %collective-permute-done.53.refs_0_), channel_id=1, source_target_pairs={{0,2},{1,3},{2,0},{3,1},{4,6},{5,7},{6,4},{7,5},{8,10},{9,11},{10,... | collective-permute-start | bytes 786440 | tf_op jit(solution)/shard_map/ppermute | solution.py:21
  193.7 25.8 %collective-permute-start.55 = (bf16[2,512,128]{2,1,0:T(8,128)(2,1)S(1)}, bf16[2,512,128]{2,1,0:T(8,128)(2,1)S(1)}, u32[]{:S(2)}, u32[]{:S(2)}) collective-permute-start(bf16[2,512,128]{2,1,0:T(8,128)(2,1)S(1)} %collective-permute-done.53.refs_0_), channel_id=1, source_target_pairs={{0,4},{1,5},{2,6},{3,7},{4,0},{5,1},{6,2},{7,3},{8,12},{9,13},{10,... | collective-permute-start | bytes 786440 | tf_op jit(solution)/shard_map/ppermute | solution.py:21
  197.5 23.7 %collective-permute-start.56 = (bf16[2,512,128]{2,1,0:T(8,128)(2,1)S(1)}, bf16[2,512,128]{2,1,0:T(8,128)(2,1)S(1)}, u32[]{:S(2)}, u32[]{:S(2)}) collective-permute-start(bf16[2,512,128]{2,1,0:T(8,128)(2,1)S(1)} %collective-permute-done.53.refs_0_), channel_id=1, source_target_pairs={{0,6},{1,7},{2,4},{3,5},{4,2},{5,3},{6,0},{7,1},{8,14},{9,15},{10,... | collective-permute-start | bytes 786440 | tf_op jit(solution)/shard_map/ppermute | solution.py:21
  198.9 33.1 %collective-permute-start.44 = (bf16[2,512,128]{2,1,0:T(8,128)(2,1)S(1)}, bf16[2,512,128]{2,1,0:T(8,128)(2,1)S(1)}, u32[]{:S(2)}, u32[]{:S(2)}) collective-permute-start(bf16[2,512,128]{2,1,0:T(8,128)(2,1)S(1)} %collective-permute-done.43.refs_0_), channel_id=1, source_target_pairs={{0,2},{1,3},{2,0},{3,1},{4,6},{5,7},{6,4},{7,5},{8,10},{9,11},{10,... | collective-permute-start | bytes 786440 | tf_op jit(solution)/shard_map/ppermute | solution.py:21
  200.2 33.4 %collective-permute-start.45 = (bf16[2,512,128]{2,1,0:T(8,128)(2,1)S(1)}, bf16[2,512,128]{2,1,0:T(8,128)(2,1)S(1)}, u32[]{:S(2)}, u32[]{:S(2)}) collective-permute-start(bf16[2,512,128]{2,1,0:T(8,128)(2,1)S(1)} %collective-permute-done.43.refs_0_), channel_id=1, source_target_pairs={{0,4},{1,5},{2,6},{3,7},{4,0},{5,1},{6,2},{7,3},{8,12},{9,13},{10,... | collective-permute-start | bytes 786440 | tf_op jit(solution)/shard_map/ppermute | solution.py:21
  219.0 33.7 %collective-permute-start.51 = (bf16[2,2,512,128]{3,2,1,0:T(8,128)(2,1)}, bf16[2,2,512,128]{3,2,1,0:T(8,128)(2,1)S(1)}, u32[]{:S(2)}, u32[]{:S(2)}) collective-permute-start(bf16[2,2,512,128]{3,2,1,0:T(8,128)(2,1)} %get-tuple-element.50), channel_id=1, source_target_pairs={{0,4},{1,5},{2,6},{3,7},{4,0},{5,1},{6,2},{7,3},{8,12},{9,13},{10,... | collective-permute-start | bytes 1572872 | tf_op jit(solution)/shard_map/ppermute | solution.py:21
  219.6 14.5 %collective-permute-start.46 = (bf16[2,512,128]{2,1,0:T(8,128)(2,1)S(1)}, bf16[2,512,128]{2,1,0:T(8,128)(2,1)S(1)}, u32[]{:S(2)}, u32[]{:S(2)}) collective-permute-start(bf16[2,512,128]{2,1,0:T(8,128)(2,1)S(1)} %collective-permute-done.43.refs_0_), channel_id=1, source_target_pairs={{0,6},{1,7},{2,4},{3,5},{4,2},{5,3},{6,0},{7,1},{8,14},{9,15},{10,... | collective-permute-start | bytes 786440 | tf_op jit(solution)/shard_map/ppermute | solution.py:21
  230.5 18.5 %collective-permute-start.57 = (bf16[2,512,128]{2,1,0:T(8,128)(2,1)}, bf16[2,512,128]{2,1,0:T(8,128)(2,1)S(1)}, u32[]{:S(2)}, u32[]{:S(2)}) collective-permute-start(bf16[2,512,128]{2,1,0:T(8,128)(2,1)} %get-tuple-element.52), channel_id=1, source_target_pairs={{0,6},{1,7},{2,4},{3,5},{4,2},{5,3},{6,0},{7,1},{8,14},{9,15},{10,... | collective-permute-start | bytes 786440 | tf_op jit(solution)/shard_map/ppermute | solution.py:21
  232.0 18.5 %collective-permute-start.58 = (bf16[2,512,128]{2,1,0:T(8,128)(2,1)}, bf16[2,512,128]{2,1,0:T(8,128)(2,1)S(1)}, u32[]{:S(2)}, u32[]{:S(2)}) collective-permute-start(bf16[2,512,128]{2,1,0:T(8,128)(2,1)} %get-tuple-element.53), channel_id=1, source_target_pairs={{0,4},{1,5},{2,6},{3,7},{4,0},{5,1},{6,2},{7,3},{8,12},{9,13},{10,... | collective-permute-start | bytes 786440 | tf_op jit(solution)/shard_map/ppermute | solution.py:21
  233.5 17.6 %collective-permute-start.59 = (bf16[2,512,128]{2,1,0:T(8,128)(2,1)}, bf16[2,512,128]{2,1,0:T(8,128)(2,1)S(1)}, u32[]{:S(2)}, u32[]{:S(2)}) collective-permute-start(bf16[2,512,128]{2,1,0:T(8,128)(2,1)} %get-tuple-element.54), channel_id=1, source_target_pairs={{0,2},{1,3},{2,0},{3,1},{4,6},{5,7},{6,4},{7,5},{8,10},{9,11},{10,... | collective-permute-start | bytes 786440 | tf_op jit(solution)/shard_map/ppermute | solution.py:21
  234.8 35.8 %collective-permute-start.41 = (bf16[2,2,512,128]{3,2,1,0:T(8,128)(2,1)}, bf16[2,2,512,128]{3,2,1,0:T(8,128)(2,1)S(1)}, u32[]{:S(2)}, u32[]{:S(2)}) collective-permute-start(bf16[2,2,512,128]{3,2,1,0:T(8,128)(2,1)} %get-tuple-element.44), channel_id=1, source_target_pairs={{0,2},{1,3},{2,0},{3,1},{4,6},{5,7},{6,4},{7,5},{8,10},{9,11},{10,... | collective-permute-start | bytes 1572872 | tf_op jit(solution)/shard_map/ppermute | solution.py:21
  249.1 14.3 %collective-permute-start.47 = (bf16[2,512,128]{2,1,0:T(8,128)(2,1)}, bf16[2,512,128]{2,1,0:T(8,128)(2,1)S(1)}, u32[]{:S(2)}, u32[]{:S(2)}) collective-permute-start(bf16[2,512,128]{2,1,0:T(8,128)(2,1)} %get-tuple-element.46), channel_id=1, source_target_pairs={{0,6},{1,7},{2,4},{3,5},{4,2},{5,3},{6,0},{7,1},{8,14},{9,15},{10,... | collective-permute-start | bytes 786440 | tf_op jit(solution)/shard_map/ppermute | solution.py:21
  250.5 14.4 %collective-permute-start.48 = (bf16[2,512,128]{2,1,0:T(8,128)(2,1)}, bf16[2,512,128]{2,1,0:T(8,128)(2,1)S(1)}, u32[]{:S(2)}, u32[]{:S(2)}) collective-permute-start(bf16[2,512,128]{2,1,0:T(8,128)(2,1)} %get-tuple-element.47), channel_id=1, source_target_pairs={{0,4},{1,5},{2,6},{3,7},{4,0},{5,1},{6,2},{7,3},{8,12},{9,13},{10,... | collective-permute-start | bytes 786440 | tf_op jit(solution)/shard_map/ppermute | solution.py:21
  251.2 17.7 %collective-permute-start.49 = (bf16[2,512,128]{2,1,0:T(8,128)(2,1)}, bf16[2,512,128]{2,1,0:T(8,128)(2,1)S(1)}, u32[]{:S(2)}, u32[]{:S(2)}) collective-permute-start(bf16[2,512,128]{2,1,0:T(8,128)(2,1)} %get-tuple-element.48), channel_id=1, source_target_pairs={{0,2},{1,3},{2,0},{3,1},{4,6},{5,7},{6,4},{7,5},{8,10},{9,11},{10,... | collective-permute-start | bytes 786440 | tf_op jit(solution)/shard_map/ppermute | solution.py:21
  252.8 19.3 %collective-permute-start.60 = (bf16[2,512,128]{2,1,0:T(8,128)(2,1)S(1)}, bf16[2,512,128]{2,1,0:T(8,128)(2,1)S(1)}, u32[]{:S(2)}, u32[]{:S(2)}) collective-permute-start(bf16[2,512,128]{2,1,0:T(8,128)(2,1)S(1)} %add_convert_fusion), channel_id=1, source_target_pairs={{0,16},{8,24},{16,0},{24,8},{1,17},{9,25},{17,1},{25,9},{2,18},{10... | collective-permute-start | bytes 786440 | tf_op jit(solution)/shard_map/ppermute | solution.py:21
  263.4 8.8 %collective-permute-start.52 = (bf16[1,2,512,128]{3,2,1,0:T(8,128)(2,1)S(1)}, bf16[1,2,512,128]{3,2,1,0:T(8,128)(2,1)S(1)}, u32[]{:S(2)}, u32[]{:S(2)}) collective-permute-start(bf16[1,2,512,128]{3,2,1,0:T(8,128)(2,1)S(1)} %add_convert_fusion.1), channel_id=1, source_target_pairs={{0,2},{1,3},{2,0},{3,1},{4,6},{5,7},{6,4},{7,5},{8,10},{9,11},{10,... | collective-permute-start | bytes 786440 | tf_op jit(solution)/shard_map/ppermute | solution.py:21
  270.7 9.7 %collective-permute-start.50 = (bf16[2,512,128]{2,1,0:T(8,128)(2,1)}, bf16[2,512,128]{2,1,0:T(8,128)(2,1)S(1)}, u32[]{:S(2)}, u32[]{:S(2)}) collective-permute-start(bf16[2,512,128]{2,1,0:T(8,128)(2,1)} %add_convert_fusion.2), channel_id=1, source_target_pairs={{0,16},{8,24},{16,0},{24,8},{1,17},{9,25},{17,1},{25,9},{2,18},{10... | collective-permute-start | bytes 786440 | tf_op jit(solution)/shard_map/ppermute | solution.py:21
  271.4 8.9 %collective-permute-start.42 = (bf16[1,2,512,128]{3,2,1,0:T(8,128)(2,1)}, bf16[1,2,512,128]{3,2,1,0:T(8,128)(2,1)}, u32[]{:S(2)}, u32[]{:S(2)}) collective-permute-start(bf16[1,2,512,128]{3,2,1,0:T(8,128)(2,1)} %add_convert_fusion.3), channel_id=1, source_target_pairs={{0,4},{1,5},{2,6},{3,7},{4,0},{5,1},{6,2},{7,3},{8,12},{9,13},{10,... | collective-permute-start | bytes 786440 | tf_op jit(solution)/shard_map/ppermute | solution.py:21
  281.4 1.6 collective-permute-start.61
  (30 other events, 298.4 us)

commit v3 on v2

--- a/solution.py
+++ b/solution.py
@@ -19,6 +19,10 @@
 
 def swap(x, axis_name, count, offset):
     return lax.ppermute(x, axis_name, [(i, i ^ offset) for i in range(count)])
+
+
+def in_vmem(arrays):
+    return [pltpu.with_memory_space_constraint(x, pltpu.VMEM) for x in arrays]
 
 
 def dot(a, b, dims):
@@ -84,6 +88,7 @@
         ),
         out_shape=[jax.ShapeDtypeStruct((rows, length), jnp.float32)] * chips,
         name="scores",
+        compiler_params=pltpu.CompilerParams(vmem_limit_bytes=24 << 20),
     )(where, *cand_parts, *bilinears, *behaviors)
 
 
@@ -110,7 +115,8 @@
         out_specs=VMEM_WHOLE,
         out_shape=jax.ShapeDtypeStruct((rows, length), jnp.bfloat16),
         name="softmax",
-    )(where, lengths, *parts)
+        compiler_params=pltpu.CompilerParams(vmem_limit_bytes=8 << 20),
+    )(where, lengths, parts[0], *in_vmem(parts[1:]))
 
 
 def pool(where, prob_parts, behaviors, cands, which):
@@ -147,14 +153,16 @@
         grid_spec=pltpu.PrefetchScalarGridSpec(
             num_scalar_prefetch=1,
             grid=(group,),
-            in_specs=[pl.BlockSpec((rows, length), lambda i, w: (0, 0))] * chips
+            in_specs=[pl.BlockSpec((rows, length), lambda i, w: (0, 0))]
+            + [VMEM_WHOLE] * (chips - 1)
             + [mine_block] * 2,
             out_specs=pl.BlockSpec((1, 2 * width, cands), lambda i, w: (i, 0, 0)),
             scratch_shapes=[pltpu.VMEM((group * cands, length), jnp.bfloat16)],
         ),
         out_shape=jax.ShapeDtypeStruct((group, 2 * width, cands), jnp.bfloat16),
         name="pool",
-    )(where, *prob_parts, *behaviors)
+        compiler_params=pltpu.CompilerParams(vmem_limit_bytes=16 << 20),
+    )(where, prob_parts[0], *in_vmem(prob_parts[1:]), *behaviors)
 
 
 def tile_of(units):
@@ -199,6 +207,7 @@
             pltpu.SemaphoreType.DMA((2, 3)),
         ],
         name="pack_expand",
+        compiler_params=pltpu.CompilerParams(vmem_limit_bytes=16 << 20),
     )(gate, up)
 
 
@@ -218,6 +227,7 @@
         out_shape=[jax.ShapeDtypeStruct((width, units), down.dtype)] * 2
         + [jax.ShapeDtypeStruct((row.shape[1], lanes), row.dtype)],
         name="pack_down",
+        compiler_params=pltpu.CompilerParams(vmem_limit_bytes=16 << 20),
     )(where, down, row)
 
 
@@ -367,8 +377,8 @@
         in_specs += [IN_PLACE]
     scratch = [pltpu.SemaphoreType.DMA((count * chips + 4 * layers,))] + scratch
     if downs:
-        inputs += down[0] + down[1]
-        in_specs += [IN_PLACE] * (2 * layers)
+        inputs += in_vmem(down[0] + down[1])
+        in_specs += [VMEM_WHOLE] * (2 * layers)
         shape = (size, chip_width, cands)
         if orders is not None:
             shape = (chips // 2,) + shape
@@ -384,6 +394,7 @@
         out_shape=out_shape,
         scratch_shapes=scratch,
         name="feed_forward",
+        compiler_params=pltpu.CompilerParams(vmem_limit_bytes=36 << 20),
     )(*inputs)
 
 

time: 284 us -> 275 us (0.968)
  Pallas kernels: 67.3 us -> 45.4 us
  waiting for transfers between devices: 140 us -> 149 us
  local copies, waits for them, and re-layouts: 3.92 us -> 8.66 us
    pallas_call x5, Pallas kernels: 38.6 us -> 29.1 us  [feed_forward(): pl.pallas_call(body, in_specs=in_specs, out_specs=[VMEM_WHOLE] * len(out_...]
    ppermute x62, waiting for transfers between devices: 140 us -> 149 us  [swap(): return lax.ppermute(x, axis_name, [(i, i ^ offset) for i in range(count)])]
    pallas_call x2, Pallas kernels: 11.2 us -> 6.46 us  [score_parts(): pl.pallas_call(body, grid_spec=pltpu.PrefetchScalarGridSpec(num_scalar_pr...]
    unnamed x64 -> x22, local copies, waits for them, and re-layouts: 2.9 us -> 6.3 us
  transfers between devices with their start and end apart: 62 -> 62, of which waited for: 21 -> 23; matrix products, arithmetic and copies ran while one was open for 2% -> 1% of each run, Pallas kernels for 24% -> 17%
where the time goes in v3:
time: 275 us
  waiting for transfers between devices  149 us (54%)
  starting transfers between devices  67 us (24%)
  Pallas kernels  45.4 us (17%)
  local copies, waits for them, and re-layouts  8.66 us (3%)
  other arithmetic  3.85 us (1%)
    ppermute x62, waiting for transfers between devices, swap(): return lax.ppermute(x, axis_name, [(i, i ^ offset) for i in range(count)])  149 us
    ppermute x62, starting transfers between devices, swap(): return lax.ppermute(x, axis_name, [(i, i ^ offset) for i in range(count)])  67 us
    pallas_call x5, Pallas kernels, feed_forward(): pl.pallas_call(body, in_specs=in_specs, out_specs=[VMEM_WHOLE] * len(out_...  29.1 us
    pallas_call x2, Pallas kernels, score_parts(): pl.pallas_call(body, grid_spec=pltpu.PrefetchScalarGridSpec(num_scalar_pr...  6.46 us
    unnamed x22, local copies, waits for them, and re-layouts  6.3 us
  transfers between devices with their start and end apart: 62, of which 23 were waited for; matrix products, arithmetic and copies ran while one was open for 1% of the time, Pallas kernels for 17%

profile of v3, /device:TPU:0, one launch (start us, length us, event | category | flops | bytes accessed | tf_op | source)
XLA Modules:
  0.0 274.5 jit_solution(15057293687202659285)
XLA Ops:
  0.6 1.2 copy-done.2
  2.5 1.8 pack_down.1
  4.3 4.1 %collective-permute-start.35 = (bf16[512,512]{1,0:T(8,128)(2,1)}, bf16[512,512]{1,0:T(8,128)(2,1)S(1)}, u32[]{:S(2)}, u32[]{:S(2)}) collective-permute-start(bf16[512,512]{1,0:T(8,128)(2,1)} %get-tuple-element.42), channel_id=1, source_target_pairs={{0,16},{8,24},{16,0},{24,8},{1,17},{9,25},{17,1},{25,9},{2,18},{10... | collective-permute-start | bytes 1572872 | tf_op jit(solution)/shard_map/ppermute | solution.py:21
  8.4 1.6 collective-permute-start.34
  12.3 1.6 collective-permute-start.15
  13.9 18.1 %collective-permute-done.35.refs_3_.refs_15_ = bf16[512,512]{1,0:T(8,128)(2,1)S(1)} collective-permute-done((bf16[512,512]{1,0:T(8,128)(2,1)}, bf16[512,512]{1,0:T(8,128)(2,1)S(1)}, u32[]{:S(2)}, u32[]{:S(2)}) %collective-permute-start.35) | collective-permute-done | bytes 524320 | tf_op jit(solution)/shard_map/ppermute | solution.py:21
  32.0 1.6 collective-permute-start.16
  36.0 1.2 pack_expand.1
  37.4 2.4 collective-permute-start.17
  40.8 6.7 %collective-permute-done.17.refs_3_ = bf16[2,512,128]{2,1,0:T(8,128)(2,1)S(1)} collective-permute-done((bf16[2,512,128]{2,1,0:T(8,128)(2,1)S(1)}, bf16[2,512,128]{2,1,0:T(8,128)(2,1)S(1)}, u32[]{:S(2)}, u32[]{:S(2)}) %collective-permute-start.17) | collective-permute-done | bytes 262176 | tf_op jit(solution)/shard_map/ppermute | solution.py:21
  47.5 1.4 collective-permute-start.2
  49.0 3.4 %collective-permute-done.1.refs_1_ = bf16[2,512,128]{2,1,0:T(8,128)(2,1)S(1)} collective-permute-done((bf16[2,512,128]{2,1,0:T(8,128)(2,1)S(1)}, bf16[2,512,128]{2,1,0:T(8,128)(2,1)S(1)}, u32[]{:S(2)}, u32[]{:S(2)}) %collective-permute-start.1) | collective-permute-done | bytes 262176 | tf_op jit(solution)/shard_map/ppermute | solution.py:21
  52.4 2.9 %collective-permute-start.27 = (bf16[1024,512]{1,0:T(8,128)(2,1)S(1)}, bf16[1024,512]{1,0:T(8,128)(2,1)S(1)}, u32[]{:S(2)}, u32[]{:S(2)}) collective-permute-start(bf16[1024,512]{1,0:T(8,128)(2,1)S(1)} %get-tuple-element.39.refs_9_.refs_5_), channel_id=1, source_target_pairs={{0,8},{8,0},{16,24},{24,16},{1,9},{9,1},{17,25},{25,17},{2,10},{10... | collective-permute-start | bytes 3145736 | tf_op jit(solution)/shard_map/ppermute | solution.py:21
  55.3 2.4 collective-permute-start.3
  57.8 5.8 %collective-permute-done.3.refs_3_ = bf16[2,512,128]{2,1,0:T(8,128)(2,1)S(1)} collective-permute-done((bf16[2,512,128]{2,1,0:T(8,128)(2,1)S(1)}, bf16[2,512,128]{2,1,0:T(8,128)(2,1)S(1)}, u32[]{:S(2)}, u32[]{:S(2)}) %collective-permute-start.3) | collective-permute-done | bytes 262176 | tf_op jit(solution)/shard_map/ppermute | solution.py:21
  63.5 2.0 collective-permute-start.36
  65.5 20.9 %collective-permute-done.28.refs_11_.refs_7_ = bf16[1024,512]{1,0:T(8,128)(2,1)S(1)} collective-permute-done((bf16[1024,512]{1,0:T(8,128)(2,1)S(1)}, bf16[1024,512]{1,0:T(8,128)(2,1)S(1)}, u32[]{:S(2)}, u32[]{:S(2)}) %collective-permute-start.28) | collective-permute-done | bytes 1048608 | tf_op jit(solution)/shard_map/ppermute | solution.py:21
  86.4 14.5 %collective-permute-done.27.refs_10_.refs_6_ = bf16[1024,512]{1,0:T(8,128)(2,1)S(1)} collective-permute-done((bf16[1024,512]{1,0:T(8,128)(2,1)S(1)}, bf16[1024,512]{1,0:T(8,128)(2,1)S(1)}, u32[]{:S(2)}, u32[]{:S(2)}) %collective-permute-start.27) | collective-permute-done | bytes 1048608 | tf_op jit(solution)/shard_map/ppermute | solution.py:21
  100.9 11.2 %collective-permute-done.36.refs_4_.refs_16_ = bf16[512,512]{1,0:T(8,128)(2,1)S(1)} collective-permute-done((bf16[512,512]{1,0:T(8,128)(2,1)S(1)}, bf16[512,512]{1,0:T(8,128)(2,1)S(1)}, u32[]{:S(2)}, u32[]{:S(2)}) %collective-permute-start.36) | collective-permute-done | bytes 524320 | tf_op jit(solution)/shard_map/ppermute | solution.py:21
  112.7 1.2 copy-done.1
  113.9 3.2 %scores.3 = (f32[64,1024]{1,0:T(8,128)S(1)}, f32[64,1024]{1,0:T(8,128)S(1)}, f32[64,1024]{1,0:T(8,128)S(1)}, f32[64,1024]{1,0:T(8,128)S(1)}) custom-call(s32[4]{0:T(128)S(1)} %pad_add_fusion.where_ref, bf16[2,512,128]{2,1,0:T(8,128)(2,1)S(1)} %pad_maximum_fusion.2.refs_0_, bf16[2,512,128]{2,1,0:T(8,128)(2,1)S(1)} %collective-permute-done.15.refs_1_, ...), custom_call_target="tpu_custom_call" | custom-call | tf_op jit(solution)/shard_map/scores/pallas_call | solution.py:79
  117.2 2.5 collective-permute-start.18
  120.8 3.2 %scores.2 = (f32[64,1024]{1,0:T(8,128)S(1)}, f32[64,1024]{1,0:T(8,128)S(1)}, f32[64,1024]{1,0:T(8,128)S(1)}, f32[64,1024]{1,0:T(8,128)S(1)}) custom-call(s32[4]{0:T(128)S(1)} %pad_add_fusion.where_ref, bf16[2,512,128]{2,1,0:T(8,128)(2,1)S(1)} %pad_maximum_fusion.1.refs_0_, bf16[2,512,128]{2,1,0:T(8,128)(2,1)S(1)} %collective-permute-done.1.refs_1_, ...), custom_call_target="tpu_custom_call" | custom-call | tf_op jit(solution)/shard_map/scores/pallas_call | solution.py:79
  124.0 9.3 %collective-permute-done.29.refs_12_.refs_8_ = bf16[1024,512]{1,0:T(8,128)(2,1)S(1)} collective-permute-done((bf16[1024,512]{1,0:T(8,128)(2,1)S(1)}, bf16[1024,512]{1,0:T(8,128)(2,1)S(1)}, u32[]{:S(2)}, u32[]{:S(2)}) %collective-permute-start.29) | collective-permute-done | bytes 1048608 | tf_op jit(solution)/shard_map/ppermute | solution.py:21
  133.3 2.4 collective-permute-start.6
  136.8 4.5 %collective-permute-done.6.refs_1_ = f32[64,1024]{1,0:T(8,128)S(1)} collective-permute-done((f32[64,1024]{1,0:T(8,128)S(1)}, f32[64,1024]{1,0:T(8,128)S(1)}, u32[]{:S(2)}, u32[]{:S(2)}) %collective-permute-start.6) | collective-permute-done | bytes 262176 | tf_op jit(solution)/shard_map/ppermute | solution.py:21
  141.3 1.5 collective-permute-start.8
  143.6 3.2 %collective-permute-done.7.refs_2_ = f32[64,1024]{1,0:T(8,128)S(1)} collective-permute-done((f32[64,1024]{1,0:T(8,128)S(1)}, f32[64,1024]{1,0:T(8,128)S(1)}, u32[]{:S(2)}, u32[]{:S(2)}) %collective-permute-start.7) | collective-permute-done | bytes 262176 | tf_op jit(solution)/shard_map/ppermute | solution.py:21
  146.8 1.5 collective-permute-start.21
  148.3 1.5 collective-permute-start.22
  149.8 2.4 collective-permute-done.21.refs_1_
  152.3 2.4 collective-permute-start.23
  156.1 2.1 collective-permute-done.23.refs_3_
  158.2 2.3 collective-permute-start.11
  160.6 1.8 collective-permute-done.10.refs_2_
  163.4 2.7 pool.3.refs_4_
  166.2 1.6 collective-permute-start.25
  168.6 2.6 pool.2.refs_0_
  171.1 1.3 collective-permute-start.12
  174.0 2.2 collective-permute-start.43
  177.7 4.9 %collective-permute-done.12.refs_1_ = bf16[2,512,128]{2,1,0:T(8,128)(2,1)S(1)} collective-permute-done((bf16[2,512,128]{2,1,0:T(8,128)(2,1)S(1)}, bf16[2,512,128]{2,1,0:T(8,128)(2,1)S(1)}, u32[]{:S(2)}, u32[]{:S(2)}) %collective-permute-start.12) | collective-permute-done | bytes 262176 | tf_op jit(solution)/shard_map/ppermute | solution.py:21
  183.1 8.4 %collective-permute-done.53.refs_0_ = bf16[2,512,128]{2,1,0:T(8,128)(2,1)S(1)} collective-permute-done((bf16[2,512,128]{2,1,0:T(8,128)(2,1)S(1)}, bf16[2,512,128]{2,1,0:T(8,128)(2,1)S(1)}, u32[]{:S(2)}, u32[]{:S(2)}) %collective-permute-start.53) | collective-permute-done | bytes 262176 | tf_op jit(solution)/shard_map/ppermute | solution.py:21
  192.0 1.4 collective-permute-start.55
  193.5 3.5 %collective-permute-done.43.refs_0_ = bf16[2,512,128]{2,1,0:T(8,128)(2,1)S(1)} collective-permute-done((bf16[2,512,128]{2,1,0:T(8,128)(2,1)S(1)}, bf16[2,512,128]{2,1,0:T(8,128)(2,1)S(1)}, u32[]{:S(2)}, u32[]{:S(2)}) %collective-permute-start.43) | collective-permute-done | bytes 262176 | tf_op jit(solution)/shard_map/ppermute | solution.py:21
  197.0 1.4 collective-permute-start.56
  199.0 1.5 collective-permute-start.45
  200.5 9.0 %feed_forward.5.refs_0_ = bf16[1024,512]{1,0:T(8,128)(2,1)S(1)} custom-call(s32[4]{0:T(128)S(1)} %pad_add_fusion.where_ref, bf16[2,512,128]{2,1,0:T(8,128)(2,1)S(1)} %pool.2.refs_0_, bf16[2,512,128]{2,1,0:T(8,128)(2,1)S(1)} %collective-permute-done.12.refs_1_, bf16[2,512,128]{2,1,0:T(8,128)(2,1)S(1)} %collective-permute-done.13.refs_2_, ...), custom_call_target="tpu_custom_call" | custom-call | tf_op jit(solution)/shard_map/feed_forward/pallas_call | solution.py:390
  209.5 3.8 %feed_forward.6 = (bf16[2,2,512,128]{3,2,1,0:T(8,128)(2,1)S(1)}, bf16[2,2,512,128]{3,2,1,0:T(8,128)(2,1)S(1)}, bf16[2,2,512,128]{3,2,1,0:T(8,128)(2,1)S(1)}, bf16[2,2,512,128]{3,2,1,0:T(8,128)(2,1)S(1)}) custom-call(s32[4]{0:T(128)S(1)} %pad_add_fusion.where_ref, bf16[1024,512]{1,0:T(8,128)(2,1)S(1)} %feed_forward.5.refs_0_, ...), custom_call_target="tpu_custom_call" | custom-call | tf_op jit(solution)/shard_map/feed_forward/pallas_call | solution.py:390
  214.0 1.5 collective-permute-start.46
  215.4 7.6 %feed_forward.9 = (bf16[2,512,128]{2,1,0:T(8,128)(2,1)S(1)}, bf16[2,512,128]{2,1,0:T(8,128)(2,1)S(1)}, bf16[2,512,128]{2,1,0:T(8,128)(2,1)S(1)}, bf16[2,512,128]{2,1,0:T(8,128)(2,1)S(1)}) custom-call(s32[4]{0:T(128)S(1)} %pad_add_fusion.where_ref, bf16[2,512,128]{2,1,0:T(8,128)(2,1)S(1)} %collective-permute-done.53.refs_0_, ...), custom_call_target="tpu_custom_call" | custom-call | tf_op jit(solution)/shard_map/feed_forward/pallas_call | solution.py:390
  223.1 1.5 collective-permute-start.57
  224.6 1.5 collective-permute-start.58
  226.6 1.5 collective-permute-start.41
  228.1 5.9 %feed_forward.7.refs_0_ = bf16[1024,256]{1,0:T(8,128)(2,1)S(1)} custom-call(s32[4]{0:T(128)S(1)} %pad_add_fusion.where_ref, bf16[2,512,128]{2,1,0:T(8,128)(2,1)S(1)} %collective-permute-done.43.refs_0_, bf16[2,512,128]{2,1,0:T(8,128)(2,1)S(1)} %collective-permute-done.44.refs_1_, bf16[2,512,128]{2,1,0:T(8,128)(2,1)S(1)} %collective-permute-done.45.refs_2_, ...), custom_call_target="tpu_custom_call" | custom-call | tf_op jit(solution)/shard_map/feed_forward/pallas_call | solution.py:390
  234.1 2.7 feed_forward.8
  236.8 1.5 collective-permute-start.47
  238.3 5.0 %collective-permute-done.58 = bf16[2,512,128]{2,1,0:T(8,128)(2,1)S(1)} collective-permute-done((bf16[2,512,128]{2,1,0:T(8,128)(2,1)S(1)}, bf16[2,512,128]{2,1,0:T(8,128)(2,1)S(1)}, u32[]{:S(2)}, u32[]{:S(2)}) %collective-permute-start.58) | collective-permute-done | bytes 262176 | tf_op jit(solution)/shard_map/ppermute | solution.py:21
  243.8 1.5 collective-permute-start.49
  245.6 10.1 %collective-permute-done.47 = bf16[2,512,128]{2,1,0:T(8,128)(2,1)S(1)} collective-permute-done((bf16[2,512,128]{2,1,0:T(8,128)(2,1)S(1)}, bf16[2,512,128]{2,1,0:T(8,128)(2,1)S(1)}, u32[]{:S(2)}, u32[]{:S(2)}) %collective-permute-start.47) | collective-permute-done | bytes 262176 | tf_op jit(solution)/shard_map/ppermute | solution.py:21
  255.7 1.6 collective-permute-start.52
  257.2 4.1 %collective-permute-done.49 = bf16[2,512,128]{2,1,0:T(8,128)(2,1)S(1)} collective-permute-done((bf16[2,512,128]{2,1,0:T(8,128)(2,1)S(1)}, bf16[2,512,128]{2,1,0:T(8,128)(2,1)S(1)}, u32[]{:S(2)}, u32[]{:S(2)}) %collective-permute-start.49) | collective-permute-done | bytes 262176 | tf_op jit(solution)/shard_map/ppermute | solution.py:21
  262.9 1.8 collective-permute-done.52
  265.8 5.0 %collective-permute-done.50 = bf16[2,512,128]{2,1,0:T(8,128)(2,1)S(1)} collective-permute-done((bf16[2,512,128]{2,1,0:T(8,128)(2,1)S(1)}, bf16[2,512,128]{2,1,0:T(8,128)(2,1)S(1)}, u32[]{:S(2)}, u32[]{:S(2)}) %collective-permute-start.50) | collective-permute-done | bytes 262176 | tf_op jit(solution)/shard_map/ppermute | solution.py:21
  272.1 1.5 collective-permute-done.61
  (109 shorter events, 25.4 us)
Async XLA Ops:
  0.0 112.2 %collective-permute-start.5 = (bf16[8,256,1024]{2,1,0:T(8,128)(2,1)}, bf16[8,256,1024]{2,1,0:T(8,128)(2,1)}, u32[]{:S(2)}, u32[]{:S(2)}) collective-permute-start(bf16[8,256,1024]{2,1,0:T(8,128)(2,1)} %refs_4_.7), channel_id=1, source_target_pairs={{0,1},{1,0},{2,3},{3,2},{4,5},{5,4},{6,7},{7,6},{8,9},{9,8},{10,11... | collective-permute-start | bytes 12582920 | tf_op jit(solution)/shard_map/ppermute | solution.py:21
  0.5 10.6 %collective-permute-start = (bf16[8,256,128]{2,1,0:T(8,128)(2,1)}, bf16[8,256,128]{2,1,0:T(8,128)(2,1)}, u32[]{:S(2)}, u32[]{:S(2)}) collective-permute-start(bf16[8,256,128]{2,1,0:T(8,128)(2,1)} %param.9), channel_id=1, source_target_pairs={{0,1},{1,0},{2,3},{3,2},{4,5},{5,4},{6,7},{7,6},{8,9},{9,8},{10,11... | collective-permute-start | bytes 1572872 | tf_op jit(solution)/shard_map/ppermute | solution.py:21
  4.3 27.7 %collective-permute-start.35 = (bf16[512,512]{1,0:T(8,128)(2,1)}, bf16[512,512]{1,0:T(8,128)(2,1)S(1)}, u32[]{:S(2)}, u32[]{:S(2)}) collective-permute-start(bf16[512,512]{1,0:T(8,128)(2,1)} %get-tuple-element.42), channel_id=1, source_target_pairs={{0,16},{8,24},{16,0},{24,8},{1,17},{9,25},{17,1},{25,9},{2,18},{10... | collective-permute-start | bytes 1572872 | tf_op jit(solution)/shard_map/ppermute | solution.py:21
  8.4 25.2 %collective-permute-start.34 = (bf16[512,512]{1,0:T(8,128)(2,1)S(1)}, bf16[512,512]{1,0:T(8,128)(2,1)S(1)}, u32[]{:S(2)}, u32[]{:S(2)}) collective-permute-start(bf16[512,512]{1,0:T(8,128)(2,1)S(1)} %get-tuple-element.41.refs_1_.refs_13_), channel_id=1, source_target_pairs={{0,8},{8,0},{16,24},{24,16},{1,9},{9,1},{17,25},{25,17},{2,10},{10... | collective-permute-start | bytes 1572872 | tf_op jit(solution)/shard_map/ppermute | solution.py:21
  9.9 27.3 %collective-permute-start.37 = (bf16[512,512]{1,0:T(8,128)(2,1)S(1)}, bf16[512,512]{1,0:T(8,128)(2,1)S(1)}, u32[]{:S(2)}, u32[]{:S(2)}) collective-permute-start(bf16[512,512]{1,0:T(8,128)(2,1)S(1)} %get-tuple-element.41.refs_1_.refs_13_), channel_id=1, source_target_pairs={{0,1},{1,0},{2,3},{3,2},{4,5},{5,4},{6,7},{7,6},{8,9},{9,8},{10,11... | collective-permute-start | bytes 1572872 | tf_op jit(solution)/shard_map/ppermute | solution.py:21
  9.9 102.7 %copy-start = (bf16[8,256,1024]{2,1,0:T(8,128)(2,1)S(1)}, bf16[8,256,1024]{2,1,0:T(8,128)(2,1)}, u32[]{:S(2)}) copy-start(bf16[8,256,1024]{2,1,0:T(8,128)(2,1)} %refs_4_.7) | copy-start | bytes 12582916
  12.3 25.0 %collective-permute-start.15 = (bf16[2,512,128]{2,1,0:T(8,128)(2,1)S(1)}, bf16[2,512,128]{2,1,0:T(8,128)(2,1)S(1)}, u32[]{:S(2)}, u32[]{:S(2)}) collective-permute-start(bf16[2,512,128]{2,1,0:T(8,128)(2,1)S(1)} %pad_maximum_fusion.2.refs_0_), channel_id=1, source_target_pairs={{0,2},{1,3},{2,0},{3,1},{4,6},{5,7},{6,4},{7,5},{8,10},{9,11},{10,... | collective-permute-start | bytes 786440 | tf_op jit(solution)/shard_map/ppermute | solution.py:21
  32.0 7.8 %collective-permute-start.16 = (bf16[2,512,128]{2,1,0:T(8,128)(2,1)S(1)}, bf16[2,512,128]{2,1,0:T(8,128)(2,1)S(1)}, u32[]{:S(2)}, u32[]{:S(2)}) collective-permute-start(bf16[2,512,128]{2,1,0:T(8,128)(2,1)S(1)} %pad_maximum_fusion.2.refs_0_), channel_id=1, source_target_pairs={{0,4},{1,5},{2,6},{3,7},{4,0},{5,1},{6,2},{7,3},{8,12},{9,13},{10,... | collective-permute-start | bytes 786440 | tf_op jit(solution)/shard_map/ppermute | solution.py:21
  33.6 30.0 %collective-permute-start.4 = (bf16[256,2048]{1,0:T(8,128)(2,1)}, bf16[256,2048]{1,0:T(8,128)(2,1)S(1)}, u32[]{:S(2)}, u32[]{:S(2)}) collective-permute-start(bf16[256,2048]{1,0:T(8,128)(2,1)} %refs_4_.6), channel_id=1, source_target_pairs={{0,1},{1,0},{2,3},{3,2},{4,5},{5,4},{6,7},{7,6},{8,9},{9,8},{10,11... | collective-permute-start | bytes 3145736 | tf_op jit(solution)/shard_map/ppermute | solution.py:21
  37.3 49.1 %collective-permute-start.28 = (bf16[1024,512]{1,0:T(8,128)(2,1)S(1)}, bf16[1024,512]{1,0:T(8,128)(2,1)S(1)}, u32[]{:S(2)}, u32[]{:S(2)}) collective-permute-start(bf16[1024,512]{1,0:T(8,128)(2,1)S(1)} %get-tuple-element.40), channel_id=1, source_target_pairs={{0,16},{8,24},{16,0},{24,8},{1,17},{9,25},{17,1},{25,9},{2,18},{10... | collective-permute-start | bytes 3145736 | tf_op jit(solution)/shard_map/ppermute | solution.py:21
  37.4 10.1 %collective-permute-start.17 = (bf16[2,512,128]{2,1,0:T(8,128)(2,1)S(1)}, bf16[2,512,128]{2,1,0:T(8,128)(2,1)S(1)}, u32[]{:S(2)}, u32[]{:S(2)}) collective-permute-start(bf16[2,512,128]{2,1,0:T(8,128)(2,1)S(1)} %pad_maximum_fusion.2.refs_0_), channel_id=1, source_target_pairs={{0,6},{1,7},{2,4},{3,5},{4,2},{5,3},{6,0},{7,1},{8,14},{9,15},{10,... | collective-permute-start | bytes 786440 | tf_op jit(solution)/shard_map/ppermute | solution.py:21
  39.8 12.5 %collective-permute-start.1 = (bf16[2,512,128]{2,1,0:T(8,128)(2,1)S(1)}, bf16[2,512,128]{2,1,0:T(8,128)(2,1)S(1)}, u32[]{:S(2)}, u32[]{:S(2)}) collective-permute-start(bf16[2,512,128]{2,1,0:T(8,128)(2,1)S(1)} %pad_maximum_fusion.1.refs_0_), channel_id=1, source_target_pairs={{0,2},{1,3},{2,0},{3,1},{4,6},{5,7},{6,4},{7,5},{8,10},{9,11},{10,... | collective-permute-start | bytes 786440 | tf_op jit(solution)/shard_map/ppermute | solution.py:21
  47.5 7.8 %collective-permute-start.2 = (bf16[2,512,128]{2,1,0:T(8,128)(2,1)S(1)}, bf16[2,512,128]{2,1,0:T(8,128)(2,1)S(1)}, u32[]{:S(2)}, u32[]{:S(2)}) collective-permute-start(bf16[2,512,128]{2,1,0:T(8,128)(2,1)S(1)} %pad_maximum_fusion.1.refs_0_), channel_id=1, source_target_pairs={{0,4},{1,5},{2,6},{3,7},{4,0},{5,1},{6,2},{7,3},{8,12},{9,13},{10,... | collective-permute-start | bytes 786440 | tf_op jit(solution)/shard_map/ppermute | solution.py:21
  52.4 48.6 %collective-permute-start.27 = (bf16[1024,512]{1,0:T(8,128)(2,1)S(1)}, bf16[1024,512]{1,0:T(8,128)(2,1)S(1)}, u32[]{:S(2)}, u32[]{:S(2)}) collective-permute-start(bf16[1024,512]{1,0:T(8,128)(2,1)S(1)} %get-tuple-element.39.refs_9_.refs_5_), channel_id=1, source_target_pairs={{0,8},{8,0},{16,24},{24,16},{1,9},{9,1},{17,25},{25,17},{2,10},{10... | collective-permute-start | bytes 3145736 | tf_op jit(solution)/shard_map/ppermute | solution.py:21
  55.3 8.2 %collective-permute-start.3 = (bf16[2,512,128]{2,1,0:T(8,128)(2,1)S(1)}, bf16[2,512,128]{2,1,0:T(8,128)(2,1)S(1)}, u32[]{:S(2)}, u32[]{:S(2)}) collective-permute-start(bf16[2,512,128]{2,1,0:T(8,128)(2,1)S(1)} %pad_maximum_fusion.1.refs_0_), channel_id=1, source_target_pairs={{0,6},{1,7},{2,4},{3,5},{4,2},{5,3},{6,0},{7,1},{8,14},{9,15},{10,... | collective-permute-start | bytes 786440 | tf_op jit(solution)/shard_map/ppermute | solution.py:21
  63.5 53.6 %collective-permute-start.30 = (bf16[1024,512]{1,0:T(8,128)(2,1)S(1)}, bf16[1024,512]{1,0:T(8,128)(2,1)S(1)}, u32[]{:S(2)}, u32[]{:S(2)}) collective-permute-start(bf16[1024,512]{1,0:T(8,128)(2,1)S(1)} %get-tuple-element.39.refs_9_.refs_5_), channel_id=1, source_target_pairs={{0,1},{1,0},{2,3},{3,2},{4,5},{5,4},{6,7},{7,6},{8,9},{9,8},{10,11... | collective-permute-start | bytes 3145736 | tf_op jit(solution)/shard_map/ppermute | solution.py:21
  63.5 48.6 %collective-permute-start.36 = (bf16[512,512]{1,0:T(8,128)(2,1)S(1)}, bf16[512,512]{1,0:T(8,128)(2,1)S(1)}, u32[]{:S(2)}, u32[]{:S(2)}) collective-permute-start(bf16[512,512]{1,0:T(8,128)(2,1)S(1)} %collective-permute-done.35.refs_3_.refs_15_), channel_id=1, source_target_pairs={{0,8},{8,0},{16,24},{24,16},{1,9},{9,1},{17,25},{25,17},{2,10},{10... | collective-permute-start | bytes 1572872 | tf_op jit(solution)/shard_map/ppermute | solution.py:21
  86.4 46.9 %collective-permute-start.29 = (bf16[1024,512]{1,0:T(8,128)(2,1)S(1)}, bf16[1024,512]{1,0:T(8,128)(2,1)S(1)}, u32[]{:S(2)}, u32[]{:S(2)}) collective-permute-start(bf16[1024,512]{1,0:T(8,128)(2,1)S(1)} %collective-permute-done.28.refs_11_.refs_7_), channel_id=1, source_target_pairs={{0,8},{8,0},{16,24},{24,16},{1,9},{9,1},{17,25},{25,17},{2,10},{10... | collective-permute-start | bytes 3145736 | tf_op jit(solution)/shard_map/ppermute | solution.py:21
  100.9 18.8 %collective-permute-start.38 = (bf16[512,512]{1,0:T(8,128)(2,1)S(1)}, bf16[512,512]{1,0:T(8,128)(2,1)S(1)}, u32[]{:S(2)}, u32[]{:S(2)}) collective-permute-start(bf16[512,512]{1,0:T(8,128)(2,1)S(1)} %collective-permute-done.34.refs_2_.refs_14_), channel_id=1, source_target_pairs={{0,1},{1,0},{2,3},{3,2},{4,5},{5,4},{6,7},{7,6},{8,9},{9,8},{10,11... | collective-permute-start | bytes 1572872 | tf_op jit(solution)/shard_map/ppermute | solution.py:21
  112.2 8.0 %collective-permute-start.39 = (bf16[512,512]{1,0:T(8,128)(2,1)S(1)}, bf16[512,512]{1,0:T(8,128)(2,1)S(1)}, u32[]{:S(2)}, u32[]{:S(2)}) collective-permute-start(bf16[512,512]{1,0:T(8,128)(2,1)S(1)} %collective-permute-done.35.refs_3_.refs_15_), channel_id=1, source_target_pairs={{0,1},{1,0},{2,3},{3,2},{4,5},{5,4},{6,7},{7,6},{8,9},{9,8},{10,11... | collective-permute-start | bytes 1572872 | tf_op jit(solution)/shard_map/ppermute | solution.py:21
  112.2 8.0 %collective-permute-start.40 = (bf16[512,512]{1,0:T(8,128)(2,1)S(1)}, bf16[512,512]{1,0:T(8,128)(2,1)S(1)}, u32[]{:S(2)}, u32[]{:S(2)}) collective-permute-start(bf16[512,512]{1,0:T(8,128)(2,1)S(1)} %collective-permute-done.36.refs_4_.refs_16_), channel_id=1, source_target_pairs={{0,1},{1,0},{2,3},{3,2},{4,5},{5,4},{6,7},{7,6},{8,9},{9,8},{10,11... | collective-permute-start | bytes 1572872 | tf_op jit(solution)/shard_map/ppermute | solution.py:21
  117.2 18.6 %collective-permute-start.18 = (f32[64,1024]{1,0:T(8,128)S(1)}, f32[64,1024]{1,0:T(8,128)S(1)}, u32[]{:S(2)}, u32[]{:S(2)}) collective-permute-start(f32[64,1024]{1,0:T(8,128)S(1)} %get-tuple-element.35), channel_id=1, source_target_pairs={{0,6},{1,7},{2,4},{3,5},{4,2},{5,3},{6,0},{7,1},{8,14},{9,15},{10,... | collective-permute-start | bytes 786440 | tf_op jit(solution)/shard_map/ppermute | solution.py:21
  119.7 16.1 %collective-permute-start.19 = (f32[64,1024]{1,0:T(8,128)S(1)}, f32[64,1024]{1,0:T(8,128)S(1)}, u32[]{:S(2)}, u32[]{:S(2)}) collective-permute-start(f32[64,1024]{1,0:T(8,128)S(1)} %get-tuple-element.36), channel_id=1, source_target_pairs={{0,4},{1,5},{2,6},{3,7},{4,0},{5,1},{6,2},{7,3},{8,12},{9,13},{10,... | collective-permute-start | bytes 786440 | tf_op jit(solution)/shard_map/ppermute | solution.py:21
  120.2 50.9 %collective-permute-start.31 = (bf16[1024,512]{1,0:T(8,128)(2,1)S(1)}, bf16[1024,512]{1,0:T(8,128)(2,1)S(1)}, u32[]{:S(2)}, u32[]{:S(2)}) collective-permute-start(bf16[1024,512]{1,0:T(8,128)(2,1)S(1)} %collective-permute-done.27.refs_10_.refs_6_), channel_id=1, source_target_pairs={{0,1},{1,0},{2,3},{3,2},{4,5},{5,4},{6,7},{7,6},{8,9},{9,8},{10,11... | collective-permute-start | bytes 3145736 | tf_op jit(solution)/shard_map/ppermute | solution.py:21
  120.2 16.1 %collective-permute-start.20 = (f32[64,1024]{1,0:T(8,128)S(1)}, f32[64,1024]{1,0:T(8,128)S(1)}, u32[]{:S(2)}, u32[]{:S(2)}) collective-permute-start(f32[64,1024]{1,0:T(8,128)S(1)} %get-tuple-element.37), channel_id=1, source_target_pairs={{0,2},{1,3},{2,0},{3,1},{4,6},{5,7},{6,4},{7,5},{8,10},{9,11},{10,... | collective-permute-start | bytes 786440 | tf_op jit(solution)/shard_map/ppermute | solution.py:21
  133.3 8.0 %collective-permute-start.6 = (f32[64,1024]{1,0:T(8,128)S(1)}, f32[64,1024]{1,0:T(8,128)S(1)}, u32[]{:S(2)}, u32[]{:S(2)}) collective-permute-start(f32[64,1024]{1,0:T(8,128)S(1)} %get-tuple-element.31), channel_id=1, source_target_pairs={{0,6},{1,7},{2,4},{3,5},{4,2},{5,3},{6,0},{7,1},{8,14},{9,15},{10,... | collective-permute-start | bytes 786440 | tf_op jit(solution)/shard_map/ppermute | solution.py:21
  135.8 36.7 %collective-permute-start.32 = (bf16[1024,512]{1,0:T(8,128)(2,1)S(1)}, bf16[1024,512]{1,0:T(8,128)(2,1)S(1)}, u32[]{:S(2)}, u32[]{:S(2)}) collective-permute-start(bf16[1024,512]{1,0:T(8,128)(2,1)S(1)} %collective-permute-done.28.refs_11_.refs_7_), channel_id=1, source_target_pairs={{0,1},{1,0},{2,3},{3,2},{4,5},{5,4},{6,7},{7,6},{8,9},{9,8},{10,11... | collective-permute-start | bytes 3145736 | tf_op jit(solution)/shard_map/ppermute | solution.py:21
  135.8 37.4 %collective-permute-start.33 = (bf16[1024,512]{1,0:T(8,128)(2,1)S(1)}, bf16[1024,512]{1,0:T(8,128)(2,1)S(1)}, u32[]{:S(2)}, u32[]{:S(2)}) collective-permute-start(bf16[1024,512]{1,0:T(8,128)(2,1)S(1)} %collective-permute-done.29.refs_12_.refs_8_), channel_id=1, source_target_pairs={{0,1},{1,0},{2,3},{3,2},{4,5},{5,4},{6,7},{7,6},{8,9},{9,8},{10,11... | collective-permute-start | bytes 3145736 | tf_op jit(solution)/shard_map/ppermute | solution.py:21
  136.3 10.6 %collective-permute-start.7 = (f32[64,1024]{1,0:T(8,128)S(1)}, f32[64,1024]{1,0:T(8,128)S(1)}, u32[]{:S(2)}, u32[]{:S(2)}) collective-permute-start(f32[64,1024]{1,0:T(8,128)S(1)} %get-tuple-element.32), channel_id=1, source_target_pairs={{0,4},{1,5},{2,6},{3,7},{4,0},{5,1},{6,2},{7,3},{8,12},{9,13},{10,... | collective-permute-start | bytes 786440 | tf_op jit(solution)/shard_map/ppermute | solution.py:21
  141.3 7.0 %collective-permute-start.8 = (f32[64,1024]{1,0:T(8,128)S(1)}, f32[64,1024]{1,0:T(8,128)S(1)}, u32[]{:S(2)}, u32[]{:S(2)}) collective-permute-start(f32[64,1024]{1,0:T(8,128)S(1)} %get-tuple-element.33), channel_id=1, source_target_pairs={{0,2},{1,3},{2,0},{3,1},{4,6},{5,7},{6,4},{7,5},{8,10},{9,11},{10,... | collective-permute-start | bytes 786440 | tf_op jit(solution)/shard_map/ppermute | solution.py:21
  146.8 5.4 %collective-permute-start.21 = (bf16[64,1024]{1,0:T(8,128)(2,1)S(1)}, bf16[64,1024]{1,0:T(8,128)(2,1)S(1)}, u32[]{:S(2)}, u32[]{:S(2)}) collective-permute-start(bf16[64,1024]{1,0:T(8,128)(2,1)S(1)} %softmax.3.refs_0_), channel_id=1, source_target_pairs={{0,2},{1,3},{2,0},{3,1},{4,6},{5,7},{6,4},{7,5},{8,10},{9,11},{10,... | collective-permute-start | bytes 393224 | tf_op jit(solution)/shard_map/ppermute | solution.py:21
  148.3 7.2 %collective-permute-start.22 = (bf16[64,1024]{1,0:T(8,128)(2,1)S(1)}, bf16[64,1024]{1,0:T(8,128)(2,1)S(1)}, u32[]{:S(2)}, u32[]{:S(2)}) collective-permute-start(bf16[64,1024]{1,0:T(8,128)(2,1)S(1)} %softmax.3.refs_0_), channel_id=1, source_target_pairs={{0,4},{1,5},{2,6},{3,7},{4,0},{5,1},{6,2},{7,3},{8,12},{9,13},{10,... | collective-permute-start | bytes 393224 | tf_op jit(solution)/shard_map/ppermute | solution.py:21
  152.3 6.0 %collective-permute-start.23 = (bf16[64,1024]{1,0:T(8,128)(2,1)S(1)}, bf16[64,1024]{1,0:T(8,128)(2,1)S(1)}, u32[]{:S(2)}, u32[]{:S(2)}) collective-permute-start(bf16[64,1024]{1,0:T(8,128)(2,1)S(1)} %softmax.3.refs_0_), channel_id=1, source_target_pairs={{0,6},{1,7},{2,4},{3,5},{4,2},{5,3},{6,0},{7,1},{8,14},{9,15},{10,... | collective-permute-start | bytes 393224 | tf_op jit(solution)/shard_map/ppermute | solution.py:21
  155.5 6.8 %collective-permute-start.10 = (bf16[64,1024]{1,0:T(8,128)(2,1)S(1)}, bf16[64,1024]{1,0:T(8,128)(2,1)S(1)}, u32[]{:S(2)}, u32[]{:S(2)}) collective-permute-start(bf16[64,1024]{1,0:T(8,128)(2,1)S(1)} %softmax.2.refs_0_), channel_id=1, source_target_pairs={{0,4},{1,5},{2,6},{3,7},{4,0},{5,1},{6,2},{7,3},{8,12},{9,13},{10,... | collective-permute-start | bytes 393224 | tf_op jit(solution)/shard_map/ppermute | solution.py:21
  158.2 8.0 %collective-permute-start.11 = (bf16[64,1024]{1,0:T(8,128)(2,1)S(1)}, bf16[64,1024]{1,0:T(8,128)(2,1)S(1)}, u32[]{:S(2)}, u32[]{:S(2)}) collective-permute-start(bf16[64,1024]{1,0:T(8,128)(2,1)S(1)} %softmax.2.refs_0_), channel_id=1, source_target_pairs={{0,6},{1,7},{2,4},{3,5},{4,2},{5,3},{6,0},{7,1},{8,14},{9,15},{10,... | collective-permute-start | bytes 393224 | tf_op jit(solution)/shard_map/ppermute | solution.py:21
  162.3 5.4 %collective-permute-start.9 = (bf16[64,1024]{1,0:T(8,128)(2,1)S(1)}, bf16[64,1024]{1,0:T(8,128)(2,1)S(1)}, u32[]{:S(2)}, u32[]{:S(2)}) collective-permute-start(bf16[64,1024]{1,0:T(8,128)(2,1)S(1)} %softmax.2.refs_0_), channel_id=1, source_target_pairs={{0,2},{1,3},{2,0},{3,1},{4,6},{5,7},{6,4},{7,5},{8,10},{9,11},{10,... | collective-permute-start | bytes 393224 | tf_op jit(solution)/shard_map/ppermute | solution.py:21
  166.2 7.8 %collective-permute-start.25 = (bf16[2,512,128]{2,1,0:T(8,128)(2,1)S(1)}, bf16[2,512,128]{2,1,0:T(8,128)(2,1)S(1)}, u32[]{:S(2)}, u32[]{:S(2)}) collective-permute-start(bf16[2,512,128]{2,1,0:T(8,128)(2,1)S(1)} %pool.3.refs_4_), channel_id=1, source_target_pairs={{0,4},{1,5},{2,6},{3,7},{4,0},{5,1},{6,2},{7,3},{8,12},{9,13},{10,... | collective-permute-start | bytes 786440 | tf_op jit(solution)/shard_map/ppermute | solution.py:21
  167.8 9.2 %collective-permute-start.24 = (bf16[2,512,128]{2,1,0:T(8,128)(2,1)S(1)}, bf16[2,512,128]{2,1,0:T(8,128)(2,1)S(1)}, u32[]{:S(2)}, u32[]{:S(2)}) collective-permute-start(bf16[2,512,128]{2,1,0:T(8,128)(2,1)S(1)} %pool.3.refs_4_), channel_id=1, source_target_pairs={{0,2},{1,3},{2,0},{3,1},{4,6},{5,7},{6,4},{7,5},{8,10},{9,11},{10,... | collective-permute-start | bytes 786440 | tf_op jit(solution)/shard_map/ppermute | solution.py:21
  171.1 11.5 %collective-permute-start.12 = (bf16[2,512,128]{2,1,0:T(8,128)(2,1)S(1)}, bf16[2,512,128]{2,1,0:T(8,128)(2,1)S(1)}, u32[]{:S(2)}, u32[]{:S(2)}) collective-permute-start(bf16[2,512,128]{2,1,0:T(8,128)(2,1)S(1)} %pool.2.refs_0_), channel_id=1, source_target_pairs={{0,2},{1,3},{2,0},{3,1},{4,6},{5,7},{6,4},{7,5},{8,10},{9,11},{10,... | collective-permute-start | bytes 786440 | tf_op jit(solution)/shard_map/ppermute | solution.py:21
  172.5 19.0 %collective-permute-start.53 = (bf16[2,512,128]{2,1,0:T(8,128)(2,1)S(1)}, bf16[2,512,128]{2,1,0:T(8,128)(2,1)S(1)}, u32[]{:S(2)}, u32[]{:S(2)}) collective-permute-start(bf16[2,512,128]{2,1,0:T(8,128)(2,1)S(1)} %pool.3.refs_4_), channel_id=1, source_target_pairs={{0,16},{8,24},{16,0},{24,8},{1,17},{9,25},{17,1},{25,9},{2,18},{10... | collective-permute-start | bytes 786440 | tf_op jit(solution)/shard_map/ppermute | solution.py:21
  173.2 18.9 %collective-permute-start.13 = (bf16[2,512,128]{2,1,0:T(8,128)(2,1)S(1)}, bf16[2,512,128]{2,1,0:T(8,128)(2,1)S(1)}, u32[]{:S(2)}, u32[]{:S(2)}) collective-permute-start(bf16[2,512,128]{2,1,0:T(8,128)(2,1)S(1)} %pool.2.refs_0_), channel_id=1, source_target_pairs={{0,4},{1,5},{2,6},{3,7},{4,0},{5,1},{6,2},{7,3},{8,12},{9,13},{10,... | collective-permute-start | bytes 786440 | tf_op jit(solution)/shard_map/ppermute | solution.py:21
  174.0 23.0 %collective-permute-start.43 = (bf16[2,512,128]{2,1,0:T(8,128)(2,1)S(1)}, bf16[2,512,128]{2,1,0:T(8,128)(2,1)S(1)}, u32[]{:S(2)}, u32[]{:S(2)}) collective-permute-start(bf16[2,512,128]{2,1,0:T(8,128)(2,1)S(1)} %pool.2.refs_0_), channel_id=1, source_target_pairs={{0,16},{8,24},{16,0},{24,8},{1,17},{9,25},{17,1},{25,9},{2,18},{10... | collective-permute-start | bytes 786440 | tf_op jit(solution)/shard_map/ppermute | solution.py:21
  177.0 21.4 %collective-permute-start.26 = (bf16[2,512,128]{2,1,0:T(8,128)(2,1)S(1)}, bf16[2,512,128]{2,1,0:T(8,128)(2,1)S(1)}, u32[]{:S(2)}, u32[]{:S(2)}) collective-permute-start(bf16[2,512,128]{2,1,0:T(8,128)(2,1)S(1)} %collective-permute-done.25.refs_6_), channel_id=1, source_target_pairs={{0,2},{1,3},{2,0},{3,1},{4,6},{5,7},{6,4},{7,5},{8,10},{9,11},{10,... | collective-permute-start | bytes 786440 | tf_op jit(solution)/shard_map/ppermute | solution.py:21
  182.6 16.4 %collective-permute-start.14 = (bf16[2,512,128]{2,1,0:T(8,128)(2,1)S(1)}, bf16[2,512,128]{2,1,0:T(8,128)(2,1)S(1)}, u32[]{:S(2)}, u32[]{:S(2)}) collective-permute-start(bf16[2,512,128]{2,1,0:T(8,128)(2,1)S(1)} %collective-permute-done.12.refs_1_), channel_id=1, source_target_pairs={{0,4},{1,5},{2,6},{3,7},{4,0},{5,1},{6,2},{7,3},{8,12},{9,13},{10,... | collective-permute-start | bytes 786440 | tf_op jit(solution)/shard_map/ppermute | solution.py:21
  191.5 21.9 %collective-permute-start.54 = (bf16[2,512,128]{2,1,0:T(8,128)(2,1)S(1)}, bf16[2,512,128]{2,1,0:T(8,128)(2,1)S(1)}, u32[]{:S(2)}, u32[]{:S(2)}) collective-permute-start(bf16[2,512,128]{2,1,0:T(8,128)(2,1)S(1)} %collective-permute-done.53.refs_0_), channel_id=1, source_target_pairs={{0,2},{1,3},{2,0},{3,1},{4,6},{5,7},{6,4},{7,5},{8,10},{9,11},{10,... | collective-permute-start | bytes 786440 | tf_op jit(solution)/shard_map/ppermute | solution.py:21
  192.0 22.0 %collective-permute-start.55 = (bf16[2,512,128]{2,1,0:T(8,128)(2,1)S(1)}, bf16[2,512,128]{2,1,0:T(8,128)(2,1)S(1)}, u32[]{:S(2)}, u32[]{:S(2)}) collective-permute-start(bf16[2,512,128]{2,1,0:T(8,128)(2,1)S(1)} %collective-permute-done.53.refs_0_), channel_id=1, source_target_pairs={{0,4},{1,5},{2,6},{3,7},{4,0},{5,1},{6,2},{7,3},{8,12},{9,13},{10,... | collective-permute-start | bytes 786440 | tf_op jit(solution)/shard_map/ppermute | solution.py:21
  197.0 18.5 %collective-permute-start.56 = (bf16[2,512,128]{2,1,0:T(8,128)(2,1)S(1)}, bf16[2,512,128]{2,1,0:T(8,128)(2,1)S(1)}, u32[]{:S(2)}, u32[]{:S(2)}) collective-permute-start(bf16[2,512,128]{2,1,0:T(8,128)(2,1)S(1)} %collective-permute-done.53.refs_0_), channel_id=1, source_target_pairs={{0,6},{1,7},{2,4},{3,5},{4,2},{5,3},{6,0},{7,1},{8,14},{9,15},{10,... | collective-permute-start | bytes 786440 | tf_op jit(solution)/shard_map/ppermute | solution.py:21
  198.4 26.2 %collective-permute-start.44 = (bf16[2,512,128]{2,1,0:T(8,128)(2,1)S(1)}, bf16[2,512,128]{2,1,0:T(8,128)(2,1)S(1)}, u32[]{:S(2)}, u32[]{:S(2)}) collective-permute-start(bf16[2,512,128]{2,1,0:T(8,128)(2,1)S(1)} %collective-permute-done.43.refs_0_), channel_id=1, source_target_pairs={{0,2},{1,3},{2,0},{3,1},{4,6},{5,7},{6,4},{7,5},{8,10},{9,11},{10,... | collective-permute-start | bytes 786440 | tf_op jit(solution)/shard_map/ppermute | solution.py:21
  199.0 27.2 %collective-permute-start.45 = (bf16[2,512,128]{2,1,0:T(8,128)(2,1)S(1)}, bf16[2,512,128]{2,1,0:T(8,128)(2,1)S(1)}, u32[]{:S(2)}, u32[]{:S(2)}) collective-permute-start(bf16[2,512,128]{2,1,0:T(8,128)(2,1)S(1)} %collective-permute-done.43.refs_0_), channel_id=1, source_target_pairs={{0,4},{1,5},{2,6},{3,7},{4,0},{5,1},{6,2},{7,3},{8,12},{9,13},{10,... | collective-permute-start | bytes 786440 | tf_op jit(solution)/shard_map/ppermute | solution.py:21
  213.4 48.2 %copy-start.5 = (bf16[2,2,512,128]{3,2,1,0:T(8,128)(2,1)}, bf16[2,2,512,128]{3,2,1,0:T(8,128)(2,1)S(1)}, u32[]{:S(2)}) copy-start(bf16[2,2,512,128]{3,2,1,0:T(8,128)(2,1)S(1)} %get-tuple-element.43) | copy-start | bytes 1572868
  213.4 32.1 %collective-permute-start.51 = (bf16[2,2,512,128]{3,2,1,0:T(8,128)(2,1)S(1)}, bf16[2,2,512,128]{3,2,1,0:T(8,128)(2,1)S(1)}, u32[]{:S(2)}, u32[]{:S(2)}) collective-permute-start(bf16[2,2,512,128]{3,2,1,0:T(8,128)(2,1)S(1)} %get-tuple-element.50), channel_id=1, source_target_pairs={{0,4},{1,5},{2,6},{3,7},{4,0},{5,1},{6,2},{7,3},{8,12},{9,13},{10,... | collective-permute-start | bytes 1572872 | tf_op jit(solution)/shard_map/ppermute | solution.py:21
  214.0 12.7 %collective-permute-start.46 = (bf16[2,512,128]{2,1,0:T(8,128)(2,1)S(1)}, bf16[2,512,128]{2,1,0:T(8,128)(2,1)S(1)}, u32[]{:S(2)}, u32[]{:S(2)}) collective-permute-start(bf16[2,512,128]{2,1,0:T(8,128)(2,1)S(1)} %collective-permute-done.43.refs_0_), channel_id=1, source_target_pairs={{0,6},{1,7},{2,4},{3,5},{4,2},{5,3},{6,0},{7,1},{8,14},{9,15},{10,... | collective-permute-start | bytes 786440 | tf_op jit(solution)/shard_map/ppermute | solution.py:21
  223.1 13.7 %collective-permute-start.57 = (bf16[2,512,128]{2,1,0:T(8,128)(2,1)S(1)}, bf16[2,512,128]{2,1,0:T(8,128)(2,1)S(1)}, u32[]{:S(2)}, u32[]{:S(2)}) collective-permute-start(bf16[2,512,128]{2,1,0:T(8,128)(2,1)S(1)} %get-tuple-element.52), channel_id=1, source_target_pairs={{0,6},{1,7},{2,4},{3,5},{4,2},{5,3},{6,0},{7,1},{8,14},{9,15},{10,... | collective-permute-start | bytes 786440 | tf_op jit(solution)/shard_map/ppermute | solution.py:21
  224.6 18.7 %collective-permute-start.58 = (bf16[2,512,128]{2,1,0:T(8,128)(2,1)S(1)}, bf16[2,512,128]{2,1,0:T(8,128)(2,1)S(1)}, u32[]{:S(2)}, u32[]{:S(2)}) collective-permute-start(bf16[2,512,128]{2,1,0:T(8,128)(2,1)S(1)} %get-tuple-element.53), channel_id=1, source_target_pairs={{0,4},{1,5},{2,6},{3,7},{4,0},{5,1},{6,2},{7,3},{8,12},{9,13},{10,... | collective-permute-start | bytes 786440 | tf_op jit(solution)/shard_map/ppermute | solution.py:21
  226.1 17.7 %collective-permute-start.59 = (bf16[2,512,128]{2,1,0:T(8,128)(2,1)S(1)}, bf16[2,512,128]{2,1,0:T(8,128)(2,1)S(1)}, u32[]{:S(2)}, u32[]{:S(2)}) collective-permute-start(bf16[2,512,128]{2,1,0:T(8,128)(2,1)S(1)} %get-tuple-element.54), channel_id=1, source_target_pairs={{0,2},{1,3},{2,0},{3,1},{4,6},{5,7},{6,4},{7,5},{8,10},{9,11},{10,... | collective-permute-start | bytes 786440 | tf_op jit(solution)/shard_map/ppermute | solution.py:21
  226.6 34.9 %collective-permute-start.41 = (bf16[2,2,512,128]{3,2,1,0:T(8,128)(2,1)S(1)}, bf16[2,2,512,128]{3,2,1,0:T(8,128)(2,1)S(1)}, u32[]{:S(2)}, u32[]{:S(2)}) collective-permute-start(bf16[2,2,512,128]{3,2,1,0:T(8,128)(2,1)S(1)} %get-tuple-element.44), channel_id=1, source_target_pairs={{0,2},{1,3},{2,0},{3,1},{4,6},{5,7},{6,4},{7,5},{8,10},{9,11},{10,... | collective-permute-start | bytes 1572872 | tf_op jit(solution)/shard_map/ppermute | solution.py:21
  236.8 18.9 %collective-permute-start.47 = (bf16[2,512,128]{2,1,0:T(8,128)(2,1)S(1)}, bf16[2,512,128]{2,1,0:T(8,128)(2,1)S(1)}, u32[]{:S(2)}, u32[]{:S(2)}) collective-permute-start(bf16[2,512,128]{2,1,0:T(8,128)(2,1)S(1)} %get-tuple-element.46), channel_id=1, source_target_pairs={{0,6},{1,7},{2,4},{3,5},{4,2},{5,3},{6,0},{7,1},{8,14},{9,15},{10,... | collective-permute-start | bytes 786440 | tf_op jit(solution)/shard_map/ppermute | solution.py:21
  243.3 13.9 %collective-permute-start.48 = (bf16[2,512,128]{2,1,0:T(8,128)(2,1)S(1)}, bf16[2,512,128]{2,1,0:T(8,128)(2,1)S(1)}, u32[]{:S(2)}, u32[]{:S(2)}) collective-permute-start(bf16[2,512,128]{2,1,0:T(8,128)(2,1)S(1)} %get-tuple-element.47), channel_id=1, source_target_pairs={{0,4},{1,5},{2,6},{3,7},{4,0},{5,1},{6,2},{7,3},{8,12},{9,13},{10,... | collective-permute-start | bytes 786440 | tf_op jit(solution)/shard_map/ppermute | solution.py:21
  243.8 17.5 %collective-permute-start.49 = (bf16[2,512,128]{2,1,0:T(8,128)(2,1)S(1)}, bf16[2,512,128]{2,1,0:T(8,128)(2,1)S(1)}, u32[]{:S(2)}, u32[]{:S(2)}) collective-permute-start(bf16[2,512,128]{2,1,0:T(8,128)(2,1)S(1)} %get-tuple-element.48), channel_id=1, source_target_pairs={{0,2},{1,3},{2,0},{3,1},{4,6},{5,7},{6,4},{7,5},{8,10},{9,11},{10,... | collective-permute-start | bytes 786440 | tf_op jit(solution)/shard_map/ppermute | solution.py:21
  245.5 17.4 %collective-permute-start.60 = (bf16[2,512,128]{2,1,0:T(8,128)(2,1)S(1)}, bf16[2,512,128]{2,1,0:T(8,128)(2,1)S(1)}, u32[]{:S(2)}, u32[]{:S(2)}) collective-permute-start(bf16[2,512,128]{2,1,0:T(8,128)(2,1)S(1)} %add_convert_fusion), channel_id=1, source_target_pairs={{0,16},{8,24},{16,0},{24,8},{1,17},{9,25},{17,1},{25,9},{2,18},{10... | collective-permute-start | bytes 786440 | tf_op jit(solution)/shard_map/ppermute | solution.py:21
  255.7 9.0 %collective-permute-start.52 = (bf16[1,2,512,128]{3,2,1,0:T(8,128)(2,1)S(1)}, bf16[1,2,512,128]{3,2,1,0:T(8,128)(2,1)S(1)}, u32[]{:S(2)}, u32[]{:S(2)}) collective-permute-start(bf16[1,2,512,128]{3,2,1,0:T(8,128)(2,1)S(1)} %add_convert_fusion.1), channel_id=1, source_target_pairs={{0,2},{1,3},{2,0},{3,1},{4,6},{5,7},{6,4},{7,5},{8,10},{9,11},{10,... | collective-permute-start | bytes 786440 | tf_op jit(solution)/shard_map/ppermute | solution.py:21
  261.5 9.3 %collective-permute-start.50 = (bf16[2,512,128]{2,1,0:T(8,128)(2,1)S(1)}, bf16[2,512,128]{2,1,0:T(8,128)(2,1)S(1)}, u32[]{:S(2)}, u32[]{:S(2)}) collective-permute-start(bf16[2,512,128]{2,1,0:T(8,128)(2,1)S(1)} %add_convert_fusion.2), channel_id=1, source_target_pairs={{0,16},{8,24},{16,0},{24,8},{1,17},{9,25},{17,1},{25,9},{2,18},{10... | collective-permute-start | bytes 786440 | tf_op jit(solution)/shard_map/ppermute | solution.py:21
  262.4 8.4 %collective-permute-start.42 = (bf16[1,2,512,128]{3,2,1,0:T(8,128)(2,1)S(1)}, bf16[1,2,512,128]{3,2,1,0:T(8,128)(2,1)S(1)}, u32[]{:S(2)}, u32[]{:S(2)}) collective-permute-start(bf16[1,2,512,128]{3,2,1,0:T(8,128)(2,1)S(1)} %add_convert_fusion.3), channel_id=1, source_target_pairs={{0,4},{1,5},{2,6},{3,7},{4,0},{5,1},{6,2},{7,3},{8,12},{9,13},{10,... | collective-permute-start | bytes 786440 | tf_op jit(solution)/shard_map/ppermute | solution.py:21
  272.0 1.6 collective-permute-start.61
  (9 other events, 77.4 us)
